TPU v7x, 512 devices: a whole 4x8x8 slice. The times are simulated.
512 devices in a mesh: gx: 16 (over x, y_hi, core), gy: 32 (over y_lo, z).
Axes of the slice: x: 4, y: 8 (y_hi: 2, y_lo: 4; y = y_hi * 4 + y_lo), z: 8, core: 2. Of those that a mesh axis runs over, the one named last changes fastest.
Arguments:
- bond_mask: int32 [3, 256, 512, 128], P(None, 'gx', 'gy'), may hold values 0 or 1
- levels: float32 [2, 3], replicated, may hold values from 0.3 to 3
- electrode: int32 [2, 256, 512], P(None, 'gx', 'gy'), may hold values 0 or 1
- leakage: float32 [256, 512, 128], P('gx', 'gy'), may hold values from 0.05 to 0.5
- source: float32 [256, 512, 128], P('gx', 'gy'), may hold values from -72 to 72
- weight: float32 [256, 512, 128], P('gx', 'gy'), may hold values from -72 to 72
Outputs:
- potential: float32 [256, 512, 128], P('gx', 'gy')
- adjoint: float32 [256, 512, 128], P('gx', 'gy')
- sensitivity: float32 [3, 256, 512, 128], P(None, 'gx', 'gy')
All inputs are finite; a program needn't handle non-finite values. No bound on the sum of `bond_mask` or of `electrode` on one device may be relied on, other than what follows from the above.
Results may differ from a plain program's by a relative error of at most 0.0003.
Values sent between devices are 32-bit elements; how exact they have to be, the bound alone decides.
No kernel may reach another device: no remote copies, remote signals or barrier semaphores. Data moves between devices by JAX's collectives and lax.ppermute only.
A program may use at most 64 MiB of HBM per device.

v0:
```python
import jax
import jax.numpy as jnp
from jax import lax
from jax.sharding import PartitionSpec as P

ITERS = 4


def extended(block, sides, width):
    for axis, dim in sides:
        count = lax.axis_size(axis)
        forward = [(i, i + 1) for i in range(count - 1)]
        backward = [(target, source) for source, target in forward]
        low = lax.ppermute(
            lax.slice_in_dim(block, block.shape[dim] - width, None, axis=dim), axis, forward
        )
        high = lax.ppermute(lax.slice_in_dim(block, 0, width, axis=dim), axis, backward)
        block = jnp.concatenate([low, block, high], axis=dim)
    return block


def passed_along(value, axis, steps):
    count = lax.axis_size(axis)
    first, last = (max(0, -steps), min(count, count - steps))
    return lax.ppermute(value, axis, [(source, source + steps) for source in range(first, last)])


def totals(left, right):
    return jnp.sum(left * right, axis=(1, 2, 3))


def operate(fields, cond, below, diag):
    padded = extended(fields, (("gx", 1), ("gy", 2)), 1)
    up_x = padded[:, 2:, 1:-1]
    dn_x = padded[:, :-2, 1:-1]
    up_y = padded[:, 1:-1, 2:]
    dn_y = padded[:, 1:-1, :-2]
    zero_plane = jnp.zeros(fields.shape[:3] + (1,), jnp.float32)
    up_z = jnp.concatenate([fields[..., 1:], zero_plane], axis=3)
    dn_z = jnp.concatenate([zero_plane, fields[..., :-1]], axis=3)
    beside = (
        cond[0] * up_x
        + below[0] * dn_x
        + cond[1] * up_y
        + below[1] * dn_y
        + cond[2] * up_z
        + below[2] * dn_z
    )
    return diag * fields - beside


def precond_total(resid, scaled):
    return lax.psum(totals(resid, scaled), ("gx", "gy"))


def solve(rhs, cond, below, diag):
    solution = jnp.zeros_like(rhs)
    resid = rhs
    scaled = resid / diag
    direction = scaled
    norm_now = precond_total(resid, scaled)
    for step in range(ITERS):
        image = operate(direction, cond, below, diag)
        curv = lax.psum(totals(direction, image), ("gx", "gy"))
        alpha = (norm_now / curv)[:, None, None, None]
        solution = solution + alpha * direction
        resid = resid - alpha * image
        if step + 1 < ITERS:
            scaled = resid / diag
            fresh = precond_total(resid, scaled)
            direction = scaled + (fresh / norm_now)[:, None, None, None] * direction
            norm_now = fresh
    return solution


def body(bond_mask, levels, electrode, leakage, source, weight):
    cx, cy, nz = leakage.shape
    shape = (cx, cy, nz)
    row_x = lax.axis_index("gx") * cx + lax.broadcasted_iota(jnp.int32, (cx, 1, 1), 0)
    row_y = lax.axis_index("gy") * cy + lax.broadcasted_iota(jnp.int32, (1, cy, 1), 1)
    col_z = lax.broadcasted_iota(jnp.int32, (1, 1, nz), 2)
    inside = jnp.stack(
        [
            jnp.broadcast_to(row_x < cx * lax.axis_size("gx") - 1, shape),
            jnp.broadcast_to(row_y < cy * lax.axis_size("gy") - 1, shape),
            jnp.broadcast_to(col_z < nz - 1, shape),
        ]
    ).astype(jnp.float32)
    cond = (
        jnp.where(bond_mask == 1, levels[1][:, None, None, None], levels[0][:, None, None, None])
        * inside
    )
    rim_x = passed_along(cond[0, -1:], "gx", 1)
    rim_y = passed_along(cond[1, :, -1:], "gy", 1)
    below_x = jnp.concatenate([rim_x, cond[0, :-1]], axis=0)
    below_y = jnp.concatenate([rim_y, cond[1, :, :-1]], axis=1)
    below_z = jnp.concatenate([jnp.zeros((cx, cy, 1), jnp.float32), cond[2, :, :, :-1]], axis=2)
    below = (below_x, below_y, below_z)
    elec = electrode.astype(jnp.float32)
    first = jnp.where(col_z == 0, elec[0][:, :, None], 0.0)
    last = jnp.where(col_z == nz - 1, elec[1][:, :, None], 0.0)
    diag = leakage + first + last + cond[0] + cond[1] + cond[2] + below_x + below_y + below_z
    rhs = jnp.stack([source + first, weight + last])
    fields = jnp.concatenate(
        [solve(rhs[0:1], cond, below, diag), solve(rhs[1:2], cond, below, diag)], axis=0
    )
    next_x = passed_along(fields[:, :1], "gx", -1)
    next_y = passed_along(fields[:, :, :1], "gy", -1)
    up_x = jnp.concatenate([fields[:, 1:], next_x], axis=1)
    up_y = jnp.concatenate([fields[:, :, 1:], next_y], axis=2)
    up_z = jnp.concatenate([fields[..., 1:], jnp.zeros((2, cx, cy, 1), jnp.float32)], axis=3)
    potential = fields[0]
    adjoint = fields[1]
    sens = jnp.stack(
        [
            -(adjoint - ups[1]) * (potential - ups[0]) * inside[d]
            for d, ups in enumerate((up_x, up_y, up_z))
        ]
    )
    return (potential, adjoint, sens)


def solution(mesh):
    return jax.shard_map(
        body,
        mesh=mesh,
        in_specs=(
            P(None, "gx", "gy", None),
            P(),
            P(None, "gx", "gy"),
            P("gx", "gy", None),
            P("gx", "gy", None),
            P("gx", "gy", None),
        ),
        out_specs=(P("gx", "gy", None), P("gx", "gy", None), P(None, "gx", "gy", None)),
        check_vma=False,
    )
```

profile of v0, /device:TPU:1, one launch (start us, length us, event | category | flops | bytes accessed | tf_op | source)
XLA Modules:
  0.0 1077.7 jit_solution(148761444872244542)
XLA Ops:
  2.7 8.8 collective-permute-start
  11.6 4.0 collective-permute-start.1
  24.2 7.5 collective-permute-start.3
  35.0 4.6 collective-permute-start.21
  41.9 4.6 collective-permute-start.5
  47.4 108.5 %all-reduce.23 = (f32[1]{0:T(128)}, f32[1]{0:T(128)}) all-reduce(f32[1]{0:T(128)} %bitcast.37, f32[1]{0:T(128)} %bitcast.40), channel_id=1, replica_groups=mesh['gx'=16,'gy'=32] {'gx','gy'}, use_global_device_ids=true, to_apply=%region_17.18 | all-reduce | flops 2 | bytes 16 | tf_op jit(solution)/shard_map/psum | solution.py:53
  158.0 93.5 %psum.122 = f32[1]{0:T(128)} all-reduce(f32[1]{0:T(128)} %bitcast.44), channel_id=1, replica_groups=mesh['gx'=16,'gy'=32] {'gx','gy'}, use_global_device_ids=true, to_apply=%region_21.22 | all-reduce | flops 1 | bytes 8 | tf_op jit(solution)/shard_map/psum | solution.py:53
  252.9 6.1 collective-permute-start.23
  261.8 6.1 collective-permute-done.22
  274.8 98.8 %all-reduce.22 = (f32[1]{0:T(128)}, f32[1]{0:T(128)}, f32[1]{0:T(128)}) all-reduce(f32[1]{0:T(128)} %bitcast.47, f32[1]{0:T(128)} %bitcast.12, f32[1]{0:T(128)} %bitcast.18), channel_id=1, replica_groups=mesh['gx'=16,'gy'=32] {'gx','gy'}, use_global_device_ids=true, to_apply=%region_23.24 | all-reduce | flops 3 | bytes 24 | tf_op jit(solution)/shard_map/psum | solution.py:64
  377.0 95.3 %all-reduce.21 = (f32[1]{0:T(128)}, f32[1]{0:T(128)}) all-reduce(f32[1]{0:T(128)} %bitcast.23, f32[1]{0:T(128)} %bitcast.49), channel_id=1, replica_groups=mesh['gx'=16,'gy'=32] {'gx','gy'}, use_global_device_ids=true, to_apply=%region_5.6 | all-reduce | flops 2 | bytes 16 | tf_op jit(solution)/shard_map/psum | solution.py:53
  475.0 5.3 collective-permute-start.27
  482.4 7.5 collective-permute-start.7
  505.7 104.2 %all-reduce.20 = (f32[1]{0:T(128)}, f32[1]{0:T(128)}) all-reduce(f32[1]{0:T(128)} %bitcast.51, f32[1]{0:T(128)} %bitcast.26), channel_id=1, replica_groups=mesh['gx'=16,'gy'=32] {'gx','gy'}, use_global_device_ids=true, to_apply=%region_27.28 | all-reduce | flops 2 | bytes 16 | tf_op jit(solution)/shard_map/psum | solution.py:64
  613.2 93.5 %psum.116 = f32[1]{0:T(128)} all-reduce(f32[1]{0:T(128)} %bitcast.28), channel_id=1, replica_groups=mesh['gx'=16,'gy'=32] {'gx','gy'}, use_global_device_ids=true, to_apply=%region_9.10 | all-reduce | flops 1 | bytes 8 | tf_op jit(solution)/shard_map/psum | solution.py:53
  708.2 6.5 collective-permute-start.11
  716.7 6.9 collective-permute-done.10
  730.6 98.3 %psum.117 = f32[1]{0:T(128)} all-reduce(f32[1]{0:T(128)} %bitcast.30), channel_id=1, replica_groups=mesh['gx'=16,'gy'=32] {'gx','gy'}, use_global_device_ids=true, to_apply=%region_11.12 | all-reduce | flops 1 | bytes 8 | tf_op jit(solution)/shard_map/psum | solution.py:64
  830.9 95.1 %all-reduce.19 = (f32[1]{0:T(128)}, f32[1]{0:T(128)}) all-reduce(f32[1]{0:T(128)} %bitcast.32, f32[1]{0:T(128)} %bitcast.53), channel_id=1, replica_groups=mesh['gx'=16,'gy'=32] {'gx','gy'}, use_global_device_ids=true, to_apply=%region_13.14 | all-reduce | flops 2 | bytes 16 | tf_op jit(solution)/shard_map/psum | solution.py:53
  928.7 5.4 collective-permute-start.31
  936.2 7.5 collective-permute-start.15
  947.0 4.0 collective-permute-start.33
  959.5 104.1 %all-reduce.18 = (f32[1]{0:T(128)}, f32[1]{0:T(128)}) all-reduce(f32[1]{0:T(128)} %bitcast.34, f32[1]{0:T(128)} %bitcast.55), channel_id=1, replica_groups=mesh['gx'=16,'gy'=32] {'gx','gy'}, use_global_device_ids=true, to_apply=%region_15.16 | all-reduce | flops 2 | bytes 16 | tf_op jit(solution)/shard_map/psum | solution.py:64
  1071.0 5.8 collective-permute-done.34
  (139 shorter events, 75.6 us)
Async XLA Ops:
  2.7 13.6 %collective-permute-start = (f32[1,16,128]{2,1,0:T(8,128)S(1)}, f32[1,16,128]{2,1,0:T(8,128)S(1)}, u32[]{:S(2)}, u32[]{:S(2)}) collective-permute-start(f32[1,16,128]{2,1,0:T(8,128)S(1)} %slice_bitcast_fusion.4), channel_id=1, source_target_pairs={{0,32},{32,64},{64,96},{96,128},{128,160},{160,192},{192,224},{224... | collective-permute-start | bytes 24584 | tf_op jit(solution)/shard_map/ppermute | solution.py:25
  18.3 15.4 %collective-permute-start.19 = (f32[1,1,16,128]{3,2,1,0:T(8,128)S(1)}, f32[1,1,16,128]{3,2,1,0:T(8,128)S(1)}, u32[]{:S(2)}, u32[]{:S(2)}) collective-permute-start(f32[1,1,16,128]{3,2,1,0:T(8,128)S(1)} %get-tuple-element.89), channel_id=1, source_target_pairs={{0,32},{32,64},{64,96},{96,128},{128,160},{160,192},{192,224},{224... | collective-permute-start | bytes 24584 | tf_op jit(solution)/shard_map/ppermute | solution.py:14
  22.2 11.5 %collective-permute-start.18 = (f32[1,1,16,128]{3,2,1,0:T(8,128)S(1)}, f32[1,1,16,128]{3,2,1,0:T(8,128)S(1)}, u32[]{:S(2)}, u32[]{:S(2)}) collective-permute-start(f32[1,1,16,128]{3,2,1,0:T(8,128)S(1)} %get-tuple-element.90), channel_id=1, source_target_pairs={{32,0},{64,32},{96,64},{128,96},{160,128},{192,160},{224,192},{256... | collective-permute-start | bytes 24584 | tf_op jit(solution)/shard_map/ppermute | solution.py:17
  24.2 15.5 %collective-permute-start.3 = (f32[1,1,16,128]{3,2,1,0:T(8,128)S(1)}, f32[1,1,16,128]{3,2,1,0:T(8,128)S(1)}, u32[]{:S(2)}, u32[]{:S(2)}) collective-permute-start(f32[1,1,16,128]{3,2,1,0:T(8,128)S(1)} %get-tuple-element.93), channel_id=1, source_target_pairs={{0,32},{32,64},{64,96},{96,128},{128,160},{160,192},{192,224},{224... | collective-permute-start | bytes 24584 | tf_op jit(solution)/shard_map/ppermute | solution.py:14
  31.7 8.9 collective-permute-start.2
  33.7 12.9 %collective-permute-start.20 = (f32[1,18,1,128]{3,2,1,0:T(1,128)S(1)}, f32[1,18,1,128]{3,2,1,0:T(1,128)S(1)}, u32[]{:S(2)}, u32[]{:S(2)}) collective-permute-start(f32[1,18,1,128]{3,2,1,0:T(1,128)S(1)} %get-tuple-element.57), channel_id=1, source_target_pairs={{1,0},{2,1},{3,2},{4,3},{5,4},{6,5},{7,6},{8,7},{9,8},{10,9},{11,1... | collective-permute-start | bytes 27656 | tf_op jit(solution)/shard_map/ppermute | solution.py:17
  35.0 11.6 %collective-permute-start.21 = (f32[1,18,1,128]{3,2,1,0:T(1,128)S(1)}, f32[1,18,1,128]{3,2,1,0:T(1,128)S(1)}, u32[]{:S(2)}, u32[]{:S(2)}) collective-permute-start(f32[1,18,1,128]{3,2,1,0:T(1,128)S(1)} %get-tuple-element.58), channel_id=1, source_target_pairs={{0,1},{1,2},{2,3},{3,4},{4,5},{5,6},{6,7},{7,8},{8,9},{9,10},{10,1... | collective-permute-start | bytes 27656 | tf_op jit(solution)/shard_map/ppermute | solution.py:14
  40.6 220.3 %collective-permute-start.4 = (f32[1,18,1,128]{3,2,1,0:T(1,128)S(1)}, f32[1,18,1,128]{3,2,1,0:T(1,128)S(1)}, u32[]{:S(2)}, u32[]{:S(2)}) collective-permute-start(f32[1,18,1,128]{3,2,1,0:T(1,128)S(1)} %get-tuple-element.59), channel_id=1, source_target_pairs={{1,0},{2,1},{3,2},{4,3},{5,4},{6,5},{7,6},{8,7},{9,8},{10,9},{11,1... | collective-permute-start | bytes 27656 | tf_op jit(solution)/shard_map/ppermute | solution.py:17
  41.9 219.0 %collective-permute-start.5 = (f32[1,18,1,128]{3,2,1,0:T(1,128)S(1)}, f32[1,18,1,128]{3,2,1,0:T(1,128)S(1)}, u32[]{:S(2)}, u32[]{:S(2)}) collective-permute-start(f32[1,18,1,128]{3,2,1,0:T(1,128)S(1)} %get-tuple-element.60), channel_id=1, source_target_pairs={{0,1},{1,2},{2,3},{3,4},{4,5},{5,6},{6,7},{7,8},{8,9},{9,10},{10,1... | collective-permute-start | bytes 27656 | tf_op jit(solution)/shard_map/ppermute | solution.py:14
  259.0 8.9 collective-permute-start.22
  475.0 16.9 %collective-permute-start.27 = (f32[1,1,16,128]{3,2,1,0:T(8,128)S(1)}, f32[1,1,16,128]{3,2,1,0:T(8,128)S(1)}, u32[]{:S(2)}, u32[]{:S(2)}) collective-permute-start(f32[1,1,16,128]{3,2,1,0:T(8,128)S(1)} %get-tuple-element.79), channel_id=1, source_target_pairs={{0,32},{32,64},{64,96},{96,128},{128,160},{160,192},{192,224},{224... | collective-permute-start | bytes 24584 | tf_op jit(solution)/shard_map/ppermute | solution.py:14
  480.4 11.5 %collective-permute-start.26 = (f32[1,1,16,128]{3,2,1,0:T(8,128)S(1)}, f32[1,1,16,128]{3,2,1,0:T(8,128)S(1)}, u32[]{:S(2)}, u32[]{:S(2)}) collective-permute-start(f32[1,1,16,128]{3,2,1,0:T(8,128)S(1)} %get-tuple-element.80), channel_id=1, source_target_pairs={{32,0},{64,32},{96,64},{128,96},{160,128},{192,160},{224,192},{256... | collective-permute-start | bytes 24584 | tf_op jit(solution)/shard_map/ppermute | solution.py:17
  482.4 14.8 %collective-permute-start.7 = (f32[1,1,16,128]{3,2,1,0:T(8,128)S(1)}, f32[1,1,16,128]{3,2,1,0:T(8,128)S(1)}, u32[]{:S(2)}, u32[]{:S(2)}) collective-permute-start(f32[1,1,16,128]{3,2,1,0:T(8,128)S(1)} %get-tuple-element.75), channel_id=1, source_target_pairs={{0,32},{32,64},{64,96},{96,128},{128,160},{160,192},{192,224},{224... | collective-permute-start | bytes 24584 | tf_op jit(solution)/shard_map/ppermute | solution.py:14
  490.0 8.9 collective-permute-start.6
  491.9 12.2 %collective-permute-start.28 = (f32[1,18,1,128]{3,2,1,0:T(1,128)S(1)}, f32[1,18,1,128]{3,2,1,0:T(1,128)S(1)}, u32[]{:S(2)}, u32[]{:S(2)}) collective-permute-start(f32[1,18,1,128]{3,2,1,0:T(1,128)S(1)} %get-tuple-element.53), channel_id=1, source_target_pairs={{1,0},{2,1},{3,2},{4,3},{5,4},{6,5},{7,6},{8,7},{9,8},{10,9},{11,1... | collective-permute-start | bytes 27656 | tf_op jit(solution)/shard_map/ppermute | solution.py:17
  493.2 10.9 %collective-permute-start.29 = (f32[1,18,1,128]{3,2,1,0:T(1,128)S(1)}, f32[1,18,1,128]{3,2,1,0:T(1,128)S(1)}, u32[]{:S(2)}, u32[]{:S(2)}) collective-permute-start(f32[1,18,1,128]{3,2,1,0:T(1,128)S(1)} %get-tuple-element.54), channel_id=1, source_target_pairs={{0,1},{1,2},{2,3},{3,4},{4,5},{5,6},{6,7},{7,8},{8,9},{9,10},{10,1... | collective-permute-start | bytes 27656 | tf_op jit(solution)/shard_map/ppermute | solution.py:14
  714.7 8.9 collective-permute-start.10
  928.7 16.9 %collective-permute-start.31 = (f32[1,1,16,128]{3,2,1,0:T(8,128)S(1)}, f32[1,1,16,128]{3,2,1,0:T(8,128)S(1)}, u32[]{:S(2)}, u32[]{:S(2)}) collective-permute-start(f32[1,1,16,128]{3,2,1,0:T(8,128)S(1)} %get-tuple-element.63), channel_id=1, source_target_pairs={{0,32},{32,64},{64,96},{96,128},{128,160},{160,192},{192,224},{224... | collective-permute-start | bytes 24584 | tf_op jit(solution)/shard_map/ppermute | solution.py:14
  934.1 11.5 %collective-permute-start.30 = (f32[1,1,16,128]{3,2,1,0:T(8,128)S(1)}, f32[1,1,16,128]{3,2,1,0:T(8,128)S(1)}, u32[]{:S(2)}, u32[]{:S(2)}) collective-permute-start(f32[1,1,16,128]{3,2,1,0:T(8,128)S(1)} %get-tuple-element.64), channel_id=1, source_target_pairs={{32,0},{64,32},{96,64},{128,96},{160,128},{192,160},{224,192},{256... | collective-permute-start | bytes 24584 | tf_op jit(solution)/shard_map/ppermute | solution.py:17
  936.2 14.8 %collective-permute-start.15 = (f32[1,1,16,128]{3,2,1,0:T(8,128)S(1)}, f32[1,1,16,128]{3,2,1,0:T(8,128)S(1)}, u32[]{:S(2)}, u32[]{:S(2)}) collective-permute-start(f32[1,1,16,128]{3,2,1,0:T(8,128)S(1)} %get-tuple-element.69), channel_id=1, source_target_pairs={{0,32},{32,64},{64,96},{96,128},{128,160},{160,192},{192,224},{224... | collective-permute-start | bytes 24584 | tf_op jit(solution)/shard_map/ppermute | solution.py:14
  943.7 8.9 collective-permute-start.14
  945.7 12.2 %collective-permute-start.32 = (f32[1,18,1,128]{3,2,1,0:T(1,128)S(1)}, f32[1,18,1,128]{3,2,1,0:T(1,128)S(1)}, u32[]{:S(2)}, u32[]{:S(2)}) collective-permute-start(f32[1,18,1,128]{3,2,1,0:T(1,128)S(1)} %get-tuple-element.45), channel_id=1, source_target_pairs={{1,0},{2,1},{3,2},{4,3},{5,4},{6,5},{7,6},{8,7},{9,8},{10,9},{11,1... | collective-permute-start | bytes 27656 | tf_op jit(solution)/shard_map/ppermute | solution.py:17
  947.0 10.9 %collective-permute-start.33 = (f32[1,18,1,128]{3,2,1,0:T(1,128)S(1)}, f32[1,18,1,128]{3,2,1,0:T(1,128)S(1)}, u32[]{:S(2)}, u32[]{:S(2)}) collective-permute-start(f32[1,18,1,128]{3,2,1,0:T(1,128)S(1)} %get-tuple-element.46), channel_id=1, source_target_pairs={{0,1},{1,2},{2,3},{3,4},{4,5},{5,6},{6,7},{7,8},{8,9},{9,10},{10,1... | collective-permute-start | bytes 27656 | tf_op jit(solution)/shard_map/ppermute | solution.py:14
  1067.8 9.0 collective-permute-start.34
  (19 other events, 94.0 us)
where the time goes:
time: 1080 us
  blocking collectives  891 us (82%)
  starting transfers between devices  125 us (12%)
  waiting for transfers between devices  25 us (2%)
  between operations  19.9 us (2%)
  other arithmetic  13.4 us (1%)
    psum x5, blocking collectives, precond_total(): return lax.psum(totals(resid, scaled), ('gx', 'gy'))  486 us
    psum x4, blocking collectives, solve(): curv = lax.psum(totals(direction, image), ('gx', 'gy'))  405 us
    ppermute x16, starting transfers between devices, extended(): lax.ppermute(lax.slice_in_dim(block, block.shape[dim] - width, None, axis...  83 us
    ppermute x16, starting transfers between devices, extended(): lax.ppermute(lax.slice_in_dim(block, 0, width, axis=dim), axis, backward)  25.7 us
  transfers between devices with their start and end apart: 36, of which 9 were waited for; matrix products, arithmetic and copies ran while one was open for 0% of the time, Pallas kernels for 0%

commit v1 on v0

v1 whole, which is shorter than its diff:
```python
import functools

import jax
import jax.numpy as jnp
from jax import lax
from jax.experimental import pallas as pl
from jax.experimental.pallas import tpu as pltpu
from jax.sharding import PartitionSpec as P

DEPTH = 4
SUMS = 14
SIDE = 64


def swapped(low_side, high_side, axis):
    count = lax.axis_size(axis)
    even = lax.axis_index(axis) % 2 == 0
    inner = [(i, i ^ 1) for i in range(count)]
    outer = [(i, i + 1) for i in range(1, count - 1, 2)]
    outer = outer + [(target, source) for source, target in outer]
    one = lax.ppermute(jnp.where(even, high_side, low_side), axis, inner)
    two = lax.ppermute(jnp.where(even, low_side, high_side), axis, outer)
    return jnp.where(even, two, one), jnp.where(even, one, two)


def up_y(v):
    return pltpu.roll(v, v.shape[0] - 1, 0)


def dn_y(v):
    return pltpu.roll(v, 1, 0)


def up_z(v):
    return pltpu.roll(v, v.shape[1] - 1, 1)


def dn_z(v):
    return pltpu.roll(v, 1, 1)


def basis_kernel(own_ref, rim_ref, sums_ref, p0, p1, p2, p3, diag, inv, v0):
    cx = own_ref.shape[2]
    planes = own_ref.shape[1]

    def field(f, x):
        return jnp.concatenate([own_ref[f, x], rim_ref[f, x]], axis=0)

    def prepare(x, carry):
        cy, cz = field(4, x), field(5, x)
        d = field(2, x) + field(3, x) + field(3, x - 1) + cy + dn_y(cy) + cz + dn_z(cz)
        r = jnp.where(d > 0.0, 1.0 / d, 0.0)
        diag[x] = d
        inv[x] = r
        v0[0, x] = field(0, x) * r
        v0[1, x] = field(1, x) * r
        return carry

    lax.fori_loop(1, planes, prepare, 0)

    def jacobi(ref, x):
        above, below = field(3, x), field(3, x - 1)
        cy, cz, r = field(4, x), field(5, x), inv[x]
        out = []
        for s in range(2):
            v = ref[s, x]
            beside = above * ref[s, x + 1] + below * ref[s, x - 1]
            beside = beside + cy * up_y(v) + dn_y(cy * v)
            beside = beside + cz * up_z(v) + dn_z(cz * v)
            out.append((v, r * beside))
        return out

    def first(x, carry):
        for s, (v, w) in enumerate(jacobi(v0, x)):
            p0[s, x] = v + w
            p1[s, x] = v - w
        return carry

    lax.fori_loop(2, planes - 1, first, 0)

    def second(x, carry):
        for s, (v, w) in enumerate(jacobi(p0, x)):
            p2[s, x] = v - w
        return carry

    lax.fori_loop(3, planes - 2, second, 0)

    def third(x, carry):
        for s, (v, w) in enumerate(jacobi(p2, x)):
            p3[s, x] = w
        return carry

    lax.fori_loop(4, planes - 3, third, 0)

    def folded(t):
        return sum(t[8 * i : 8 * i + 8] for i in range(1, cx // 8)) + t[0:8] if cx > 8 else t

    def moments(x, carry):
        out = []
        d = diag[x][:cx]
        gx, gy, gz = own_ref[3, x], own_ref[4, x], own_ref[5, x]
        for s in range(2):
            b = own_ref[s, x]
            q = p3[s, x]
            q0, q1, q2, q3 = p0[s, x][:cx], p1[s, x][:cx], p2[s, x][:cx], q[:cx]
            a0 = d * q2
            a1 = d * (2.0 * q1 - q2)
            a2 = d * (q2 - q3)
            links = gx * p3[s, x + 1][:cx] + gy * up_y(q)[:cx] + gz * up_z(q3)
            terms = [a0 * q0, a0 * q1, a0 * q2, a0 * q3, a1 * q1, a1 * q2, a1 * q3]
            terms += [a2 * q2, a2 * q3, (d * q3 - 2.0 * links) * q3]
            terms += [b * q0, b * q1, b * q2, b * q3]
            out += [c + folded(t) for c, t in zip(carry[s * SUMS :], terms)]
        return tuple(out)

    zero = jnp.zeros((8, 128), jnp.float32)
    totals = lax.fori_loop(4, planes - 4, moments, (zero,) * (2 * SUMS))
    lanes = lax.broadcasted_iota(jnp.int32, (1, 128), 1)
    row = jnp.zeros((1, 128), jnp.float32)
    for k, t in enumerate(totals):
        at = k if k < SUMS else SIDE + k - SUMS
        whole = jnp.sum(jnp.sum(t, axis=0, keepdims=True), axis=1, keepdims=True)
        row = row + jnp.where(lanes == at, whole, 0.0)
    sums_ref[...] = row


def combine_kernel(edge_ref, sums_ref, p0, p1, p2, p3, pot_ref, adj_ref, sens_ref, both):
    cx, cy, nz = pot_ref.shape
    total = jnp.sum(jnp.sum(sums_ref[...], axis=0), axis=0, keepdims=True)
    pair = jnp.concatenate([total, pltpu.roll(total, 128 - SIDE, 1)], axis=0)
    lanes = lax.broadcasted_iota(jnp.int32, (2, 128), 1)
    picked = [jnp.sum(jnp.where(lanes == k, pair, 0.0), axis=1, keepdims=True) for k in range(SUMS)]
    energy = {}
    order = iter(picked)
    for i in range(4):
        for j in range(i, 4):
            energy[i, j] = energy[j, i] = next(order)
    right = [next(order) for _ in range(4)]
    scale = [1.0 / jnp.sqrt(energy[i, i]) for i in range(4)]
    m = {(i, j): energy[i, j] * scale[i] * scale[j] for i in range(4) for j in range(4)}
    g = [right[i] * scale[i] for i in range(4)]
    pivot = [None] * 4
    for k in range(4):
        pivot[k] = jnp.where(m[k, k] > 4e-7, 1.0 / m[k, k], 0.0)
        for i in range(k + 1, 4):
            f = m[i, k] * pivot[k]
            for j in range(k, 4):
                m[i, j] = m[i, j] - f * m[k, j]
            g[i] = g[i] - f * g[k]
    c = [None] * 4
    for k in (3, 2, 1, 0):
        t = g[k]
        for j in range(k + 1, 4):
            t = t - m[k, j] * c[j]
        c[k] = t * pivot[k]
    c = [c[k] * scale[k] for k in range(4)]

    def mix(x, carry):
        for s in range(2):
            v = sum(c[k][s : s + 1] * ref[s, x + DEPTH] for k, ref in ((1, p1), (2, p2), (3, p3)))
            both[s, x] = v + c[0][s : s + 1] * p0[s, x + DEPTH]
        return carry

    lax.fori_loop(0, cx + 1, mix, 0)
    rows = lax.broadcasted_iota(jnp.int32, (cy, nz), 0)
    cols = lax.broadcasted_iota(jnp.int32, (cy, nz), 1)
    end_x, end_y = edge_ref[0], edge_ref[1]
    in_y = jnp.where((rows == cy - 1) & (end_y == 1), 0.0, 1.0)
    in_z = jnp.where(cols == nz - 1, 0.0, 1.0)

    def finish(x, carry):
        p, a = both[0, x], both[1, x]
        pot, adj = p[:cy], a[:cy]
        pot_ref[x] = pot
        adj_ref[x] = adj
        in_x = jnp.where((x == cx - 1) & (end_x == 1), 0.0, 1.0)
        sens_ref[0, x] = -(adj - both[1, x + 1][:cy]) * (pot - both[0, x + 1][:cy]) * in_x
        sens_ref[1, x] = -(adj - up_y(a)[:cy]) * (pot - up_y(p)[:cy]) * in_y
        sens_ref[2, x] = -(adj - up_z(adj)) * (pot - up_z(pot)) * in_z
        return carry

    lax.fori_loop(0, cx, finish, 0)


def body(bond_mask, levels, electrode, leakage, source, weight):
    cx, cy, nz = leakage.shape
    shape = (cx, cy, nz)
    nx, ny = lax.axis_size("gx"), lax.axis_size("gy")
    ix, iy = lax.axis_index("gx"), lax.axis_index("gy")
    row_x = ix * cx + lax.broadcasted_iota(jnp.int32, (cx, 1, 1), 0)
    row_y = iy * cy + lax.broadcasted_iota(jnp.int32, (1, cy, 1), 1)
    col_z = lax.broadcasted_iota(jnp.int32, (1, 1, nz), 2)
    inside = jnp.stack(
        [
            jnp.broadcast_to(row_x < cx * nx - 1, shape),
            jnp.broadcast_to(row_y < cy * ny - 1, shape),
            jnp.broadcast_to(col_z < nz - 1, shape),
        ]
    ).astype(jnp.float32)
    cond = (
        jnp.where(bond_mask == 1, levels[1][:, None, None, None], levels[0][:, None, None, None])
        * inside
    )
    elec = electrode.astype(jnp.float32)
    first = jnp.where(col_z == 0, elec[0][:, :, None], 0.0)
    last = jnp.where(col_z == nz - 1, elec[1][:, :, None], 0.0)
    fields = jnp.stack(
        [source + first, weight + last, leakage + first + last, cond[0], cond[1], cond[2]]
    )
    low, high = swapped(fields[:, :DEPTH], fields[:, cx - DEPTH :], "gx")
    wide = jnp.concatenate([low, fields, high], axis=1)
    low, high = swapped(wide[:, :, :DEPTH], wide[:, :, cy - DEPTH :], "gy")
    rim = jnp.concatenate([high, low], axis=2)
    planes, rows = cx + 2 * DEPTH, cy + 2 * DEPTH
    vmem = pl.BlockSpec(memory_space=pltpu.VMEM)
    block = jax.ShapeDtypeStruct((2, planes, rows, nz), jnp.float32)
    sums, *basis = pl.pallas_call(
        basis_kernel,
        out_shape=[jax.ShapeDtypeStruct((1, 128), jnp.float32)] + [block] * 4,
        in_specs=[vmem] * 2,
        out_specs=[vmem] * 5,
        scratch_shapes=[
            pltpu.VMEM((planes, rows, nz), jnp.float32),
            pltpu.VMEM((planes, rows, nz), jnp.float32),
            pltpu.VMEM((2, planes, rows, nz), jnp.float32),
        ],
        compiler_params=pltpu.CompilerParams(vmem_limit_bytes=24 * 2**20),
        name="basis",
    )(wide, rim)
    parts = nx * ny
    spread = jnp.broadcast_to(sums[None], (parts, 1, 128))
    gathered = lax.all_to_all(spread, ("gx", "gy"), 0, 0, tiled=True)
    edge = jnp.stack([ix == nx - 1, iy == ny - 1]).astype(jnp.int32)
    return pl.pallas_call(
        combine_kernel,
        out_shape=[
            jax.ShapeDtypeStruct(shape, jnp.float32),
            jax.ShapeDtypeStruct(shape, jnp.float32),
            jax.ShapeDtypeStruct((3, *shape), jnp.float32),
        ],
        in_specs=[pl.BlockSpec(memory_space=pltpu.SMEM)] + [vmem] * 5,
        out_specs=[vmem] * 3,
        scratch_shapes=[pltpu.VMEM((2, cx + 1, rows, nz), jnp.float32)],
        compiler_params=pltpu.CompilerParams(vmem_limit_bytes=24 * 2**20),
        name="combine",
    )(edge, gathered.reshape(parts // 8, 8, 128), *basis)


def solution(mesh):
    return jax.shard_map(
        body,
        mesh=mesh,
        in_specs=(
            P(None, "gx", "gy", None),
            P(),
            P(None, "gx", "gy"),
            P("gx", "gy", None),
            P("gx", "gy", None),
            P("gx", "gy", None),
        ),
        out_specs=(P("gx", "gy", None), P("gx", "gy", None), P(None, "gx", "gy", None)),
        check_vma=False,
    )
```

time: 1080 us -> 89.7 us (0.08)
  blocking collectives: 891 us -> 0 us
  starting transfers between devices: 125 us -> 41.5 us
  between operations: 19.9 us -> 0.89 us
  Pallas kernels: 0 us -> 11.2 us
  other arithmetic: 13.4 us -> 2.58 us
    psum x9 -> x0, blocking collectives: 891 us -> none  [the longest x5 486 us: precond_total(): return lax.psum(totals(resid, scaled), ('gx', 'gy'))]
    ppermute x36 -> x4, starting transfers between devices: 125 us -> 13.4 us  [the longest x2 10.7 us: swapped(): one = lax.ppermute(jnp.where(even, high_side, low_side), axis, inner)]
    all_to_all x0 -> x1, starting transfers between devices: none -> 28.2 us  [body(): gathered = lax.all_to_all(spread, ('gx', 'gy'), 0, 0, tiled=True)]
    all_to_all x0 -> x1, waiting for transfers between devices: none -> 17.2 us  [body(): gathered = lax.all_to_all(spread, ('gx', 'gy'), 0, 0, tiled=True)]
    pallas_call x0 -> x2, Pallas kernels: none -> 11.2 us  [the longest x1 8.2 us: body(): pl.pallas_call(basis_kernel, out_shape=[jax.ShapeDtypeStruct((1, 128), jn...]
    ppermute x36 -> x4, waiting for transfers between devices: 25 us -> 14.2 us  [the longest x2 9.35 us: swapped(): two = lax.ppermute(jnp.where(even, low_side, high_side), axis, outer)]
  transfers between devices with their start and end apart: 36 -> 5, of which waited for: 9 -> 3; matrix products, arithmetic and copies ran while one was open for 0% -> 0% of each run, Pallas kernels for 0% -> 0%
where the time goes in v1:
time: 89.7 us; the launch traced here: 89.4 us
  starting transfers between devices  41.5 us (46%)
  waiting for transfers between devices  31.4 us (35%)
  Pallas kernels  11.2 us (12%)
  other arithmetic  2.58 us (3%)
  local copies, waits for them, and re-layouts  1.81 us (2%)
    all_to_all x1, starting transfers between devices, body(): gathered = lax.all_to_all(spread, ('gx', 'gy'), 0, 0, tiled=True)  28.2 us
    all_to_all x1, waiting for transfers between devices, body(): gathered = lax.all_to_all(spread, ('gx', 'gy'), 0, 0, tiled=True)  17.2 us
    ppermute x2, starting transfers between devices, swapped(): one = lax.ppermute(jnp.where(even, high_side, low_side), axis, inner)  10.7 us
    ppermute x2, waiting for transfers between devices, swapped(): two = lax.ppermute(jnp.where(even, low_side, high_side), axis, outer)  9.35 us
    pallas_call x1, Pallas kernels, body(): pl.pallas_call(basis_kernel, out_shape=[jax.ShapeDtypeStruct((1, 128), jn...  8.2 us
    ppermute x2, waiting for transfers between devices, swapped(): one = lax.ppermute(jnp.where(even, high_side, low_side), axis, inner)  4.85 us
    pallas_call x1, Pallas kernels, body(): pl.pallas_call(combine_kernel, out_shape=[jax.ShapeDtypeStruct(shape, jnp...  2.99 us
    ppermute x2, starting transfers between devices, swapped(): two = lax.ppermute(jnp.where(even, low_side, high_side), axis, outer)  2.66 us
  transfers between devices with their start and end apart: 5, of which 3 were waited for; matrix products, arithmetic and copies ran while one was open for 0% of the time, Pallas kernels for 0%

profile of v1, /device:TPU:1, one launch (start us, length us, event | category | flops | bytes accessed | tf_op | source)
XLA Modules:
  0.0 89.4 jit_solution(309618042387427237)
XLA Ops:
  0.6 0.0 copy-start.2
  0.7 0.8 slice_bitcast_fusion.3
  1.5 0.7 convert_element_type.8
  2.3 0.1 stack_broadcast_in_dim.7
  2.3 0.1 stack_broadcast_in_dim.6
  2.4 1.1 %select_select_fusion = f32[3,16,16,128]{3,2,1,0:T(8,128)S(1)} fusion(pred[1,16,16,128]{3,2,1,0:T(8,128)(4,1)S(1)} %stack_broadcast_in_dim.8, pred[1,16,16,128]{3,2,1,0:T(8,128)(4,1)S(1)} %stack_broadcast_in_dim.7, pred[1,16,16,128]{3,2,1,0:T(8,128)(4,1)S(1)} %stack_broadcast_in_dim.6, s32[3,16,16,128]{3,2,1,0:T(8,128)} %param.6, f32[3]{0:T(128)S(1)} %get-tuple-element.28, ...), kind=kLoop, calls=%fused_computation.2 | loop fusion | flops 491520 | bytes 884760 | tf_op jit(solution)/shard_map/mul | solution.py:201
  3.6 0.1 fusion
  3.8 8.8 %collective-permute-start.1 = (f32[6,4,16,128]{3,2,1,0:T(8,128)S(1)}, f32[6,4,16,128]{3,2,1,0:T(8,128)S(1)}, u32[]{:S(2)}, u32[]{:S(2)}) collective-permute-start(f32[6,4,16,128]{3,2,1,0:T(8,128)S(1)} %broadcast_select_fusion.4), channel_id=1, source_target_pairs={{0,32},{32,0},{64,96},{96,64},{128,160},{160,128},{192,224},{224,1... | collective-permute-start | bytes 589832 | tf_op jit(solution)/shard_map/ppermute | solution.py:21
  12.6 2.0 %collective-permute-start = (f32[6,4,16,128]{3,2,1,0:T(8,128)S(1)}, f32[6,4,16,128]{3,2,1,0:T(8,128)S(1)}, u32[]{:S(2)}, u32[]{:S(2)}) collective-permute-start(f32[6,4,16,128]{3,2,1,0:T(8,128)S(1)} %get-tuple-element.13), channel_id=1, source_target_pairs={{32,64},{96,128},{160,192},{224,256},{288,320},{352,384},{416,448}... | collective-permute-start | bytes 589832 | tf_op jit(solution)/shard_map/ppermute | solution.py:22
  14.6 0.0 collective-permute-done.1
  14.6 9.3 %collective-permute-done = f32[6,4,16,128]{3,2,1,0:T(8,128)S(1)} collective-permute-done((f32[6,4,16,128]{3,2,1,0:T(8,128)S(1)}, f32[6,4,16,128]{3,2,1,0:T(8,128)S(1)}, u32[]{:S(2)}, u32[]{:S(2)}) %collective-permute-start) | collective-permute-done | bytes 196640 | tf_op jit(solution)/shard_map/ppermute | solution.py:22
  24.0 0.1 pad_maximum_fusion.own_ref
  24.1 0.1 slice_select_fusion.1
  24.2 1.9 %collective-permute-start.2 = (f32[6,24,4,128]{3,2,1,0:T(4,128)S(1)}, f32[6,24,4,128]{3,2,1,0:T(4,128)S(1)}, u32[]{:S(2)}, u32[]{:S(2)}) collective-permute-start(f32[6,24,4,128]{3,2,1,0:T(4,128)S(1)} %get-tuple-element.16), channel_id=1, source_target_pairs={{0,1},{1,0},{2,3},{3,2},{4,5},{5,4},{6,7},{7,6},{8,9},{9,8},{10,11... | collective-permute-start | bytes 884744 | tf_op jit(solution)/shard_map/ppermute | solution.py:21
  26.2 0.7 collective-permute-start.3
  26.9 4.9 %collective-permute-done.2 = f32[6,24,4,128]{3,2,1,0:T(4,128)S(1)} collective-permute-done((f32[6,24,4,128]{3,2,1,0:T(4,128)S(1)}, f32[6,24,4,128]{3,2,1,0:T(4,128)S(1)}, u32[]{:S(2)}, u32[]{:S(2)}) %collective-permute-start.2) | collective-permute-done | bytes 294944 | tf_op jit(solution)/shard_map/ppermute | solution.py:21
  31.7 0.0 collective-permute-done.3
  31.8 0.1 pad_maximum_fusion.1.rim_ref
  31.9 8.2 %basis.1 = (f32[1,128]{1,0:T(1,128)S(1)}, f32[2,24,24,128]{3,2,1,0:T(8,128)S(1)}, f32[2,24,24,128]{3,2,1,0:T(8,128)S(1)}, f32[2,24,24,128]{3,2,1,0:T(8,128)S(1)}, f32[2,24,24,128]{3,2,1,0:T(8,128)S(1)}) custom-call(f32[6,24,16,128]{3,2,1,0:T(8,128)S(1)} %pad_maximum_fusion.own_ref, f32[6,24,8,128]{3,2,1,0:T(8,128)S(1)} %pad_maximum_fusion.1.rim_ref), custom_call_target="tpu_custom_call" | custom-call | tf_op jit(solution)/shard_map/basis/pallas_call | solution.py:217
  40.1 0.8 broadcast_in_dim.75
  41.0 28.2 %all-to-all-start = ((f32[512,1,128]{2,1,0:T(1,128)}), f32[512,1,128]{2,1,0:T(1,128)S(1)}, u32[]{:S(2)}, u32[]{:S(2)}) async-start(f32[512,1,128]{2,1,0:T(1,128)} %broadcast_in_dim.75), calls=%async_computation | async-start | bytes 524288 | tf_op jit(solution)/shard_map/all_to_all | solution.py:232
  69.1 0.1 add_convert_fusion.edge_ref
  69.2 17.2 %all-to-all-done = f32[512,1,128]{2,1,0:T(1,128)S(1)} async-done(((f32[512,1,128]{2,1,0:T(1,128)}), f32[512,1,128]{2,1,0:T(1,128)S(1)}, u32[]{:S(2)}, u32[]{:S(2)}) %all-to-all-start) | async-done | bytes 262176 | tf_op jit(solution)/shard_map/all_to_all | solution.py:232
  86.4 3.0 %combine.1 = (f32[16,16,128]{2,1,0:T(8,128)}, f32[16,16,128]{2,1,0:T(8,128)}, f32[3,16,16,128]{3,2,1,0:T(8,128)}) custom-call(s32[2]{0:T(128)S(1)} %add_convert_fusion.edge_ref, f32[64,8,128]{2,1,0:T(8,128)S(1)} %bitcast.22, f32[2,24,24,128]{3,2,1,0:T(8,128)S(1)} %get-tuple-element.9.p0, f32[2,24,24,128]{3,2,1,0:T(8,128)S(1)} %get-tuple-element.10.p1, ...), custom_call_target="tpu_custom_call" | custom-call | tf_op jit(solution)/shard_map/combine/pallas_call | solution.py:234
  (15 shorter events, 0.2 us)
Async XLA Ops:
  0.6 3.0 %copy-start.2 = (f32[16,16,128]{2,1,0:T(8,128)S(1)}, f32[16,16,128]{2,1,0:T(8,128)}, u32[]{:S(2)}) copy-start(f32[16,16,128]{2,1,0:T(8,128)} %param.11) | copy-start | bytes 393220
  0.6 3.0 %copy-start = (f32[16,16,128]{2,1,0:T(8,128)S(1)}, f32[16,16,128]{2,1,0:T(8,128)}, u32[]{:S(2)}) copy-start(f32[16,16,128]{2,1,0:T(8,128)} %param.10) | copy-start | bytes 393220
  0.7 3.0 %copy-start.1 = (f32[16,16,128]{2,1,0:T(8,128)S(1)}, f32[16,16,128]{2,1,0:T(8,128)}, u32[]{:S(2)}) copy-start(f32[16,16,128]{2,1,0:T(8,128)} %param.9) | copy-start | bytes 393220
  3.8 10.8 %collective-permute-start.1 = (f32[6,4,16,128]{3,2,1,0:T(8,128)S(1)}, f32[6,4,16,128]{3,2,1,0:T(8,128)S(1)}, u32[]{:S(2)}, u32[]{:S(2)}) collective-permute-start(f32[6,4,16,128]{3,2,1,0:T(8,128)S(1)} %broadcast_select_fusion.4), channel_id=1, source_target_pairs={{0,32},{32,0},{64,96},{96,64},{128,160},{160,128},{192,224},{224,1... | collective-permute-start | bytes 589832 | tf_op jit(solution)/shard_map/ppermute | solution.py:21
  12.6 11.4 %collective-permute-start = (f32[6,4,16,128]{3,2,1,0:T(8,128)S(1)}, f32[6,4,16,128]{3,2,1,0:T(8,128)S(1)}, u32[]{:S(2)}, u32[]{:S(2)}) collective-permute-start(f32[6,4,16,128]{3,2,1,0:T(8,128)S(1)} %get-tuple-element.13), channel_id=1, source_target_pairs={{32,64},{96,128},{160,192},{224,256},{288,320},{352,384},{416,448}... | collective-permute-start | bytes 589832 | tf_op jit(solution)/shard_map/ppermute | solution.py:22
  24.2 7.5 %collective-permute-start.2 = (f32[6,24,4,128]{3,2,1,0:T(4,128)S(1)}, f32[6,24,4,128]{3,2,1,0:T(4,128)S(1)}, u32[]{:S(2)}, u32[]{:S(2)}) collective-permute-start(f32[6,24,4,128]{3,2,1,0:T(4,128)S(1)} %get-tuple-element.16), channel_id=1, source_target_pairs={{0,1},{1,0},{2,3},{3,2},{4,5},{5,4},{6,7},{7,6},{8,9},{9,8},{10,11... | collective-permute-start | bytes 884744 | tf_op jit(solution)/shard_map/ppermute | solution.py:21
  26.2 5.5 %collective-permute-start.3 = (f32[6,24,4,128]{3,2,1,0:T(4,128)S(1)}, f32[6,24,4,128]{3,2,1,0:T(4,128)S(1)}, u32[]{:S(2)}, u32[]{:S(2)}) collective-permute-start(f32[6,24,4,128]{3,2,1,0:T(4,128)S(1)} %get-tuple-element.17), channel_id=1, source_target_pairs={{1,2},{3,4},{5,6},{7,8},{9,10},{11,12},{13,14},{15,16},{17,18},{19... | collective-permute-start | bytes 884744 | tf_op jit(solution)/shard_map/ppermute | solution.py:22
  41.0 45.5 %all-to-all-start = ((f32[512,1,128]{2,1,0:T(1,128)}), f32[512,1,128]{2,1,0:T(1,128)S(1)}, u32[]{:S(2)}, u32[]{:S(2)}) async-start(f32[512,1,128]{2,1,0:T(1,128)} %broadcast_in_dim.75), calls=%async_computation | async-start | bytes 524288 | tf_op jit(solution)/shard_map/all_to_all | solution.py:232

commit v2 on v1

--- a/solution.py
+++ b/solution.py
@@ -9,6 +9,7 @@
 
 DEPTH = 4
 SUMS = 14
+SLOTS = 22
 SIDE = 64
 
 
@@ -23,6 +24,20 @@
     return jnp.where(even, two, one), jnp.where(even, one, two)
 
 
+def slot(f, j, above=False):
+    start = (0, 4, 8, 12, 15, 19)[f]
+    return start + j - (0 if above or f in (0, 1, 2, 4) else 1)
+
+
+def slab(fields, above):
+    cx = fields.shape[1]
+    out = []
+    for f in range(6):
+        count = 3 if f in (3, 5) else DEPTH
+        out.append(fields[f, :count] if above else fields[f, cx - count :])
+    return jnp.concatenate(out, axis=0)
+
+
 def up_y(v):
     return pltpu.roll(v, v.shape[0] - 1, 0)
 
@@ -39,24 +54,27 @@
     return pltpu.roll(v, 1, 1)
 
 
-def basis_kernel(own_ref, rim_ref, sums_ref, p0, p1, p2, p3, diag, inv, v0):
+def basis_kernel(own_ref, side_ref, rim_ref, corner_ref, sums_ref, p0, p1, p2, p3, diag, inv, v0):
     cx = own_ref.shape[2]
-    planes = own_ref.shape[1]
+    planes = cx + 2 * DEPTH
 
     def field(f, x):
-        return jnp.concatenate([own_ref[f, x], rim_ref[f, x]], axis=0)
-
-    def prepare(x, carry):
-        cy, cz = field(4, x), field(5, x)
-        d = field(2, x) + field(3, x) + field(3, x - 1) + cy + dn_y(cy) + cz + dn_z(cz)
+        if DEPTH <= x < DEPTH + cx:
+            return jnp.concatenate([own_ref[f, x - DEPTH], rim_ref[f, x - DEPTH]], axis=0)
+        k = slot(f, x) if x < DEPTH else SLOTS + slot(f, x - DEPTH - cx, above=True)
+        return jnp.concatenate([side_ref[k], corner_ref[k]], axis=0)
+
+    rows = lax.broadcasted_iota(jnp.int32, (cx + 2 * DEPTH, 128), 0)
+    seam = (rows == 0) | (rows == cx)
+    for x in range(1, planes):
+        d = field(2, x) + jnp.where(seam, dn_y(field(4, x)), 0.0)
+        if x in (DEPTH, DEPTH + cx):
+            d = d + field(3, x - 1)
         r = jnp.where(d > 0.0, 1.0 / d, 0.0)
         diag[x] = d
         inv[x] = r
         v0[0, x] = field(0, x) * r
         v0[1, x] = field(1, x) * r
-        return carry
-
-    lax.fori_loop(1, planes, prepare, 0)
 
     def jacobi(ref, x):
         above, below = field(3, x), field(3, x - 1)
@@ -70,37 +88,26 @@
             out.append((v, r * beside))
         return out
 
-    def first(x, carry):
+    for x in range(2, planes - 1):
         for s, (v, w) in enumerate(jacobi(v0, x)):
             p0[s, x] = v + w
             p1[s, x] = v - w
-        return carry
-
-    lax.fori_loop(2, planes - 1, first, 0)
-
-    def second(x, carry):
+    for x in range(3, planes - 2):
         for s, (v, w) in enumerate(jacobi(p0, x)):
             p2[s, x] = v - w
-        return carry
-
-    lax.fori_loop(3, planes - 2, second, 0)
-
-    def third(x, carry):
+    for x in range(4, planes - 3):
         for s, (v, w) in enumerate(jacobi(p2, x)):
             p3[s, x] = w
-        return carry
-
-    lax.fori_loop(4, planes - 3, third, 0)
 
     def folded(t):
         return sum(t[8 * i : 8 * i + 8] for i in range(1, cx // 8)) + t[0:8] if cx > 8 else t
 
-    def moments(x, carry):
-        out = []
-        d = diag[x][:cx]
-        gx, gy, gz = own_ref[3, x], own_ref[4, x], own_ref[5, x]
-        for s in range(2):
-            b = own_ref[s, x]
+    totals = [jnp.zeros((8, 128), jnp.float32)] * (2 * SUMS)
+    for s in range(2):
+        for x in range(DEPTH, planes - DEPTH):
+            d = diag[x][:cx]
+            gx, gy, gz = own_ref[3, x - DEPTH], own_ref[4, x - DEPTH], own_ref[5, x - DEPTH]
+            b = own_ref[s, x - DEPTH]
             q = p3[s, x]
             q0, q1, q2, q3 = p0[s, x][:cx], p1[s, x][:cx], p2[s, x][:cx], q[:cx]
             a0 = d * q2
@@ -110,11 +117,8 @@
             terms = [a0 * q0, a0 * q1, a0 * q2, a0 * q3, a1 * q1, a1 * q2, a1 * q3]
             terms += [a2 * q2, a2 * q3, (d * q3 - 2.0 * links) * q3]
             terms += [b * q0, b * q1, b * q2, b * q3]
-            out += [c + folded(t) for c, t in zip(carry[s * SUMS :], terms)]
-        return tuple(out)
-
-    zero = jnp.zeros((8, 128), jnp.float32)
-    totals = lax.fori_loop(4, planes - 4, moments, (zero,) * (2 * SUMS))
+            for k, t in enumerate(terms):
+                totals[s * SUMS + k] = totals[s * SUMS + k] + folded(t)
     lanes = lax.broadcasted_iota(jnp.int32, (1, 128), 1)
     row = jnp.zeros((1, 128), jnp.float32)
     for k, t in enumerate(totals):
@@ -204,20 +208,26 @@
     elec = electrode.astype(jnp.float32)
     first = jnp.where(col_z == 0, elec[0][:, :, None], 0.0)
     last = jnp.where(col_z == nz - 1, elec[1][:, :, None], 0.0)
-    fields = jnp.stack(
-        [source + first, weight + last, leakage + first + last, cond[0], cond[1], cond[2]]
-    )
-    low, high = swapped(fields[:, :DEPTH], fields[:, cx - DEPTH :], "gx")
-    wide = jnp.concatenate([low, fields, high], axis=1)
-    low, high = swapped(wide[:, :, :DEPTH], wide[:, :, cy - DEPTH :], "gy")
+    shifted = [
+        jnp.concatenate([jnp.zeros((1, cy, nz)), cond[0, :-1]], axis=0),
+        jnp.concatenate([jnp.zeros((cx, 1, nz)), cond[1, :, :-1]], axis=1),
+        jnp.concatenate([jnp.zeros((cx, cy, 1)), cond[2, :, :, :-1]], axis=2),
+    ]
+    part = leakage + first + last + cond[0] + cond[1] + cond[2] + sum(shifted)
+    fields = jnp.stack([source + first, weight + last, part, cond[0], cond[1], cond[2]])
+    low, high = swapped(slab(fields, True), slab(fields, False), "gx")
+    side = jnp.concatenate([low, high], axis=0)
+    low, high = swapped(fields[:, :, :DEPTH], fields[:, :, cy - DEPTH :], "gy")
     rim = jnp.concatenate([high, low], axis=2)
+    low, high = swapped(side[:, :DEPTH], side[:, cy - DEPTH :], "gy")
+    corner = jnp.concatenate([high, low], axis=1)
     planes, rows = cx + 2 * DEPTH, cy + 2 * DEPTH
     vmem = pl.BlockSpec(memory_space=pltpu.VMEM)
     block = jax.ShapeDtypeStruct((2, planes, rows, nz), jnp.float32)
     sums, *basis = pl.pallas_call(
         basis_kernel,
         out_shape=[jax.ShapeDtypeStruct((1, 128), jnp.float32)] + [block] * 4,
-        in_specs=[vmem] * 2,
+        in_specs=[vmem] * 4,
         out_specs=[vmem] * 5,
         scratch_shapes=[
             pltpu.VMEM((planes, rows, nz), jnp.float32),
@@ -226,7 +236,7 @@
         ],
         compiler_params=pltpu.CompilerParams(vmem_limit_bytes=24 * 2**20),
         name="basis",
-    )(wide, rim)
+    )(fields, side, rim, corner)
     parts = nx * ny
     spread = jnp.broadcast_to(sums[None], (parts, 1, 128))
     gathered = lax.all_to_all(spread, ("gx", "gy"), 0, 0, tiled=True)

time: 89.7 us -> 76 us (0.85)
  waiting for transfers between devices: 31.4 us -> 18.2 us
  Pallas kernels: 11.2 us -> 4.45 us
  starting transfers between devices: 41.5 us -> 47.2 us
  local copies, waits for them, and re-layouts: 1.81 us -> 2.73 us
    ppermute x2 -> x3, waiting for transfers between devices: 9.35 us -> 0.01 us  [swapped(): two = lax.ppermute(jnp.where(even, low_side, high_side), axis, outer)]
    ppermute x2 -> x3, starting transfers between devices: 2.66 us -> 10.2 us  [swapped(): two = lax.ppermute(jnp.where(even, low_side, high_side), axis, outer)]
    pallas_call x1, Pallas kernels: 8.2 us -> 1.47 us  [body(): pl.pallas_call(basis_kernel, out_shape=[jax.ShapeDtypeStruct((1, 128), jn...]
    all_to_all x1, starting transfers between devices: 28.2 us -> 23.8 us  [body(): gathered = lax.all_to_all(spread, ('gx', 'gy'), 0, 0, tiled=True)]
    ppermute x2 -> x3, waiting for transfers between devices: 4.85 us -> 1.04 us  [swapped(): one = lax.ppermute(jnp.where(even, high_side, low_side), axis, inner)]
    ppermute x2 -> x3, starting transfers between devices: 10.7 us -> 13.2 us  [swapped(): one = lax.ppermute(jnp.where(even, high_side, low_side), axis, inner)]
    unnamed x6 -> x16, local copies, waits for them, and re-layouts: 0.01 us -> 1.66 us
  transfers between devices with their start and end apart: 5 -> 7, of which waited for: 3 -> 2; matrix products, arithmetic and copies ran while one was open for 0% -> 1% of each run, Pallas kernels for 0% -> 0%
where the time goes in v2:
time: 76 us; the launch traced here: 75.6 us
  starting transfers between devices  47.2 us (62%)
  waiting for transfers between devices  18.2 us (24%)
  Pallas kernels  4.45 us (6%)
  local copies, waits for them, and re-layouts  2.73 us (4%)
  other arithmetic  1.89 us (2%)
  between operations  1.03 us (1%)
    all_to_all x1, starting transfers between devices, body(): gathered = lax.all_to_all(spread, ('gx', 'gy'), 0, 0, tiled=True)  23.8 us
    all_to_all x1, waiting for transfers between devices, body(): gathered = lax.all_to_all(spread, ('gx', 'gy'), 0, 0, tiled=True)  17.2 us
    ppermute x3, starting transfers between devices, swapped(): one = lax.ppermute(jnp.where(even, high_side, low_side), axis, inner)  13.2 us
    ppermute x3, starting transfers between devices, swapped(): two = lax.ppermute(jnp.where(even, low_side, high_side), axis, outer)  10.2 us
    pallas_call x1, Pallas kernels, body(): pl.pallas_call(combine_kernel, out_shape=[jax.ShapeDtypeStruct(shape, jnp...  2.99 us
    unnamed x16, local copies, waits for them, and re-layouts  1.66 us
  transfers between devices with their start and end apart: 7, of which 2 were waited for; matrix products, arithmetic and copies ran while one was open for 1% of the time, Pallas kernels for 0%

profile of v2, /device:TPU:1, one launch (start us, length us, event | category | flops | bytes accessed | tf_op | source)
XLA Modules:
  0.0 75.6 jit_solution(6506302447854394404)
XLA Ops:
  0.7 0.7 copy-done.4
  1.4 0.1 stack_broadcast_in_dim.7
  1.5 0.1 stack_broadcast_in_dim.6
  1.6 1.1 %select_select_fusion = f32[3,16,16,128]{3,2,1,0:T(8,128)S(1)} fusion(pred[1,16,16,128]{3,2,1,0:T(8,128)(4,1)S(1)} %stack_broadcast_in_dim.8, pred[1,16,16,128]{3,2,1,0:T(8,128)(4,1)S(1)} %stack_broadcast_in_dim.7, pred[1,16,16,128]{3,2,1,0:T(8,128)(4,1)S(1)} %stack_broadcast_in_dim.6, s32[3,16,16,128]{3,2,1,0:T(8,128)} %param.6, f32[3]{0:T(128)S(1)} %get-tuple-element.39, ...), kind=kLoop, calls=%fused_computation.7 | loop fusion | flops 491520 | bytes 884760 | tf_op jit(solution)/shard_map/mul | solution.py:205
  2.8 0.6 copy-done.3
  3.5 0.2 copy-done.2
  3.7 0.1 copy-done
  3.8 0.2 fusion
  4.1 8.8 %collective-permute-start = (f32[22,16,128]{2,1,0:T(8,128)S(1)}, f32[22,16,128]{2,1,0:T(8,128)S(1)}, u32[]{:S(2)}, u32[]{:S(2)}) collective-permute-start(f32[22,16,128]{2,1,0:T(8,128)S(1)} %get-tuple-element.23), channel_id=1, source_target_pairs={{32,64},{96,128},{160,192},{224,256},{288,320},{352,384},{416,448}... | collective-permute-start | bytes 540680 | tf_op jit(solution)/shard_map/ppermute | solution.py:23
  13.0 1.9 %collective-permute-start.1 = (f32[22,16,128]{2,1,0:T(8,128)S(1)}, f32[22,16,128]{2,1,0:T(8,128)S(1)}, u32[]{:S(2)}, u32[]{:S(2)}) collective-permute-start(f32[22,16,128]{2,1,0:T(8,128)S(1)} %get-tuple-element.24), channel_id=1, source_target_pairs={{0,32},{32,0},{64,96},{96,64},{128,160},{160,128},{192,224},{224,1... | collective-permute-start | bytes 540680 | tf_op jit(solution)/shard_map/ppermute | solution.py:22
  14.9 0.1 pad_maximum_fusion.own_ref
  15.0 0.1 slice_select_fusion.1
  15.1 4.0 %collective-permute-start.2 = (f32[6,16,4,128]{3,2,1,0:T(4,128)S(1)}, f32[6,16,4,128]{3,2,1,0:T(4,128)S(1)}, u32[]{:S(2)}, u32[]{:S(2)}) collective-permute-start(f32[6,16,4,128]{3,2,1,0:T(4,128)S(1)} %get-tuple-element.13), channel_id=1, source_target_pairs={{0,1},{1,0},{2,3},{3,2},{4,5},{5,4},{6,7},{7,6},{8,9},{9,8},{10,11... | collective-permute-start | bytes 589832 | tf_op jit(solution)/shard_map/ppermute | solution.py:22
  19.1 0.7 collective-permute-start.3
  19.9 7.3 %collective-permute-start.4 = (f32[44,4,128]{2,1,0:T(4,128)S(1)}, f32[44,4,128]{2,1,0:T(4,128)S(1)}, u32[]{:S(2)}, u32[]{:S(2)}) collective-permute-start(f32[44,4,128]{2,1,0:T(4,128)S(1)} %get-tuple-element.19), channel_id=1, source_target_pairs={{0,1},{1,0},{2,3},{3,2},{4,5},{5,4},{6,7},{7,6},{8,9},{9,8},{10,11... | collective-permute-start | bytes 270344 | tf_op jit(solution)/shard_map/ppermute | solution.py:22
  27.2 0.7 collective-permute-start.5
  28.0 0.1 pad_maximum_fusion.2.rim_ref
  28.1 1.0 %collective-permute-done.4 = f32[44,4,128]{2,1,0:T(4,128)S(1)} collective-permute-done((f32[44,4,128]{2,1,0:T(4,128)S(1)}, f32[44,4,128]{2,1,0:T(4,128)S(1)}, u32[]{:S(2)}, u32[]{:S(2)}) %collective-permute-start.4) | collective-permute-done | bytes 90144 | tf_op jit(solution)/shard_map/ppermute | solution.py:22
  29.2 1.5 %basis.1 = (f32[1,128]{1,0:T(1,128)S(1)}, f32[2,24,24,128]{3,2,1,0:T(8,128)S(1)}, f32[2,24,24,128]{3,2,1,0:T(8,128)S(1)}, f32[2,24,24,128]{3,2,1,0:T(8,128)S(1)}, f32[2,24,24,128]{3,2,1,0:T(8,128)S(1)}) custom-call(f32[6,16,16,128]{3,2,1,0:T(8,128)S(1)} %pad_maximum_fusion.own_ref, f32[44,16,128]{2,1,0:T(8,128)S(1)} %pad_maximum_fusion.1.side_ref, ...), custom_call_target="tpu_custom_call" | custom-call | tf_op jit(solution)/shard_map/basis/pallas_call | solution.py:227
  30.7 0.8 %broadcast_in_dim.78 = f32[512,1,128]{2,1,0:T(1,128)} broadcast(f32[128]{0:T(128)S(1)} %bitcast.93), dimensions={2} | broadcast | bytes 262656 | tf_op jit(solution)/shard_map/broadcast_in_dim | solution.py:241
  31.5 23.8 %all-to-all-start = ((f32[512,1,128]{2,1,0:T(1,128)}), f32[512,1,128]{2,1,0:T(1,128)S(1)}, u32[]{:S(2)}, u32[]{:S(2)}) async-start(f32[512,1,128]{2,1,0:T(1,128)} %broadcast_in_dim.78), calls=%async_computation | async-start | bytes 524288 | tf_op jit(solution)/shard_map/all_to_all | solution.py:242
  55.3 0.1 add_convert_fusion.edge_ref
  55.4 17.2 %all-to-all-done = f32[512,1,128]{2,1,0:T(1,128)S(1)} async-done(((f32[512,1,128]{2,1,0:T(1,128)}), f32[512,1,128]{2,1,0:T(1,128)S(1)}, u32[]{:S(2)}, u32[]{:S(2)}) %all-to-all-start) | async-done | bytes 262176 | tf_op jit(solution)/shard_map/all_to_all | solution.py:242
  72.6 3.0 %combine.1 = (f32[16,16,128]{2,1,0:T(8,128)}, f32[16,16,128]{2,1,0:T(8,128)}, f32[3,16,16,128]{3,2,1,0:T(8,128)}) custom-call(s32[2]{0:T(128)S(1)} %add_convert_fusion.edge_ref, f32[64,8,128]{2,1,0:T(8,128)S(1)} %bitcast.92, f32[2,24,24,128]{3,2,1,0:T(8,128)S(1)} %get-tuple-element.9.p0, f32[2,24,24,128]{3,2,1,0:T(8,128)S(1)} %get-tuple-element.10.p1, ...), custom_call_target="tpu_custom_call" | custom-call | tf_op jit(solution)/shard_map/combine/pallas_call | solution.py:244
  (37 shorter events, 0.4 us)
Async XLA Ops:
  0.7 0.7 copy-start.4
  2.7 0.7 copy-start.3
  2.7 0.9 %copy-start.2 = (f32[16,16,128]{2,1,0:T(8,128)S(1)}, f32[16,16,128]{2,1,0:T(8,128)}, u32[]{:S(2)}) copy-start(f32[16,16,128]{2,1,0:T(8,128)} %param.11) | copy-start | bytes 393220
  2.8 1.0 %copy-start = (f32[16,16,128]{2,1,0:T(8,128)S(1)}, f32[16,16,128]{2,1,0:T(8,128)}, u32[]{:S(2)}) copy-start(f32[16,16,128]{2,1,0:T(8,128)} %param.10) | copy-start | bytes 393220
  2.8 1.0 %copy-start.1 = (f32[16,16,128]{2,1,0:T(8,128)S(1)}, f32[16,16,128]{2,1,0:T(8,128)}, u32[]{:S(2)}) copy-start(f32[16,16,128]{2,1,0:T(8,128)} %param.9) | copy-start | bytes 393220
  4.1 15.7 %collective-permute-start = (f32[22,16,128]{2,1,0:T(8,128)S(1)}, f32[22,16,128]{2,1,0:T(8,128)S(1)}, u32[]{:S(2)}, u32[]{:S(2)}) collective-permute-start(f32[22,16,128]{2,1,0:T(8,128)S(1)} %get-tuple-element.23), channel_id=1, source_target_pairs={{32,64},{96,128},{160,192},{224,256},{288,320},{352,384},{416,448}... | collective-permute-start | bytes 540680 | tf_op jit(solution)/shard_map/ppermute | solution.py:23
  13.0 6.8 %collective-permute-start.1 = (f32[22,16,128]{2,1,0:T(8,128)S(1)}, f32[22,16,128]{2,1,0:T(8,128)S(1)}, u32[]{:S(2)}, u32[]{:S(2)}) collective-permute-start(f32[22,16,128]{2,1,0:T(8,128)S(1)} %get-tuple-element.24), channel_id=1, source_target_pairs={{0,32},{32,0},{64,96},{96,64},{128,160},{160,128},{192,224},{224,1... | collective-permute-start | bytes 540680 | tf_op jit(solution)/shard_map/ppermute | solution.py:22
  15.1 12.8 %collective-permute-start.2 = (f32[6,16,4,128]{3,2,1,0:T(4,128)S(1)}, f32[6,16,4,128]{3,2,1,0:T(4,128)S(1)}, u32[]{:S(2)}, u32[]{:S(2)}) collective-permute-start(f32[6,16,4,128]{3,2,1,0:T(4,128)S(1)} %get-tuple-element.13), channel_id=1, source_target_pairs={{0,1},{1,0},{2,3},{3,2},{4,5},{5,4},{6,7},{7,6},{8,9},{9,8},{10,11... | collective-permute-start | bytes 589832 | tf_op jit(solution)/shard_map/ppermute | solution.py:22
  19.1 8.8 %collective-permute-start.3 = (f32[6,16,4,128]{3,2,1,0:T(4,128)S(1)}, f32[6,16,4,128]{3,2,1,0:T(4,128)S(1)}, u32[]{:S(2)}, u32[]{:S(2)}) collective-permute-start(f32[6,16,4,128]{3,2,1,0:T(4,128)S(1)} %get-tuple-element.14), channel_id=1, source_target_pairs={{1,2},{3,4},{5,6},{7,8},{9,10},{11,12},{13,14},{15,16},{17,18},{19... | collective-permute-start | bytes 589832 | tf_op jit(solution)/shard_map/ppermute | solution.py:23
  19.9 9.2 %collective-permute-start.4 = (f32[44,4,128]{2,1,0:T(4,128)S(1)}, f32[44,4,128]{2,1,0:T(4,128)S(1)}, u32[]{:S(2)}, u32[]{:S(2)}) collective-permute-start(f32[44,4,128]{2,1,0:T(4,128)S(1)} %get-tuple-element.19), channel_id=1, source_target_pairs={{0,1},{1,0},{2,3},{3,2},{4,5},{5,4},{6,7},{7,6},{8,9},{9,8},{10,11... | collective-permute-start | bytes 270344 | tf_op jit(solution)/shard_map/ppermute | solution.py:22
  27.2 1.9 %collective-permute-start.5 = (f32[44,4,128]{2,1,0:T(4,128)S(1)}, f32[44,4,128]{2,1,0:T(4,128)S(1)}, u32[]{:S(2)}, u32[]{:S(2)}) collective-permute-start(f32[44,4,128]{2,1,0:T(4,128)S(1)} %get-tuple-element.20), channel_id=1, source_target_pairs={{1,2},{3,4},{5,6},{7,8},{9,10},{11,12},{13,14},{15,16},{17,18},{19... | collective-permute-start | bytes 270344 | tf_op jit(solution)/shard_map/ppermute | solution.py:23
  31.5 41.1 %all-to-all-start = ((f32[512,1,128]{2,1,0:T(1,128)}), f32[512,1,128]{2,1,0:T(1,128)S(1)}, u32[]{:S(2)}, u32[]{:S(2)}) async-start(f32[512,1,128]{2,1,0:T(1,128)} %broadcast_in_dim.78), calls=%async_computation | async-start | bytes 524288 | tf_op jit(solution)/shard_map/all_to_all | solution.py:242

commit v3 on v2

--- a/solution.py
+++ b/solution.py
@@ -13,15 +13,30 @@
 SIDE = 64
 
 
-def swapped(low_side, high_side, axis):
+def swapped(one, two, axis, even):
     count = lax.axis_size(axis)
-    even = lax.axis_index(axis) % 2 == 0
     inner = [(i, i ^ 1) for i in range(count)]
     outer = [(i, i + 1) for i in range(1, count - 1, 2)]
     outer = outer + [(target, source) for source, target in outer]
-    one = lax.ppermute(jnp.where(even, high_side, low_side), axis, inner)
-    two = lax.ppermute(jnp.where(even, low_side, high_side), axis, outer)
+    two = lax.ppermute(two, axis, outer)
+    one = lax.ppermute(one, axis, inner)
     return jnp.where(even, two, one), jnp.where(even, one, two)
+
+
+def up_y(v):
+    return pltpu.roll(v, v.shape[0] - 1, 0)
+
+
+def dn_y(v):
+    return pltpu.roll(v, 1, 0)
+
+
+def up_z(v):
+    return pltpu.roll(v, v.shape[1] - 1, 1)
+
+
+def dn_z(v):
+    return pltpu.roll(v, 1, 1)
 
 
 def slot(f, j, above=False):
@@ -29,29 +44,57 @@
     return start + j - (0 if above or f in (0, 1, 2, 4) else 1)
 
 
-def slab(fields, above):
-    cx = fields.shape[1]
+def slab():
     out = []
     for f in range(6):
         count = 3 if f in (3, 5) else DEPTH
-        out.append(fields[f, :count] if above else fields[f, cx - count :])
-    return jnp.concatenate(out, axis=0)
-
-
-def up_y(v):
-    return pltpu.roll(v, v.shape[0] - 1, 0)
-
-
-def dn_y(v):
-    return pltpu.roll(v, 1, 0)
-
-
-def up_z(v):
-    return pltpu.roll(v, v.shape[1] - 1, 1)
-
-
-def dn_z(v):
-    return pltpu.roll(v, 1, 1)
+        out += [(f, k, k - count) for k in range(count)]
+    return out
+
+
+def pack_kernel(flag_ref, level_ref, mask_ref, elec_ref, leak_ref, source_ref, weight_ref,
+                own_ref, x_one, x_two, y_one, y_two):
+    cx, cy, nz = leak_ref.shape
+    rows = lax.broadcasted_iota(jnp.int32, (cy, nz), 0)
+    cols = lax.broadcasted_iota(jnp.int32, (cy, nz), 1)
+    even_x, even_y = flag_ref[0] == 1, flag_ref[1] == 1
+    keep_x = jnp.where(flag_ref[2] == 1, 0.0, 1.0)
+    keep_y = jnp.where((rows == cy - 1) & (flag_ref[3] == 1), 0.0, 1.0)
+    keep_z = jnp.where(cols == nz - 1, 0.0, 1.0)
+    square = lax.broadcasted_iota(jnp.int32, (cy, cy), 0) == lax.broadcasted_iota(jnp.int32, (cy, cy), 1)
+    before = None
+    for x in range(cx):
+        c = [
+            jnp.where(mask_ref[d, x] == 1, level_ref[1, d], level_ref[0, d]) for d in range(3)
+        ]
+        if x == cx - 1:
+            c[0] = c[0] * keep_x
+        c[1] = c[1] * keep_y
+        c[2] = c[2] * keep_z
+        ends = []
+        for e, at in ((0, 0), (1, nz - 1)):
+            row = jnp.broadcast_to(elec_ref[e, x : x + 1].astype(jnp.float32), (cy, cy))
+            column = jnp.sum(jnp.where(square, row, 0.0), axis=1, keepdims=True)
+            ends.append(jnp.where(cols == at, column, 0.0))
+        part = leak_ref[x] + ends[0] + ends[1] + c[0] + c[1] + c[2]
+        part = part + jnp.where(rows == 0, 0.0, dn_y(c[1])) + dn_z(c[2])
+        if x:
+            part = part + before
+        before = c[0]
+        own_ref[0, x] = source_ref[x] + ends[0]
+        own_ref[1, x] = weight_ref[x] + ends[1]
+        own_ref[2, x] = part
+        for d in range(3):
+            own_ref[3 + d, x] = c[d]
+    for k, (f, above, below) in enumerate(slab()):
+        low, high = own_ref[f, above], own_ref[f, cx + below]
+        x_one[k] = jnp.where(even_x, high, low)
+        x_two[k] = jnp.where(even_x, low, high)
+    for f in range(6):
+        for x in range(cx):
+            low, high = own_ref[f, x, :DEPTH], own_ref[f, x, cy - DEPTH :]
+            y_one[f, x] = jnp.where(even_y, high, low)
+            y_two[f, x] = jnp.where(even_y, low, high)
 
 
 def basis_kernel(own_ref, side_ref, rim_ref, corner_ref, sums_ref, p0, p1, p2, p3, diag, inv, v0):
@@ -125,7 +168,8 @@
         at = k if k < SUMS else SIDE + k - SUMS
         whole = jnp.sum(jnp.sum(t, axis=0, keepdims=True), axis=1, keepdims=True)
         row = row + jnp.where(lanes == at, whole, 0.0)
-    sums_ref[...] = row
+    for k in range(sums_ref.shape[0]):
+        sums_ref[k] = jnp.broadcast_to(row, sums_ref.shape[1:])
 
 
 def combine_kernel(edge_ref, sums_ref, p0, p1, p2, p3, pot_ref, adj_ref, sens_ref, both):
@@ -159,31 +203,24 @@
         c[k] = t * pivot[k]
     c = [c[k] * scale[k] for k in range(4)]
 
-    def mix(x, carry):
+    for x in range(cx + 1):
         for s in range(2):
             v = sum(c[k][s : s + 1] * ref[s, x + DEPTH] for k, ref in ((1, p1), (2, p2), (3, p3)))
             both[s, x] = v + c[0][s : s + 1] * p0[s, x + DEPTH]
-        return carry
-
-    lax.fori_loop(0, cx + 1, mix, 0)
     rows = lax.broadcasted_iota(jnp.int32, (cy, nz), 0)
     cols = lax.broadcasted_iota(jnp.int32, (cy, nz), 1)
-    end_x, end_y = edge_ref[0], edge_ref[1]
-    in_y = jnp.where((rows == cy - 1) & (end_y == 1), 0.0, 1.0)
+    in_x = jnp.where(edge_ref[2] == 1, 0.0, 1.0)
+    in_y = jnp.where((rows == cy - 1) & (edge_ref[3] == 1), 0.0, 1.0)
     in_z = jnp.where(cols == nz - 1, 0.0, 1.0)
-
-    def finish(x, carry):
+    for x in range(cx):
         p, a = both[0, x], both[1, x]
         pot, adj = p[:cy], a[:cy]
         pot_ref[x] = pot
         adj_ref[x] = adj
-        in_x = jnp.where((x == cx - 1) & (end_x == 1), 0.0, 1.0)
-        sens_ref[0, x] = -(adj - both[1, x + 1][:cy]) * (pot - both[0, x + 1][:cy]) * in_x
+        along = -(adj - both[1, x + 1][:cy]) * (pot - both[0, x + 1][:cy])
+        sens_ref[0, x] = along * in_x if x == cx - 1 else along
         sens_ref[1, x] = -(adj - up_y(a)[:cy]) * (pot - up_y(p)[:cy]) * in_y
         sens_ref[2, x] = -(adj - up_z(adj)) * (pot - up_z(pot)) * in_z
-        return carry
-
-    lax.fori_loop(0, cx, finish, 0)
 
 
 def body(bond_mask, levels, electrode, leakage, source, weight):
@@ -191,42 +228,34 @@
     shape = (cx, cy, nz)
     nx, ny = lax.axis_size("gx"), lax.axis_size("gy")
     ix, iy = lax.axis_index("gx"), lax.axis_index("gy")
-    row_x = ix * cx + lax.broadcasted_iota(jnp.int32, (cx, 1, 1), 0)
-    row_y = iy * cy + lax.broadcasted_iota(jnp.int32, (1, cy, 1), 1)
-    col_z = lax.broadcasted_iota(jnp.int32, (1, 1, nz), 2)
-    inside = jnp.stack(
-        [
-            jnp.broadcast_to(row_x < cx * nx - 1, shape),
-            jnp.broadcast_to(row_y < cy * ny - 1, shape),
-            jnp.broadcast_to(col_z < nz - 1, shape),
-        ]
-    ).astype(jnp.float32)
-    cond = (
-        jnp.where(bond_mask == 1, levels[1][:, None, None, None], levels[0][:, None, None, None])
-        * inside
-    )
-    elec = electrode.astype(jnp.float32)
-    first = jnp.where(col_z == 0, elec[0][:, :, None], 0.0)
-    last = jnp.where(col_z == nz - 1, elec[1][:, :, None], 0.0)
-    shifted = [
-        jnp.concatenate([jnp.zeros((1, cy, nz)), cond[0, :-1]], axis=0),
-        jnp.concatenate([jnp.zeros((cx, 1, nz)), cond[1, :, :-1]], axis=1),
-        jnp.concatenate([jnp.zeros((cx, cy, 1)), cond[2, :, :, :-1]], axis=2),
-    ]
-    part = leakage + first + last + cond[0] + cond[1] + cond[2] + sum(shifted)
-    fields = jnp.stack([source + first, weight + last, part, cond[0], cond[1], cond[2]])
-    low, high = swapped(slab(fields, True), slab(fields, False), "gx")
+    even_x, even_y = ix % 2 == 0, iy % 2 == 0
+    flags = jnp.stack([even_x, even_y, ix == nx - 1, iy == ny - 1]).astype(jnp.int32)
+    vmem = pl.BlockSpec(memory_space=pltpu.VMEM)
+    smem = pl.BlockSpec(memory_space=pltpu.SMEM)
+    slots = jax.ShapeDtypeStruct((SLOTS, cy, nz), jnp.float32)
+    strip = jax.ShapeDtypeStruct((6, cx, DEPTH, nz), jnp.float32)
+    fields, x_one, x_two, y_one, y_two = pl.pallas_call(
+        pack_kernel,
+        out_shape=[jax.ShapeDtypeStruct((6, *shape), jnp.float32), slots, slots, strip, strip],
+        in_specs=[smem] * 2 + [vmem] * 5,
+        out_specs=[vmem] * 5,
+        compiler_params=pltpu.CompilerParams(vmem_limit_bytes=24 * 2**20),
+        name="pack",
+    )(flags, levels, bond_mask, electrode, leakage, source, weight)
+    low, high = swapped(x_one, x_two, "gx", even_x)
     side = jnp.concatenate([low, high], axis=0)
-    low, high = swapped(fields[:, :, :DEPTH], fields[:, :, cy - DEPTH :], "gy")
+    first, last = side[:, :DEPTH], side[:, cy - DEPTH :]
+    corner_one, corner_two = jnp.where(even_y, last, first), jnp.where(even_y, first, last)
+    low, high = swapped(y_one, y_two, "gy", even_y)
     rim = jnp.concatenate([high, low], axis=2)
-    low, high = swapped(side[:, :DEPTH], side[:, cy - DEPTH :], "gy")
+    low, high = swapped(corner_one, corner_two, "gy", even_y)
     corner = jnp.concatenate([high, low], axis=1)
     planes, rows = cx + 2 * DEPTH, cy + 2 * DEPTH
-    vmem = pl.BlockSpec(memory_space=pltpu.VMEM)
     block = jax.ShapeDtypeStruct((2, planes, rows, nz), jnp.float32)
+    parts = nx * ny
     sums, *basis = pl.pallas_call(
         basis_kernel,
-        out_shape=[jax.ShapeDtypeStruct((1, 128), jnp.float32)] + [block] * 4,
+        out_shape=[jax.ShapeDtypeStruct((parts // 8, 8, 128), jnp.float32)] + [block] * 4,
         in_specs=[vmem] * 4,
         out_specs=[vmem] * 5,
         scratch_shapes=[
@@ -237,10 +266,7 @@
         compiler_params=pltpu.CompilerParams(vmem_limit_bytes=24 * 2**20),
         name="basis",
     )(fields, side, rim, corner)
-    parts = nx * ny
-    spread = jnp.broadcast_to(sums[None], (parts, 1, 128))
-    gathered = lax.all_to_all(spread, ("gx", "gy"), 0, 0, tiled=True)
-    edge = jnp.stack([ix == nx - 1, iy == ny - 1]).astype(jnp.int32)
+    gathered = lax.all_to_all(sums.reshape(parts, 1, 128), ("gx", "gy"), 0, 0, tiled=True)
     return pl.pallas_call(
         combine_kernel,
         out_shape=[
@@ -248,12 +274,12 @@
             jax.ShapeDtypeStruct(shape, jnp.float32),
             jax.ShapeDtypeStruct((3, *shape), jnp.float32),
         ],
-        in_specs=[pl.BlockSpec(memory_space=pltpu.SMEM)] + [vmem] * 5,
+        in_specs=[smem] + [vmem] * 5,
         out_specs=[vmem] * 3,
         scratch_shapes=[pltpu.VMEM((2, cx + 1, rows, nz), jnp.float32)],
         compiler_params=pltpu.CompilerParams(vmem_limit_bytes=24 * 2**20),
         name="combine",
-    )(edge, gathered.reshape(parts // 8, 8, 128), *basis)
+    )(flags, gathered.reshape(parts // 8, 8, 128), *basis)
 
 
 def solution(mesh):

time: 76 us -> 76 us (level)
  blocking collectives: 0 us -> 41.1 us
  starting transfers between devices: 47.2 us -> 23.4 us
  waiting for transfers between devices: 18.2 us -> 1.05 us
  local copies, waits for them, and re-layouts: 2.73 us -> 4.32 us
  other arithmetic: 1.89 us -> 0.34 us
    all_to_all x0 -> x1, blocking collectives: none -> 41.1 us  [body(): lax.all_to_all(sums.reshape(parts, 1, 128), ('gx', 'gy'), 0, 0, tiled=True)]
    all_to_all x1 -> x0, starting transfers between devices: 23.8 us -> none  [body(): gathered = lax.all_to_all(spread, ('gx', 'gy'), 0, 0, tiled=True)]
    all_to_all x1 -> x0, waiting for transfers between devices: 17.2 us -> none  [body(): gathered = lax.all_to_all(spread, ('gx', 'gy'), 0, 0, tiled=True)]
    unnamed x16 -> x12, local copies, waits for them, and re-layouts: 1.66 us -> 4.32 us
    pallas_call x1 -> x2, Pallas kernels: 1.47 us -> 2.71 us  [the longest x1 1.6 us: body(): pl.pallas_call(basis_kernel, out_shape=[jax.ShapeDtypeStruct((parts // 8,...]
    pallas_call x1, Pallas kernels: 2.99 us -> 1.81 us  [body(): pl.pallas_call(combine_kernel, out_shape=[jax.ShapeDtypeStruct(shape, jnp...]
    mul x1 -> x0, other arithmetic: 1.14 us -> none  [body(): jnp.where(bond_mask == 1, levels[1][:, None, None, None], levels[0][:, No...]
    broadcast_in_dim x3 -> x0, local copies, waits for them, and re-layouts: 0.85 us -> none  [the longest x1 0.84 us: body(): spread = jnp.broadcast_to(sums[None], (parts, 1, 128))]
  transfers between devices with their start and end apart: 7 -> 6, of which waited for: 2 -> 1; matrix products, arithmetic and copies ran while one was open for 1% -> 0% of each run, Pallas kernels for 0% -> 0%
where the time goes in v3:
time: 76 us; the launch traced here: 75.6 us
  blocking collectives  41.1 us (54%)
  starting transfers between devices  23.4 us (31%)
  Pallas kernels  4.51 us (6%)
  local copies, waits for them, and re-layouts  4.32 us (6%)
  waiting for transfers between devices  1.05 us (1%)
  between operations  0.82 us (1%)
    all_to_all x1, blocking collectives, body(): lax.all_to_all(sums.reshape(parts, 1, 128), ('gx', 'gy'), 0, 0, tiled=True)  41.1 us
    ppermute x3, starting transfers between devices, swapped(): one = lax.ppermute(one, axis, inner)  13.2 us
    ppermute x3, starting transfers between devices, swapped(): two = lax.ppermute(two, axis, outer)  10.2 us
    unnamed x12, local copies, waits for them, and re-layouts  4.32 us
    pallas_call x1, Pallas kernels, body(): pl.pallas_call(combine_kernel, out_shape=[jax.ShapeDtypeStruct(shape, jnp...  1.81 us
    pallas_call x1, Pallas kernels, body(): pl.pallas_call(basis_kernel, out_shape=[jax.ShapeDtypeStruct((parts // 8,...  1.6 us
  transfers between devices with their start and end apart: 6, of which 1 were waited for; matrix products, arithmetic and copies ran while one was open for 0% of the time, Pallas kernels for 0%

profile of v3, /device:TPU:1, one launch (start us, length us, event | category | flops | bytes accessed | tf_op | source)
XLA Modules:
  0.0 75.6 jit_solution(6494339253561279217)
XLA Ops:
  0.7 0.1 add_convert_fusion.flag_ref.edge_ref
  0.8 0.6 copy-done.4
  1.4 0.0 copy-done.5
  1.4 1.0 %copy-done = s32[3,16,16,128]{3,2,1,0:T(8,128)S(1)} copy-done((s32[3,16,16,128]{3,2,1,0:T(8,128)S(1)}, s32[3,16,16,128]{3,2,1,0:T(8,128)}, u32[]{:S(2)}) %copy-start) | copy-done | bytes 393240
  2.4 0.9 %copy-done.1 = f32[16,16,128]{2,1,0:T(8,128)S(1)} copy-done((f32[16,16,128]{2,1,0:T(8,128)S(1)}, f32[16,16,128]{2,1,0:T(8,128)}, u32[]{:S(2)}) %copy-start.1) | copy-done | bytes 131096
  3.3 0.9 %copy-done.2 = f32[16,16,128]{2,1,0:T(8,128)S(1)} copy-done((f32[16,16,128]{2,1,0:T(8,128)S(1)}, f32[16,16,128]{2,1,0:T(8,128)}, u32[]{:S(2)}) %copy-start.2) | copy-done | bytes 131096
  4.2 0.9 %copy-done.3 = f32[16,16,128]{2,1,0:T(8,128)S(1)} copy-done((f32[16,16,128]{2,1,0:T(8,128)S(1)}, f32[16,16,128]{2,1,0:T(8,128)}, u32[]{:S(2)}) %copy-start.3) | copy-done | bytes 131096
  5.1 1.1 %pack.1 = (f32[6,16,16,128]{3,2,1,0:T(8,128)S(1)}, f32[22,16,128]{2,1,0:T(8,128)S(1)}, f32[22,16,128]{2,1,0:T(8,128)S(1)}, f32[6,16,4,128]{3,2,1,0:T(4,128)S(1)}, f32[6,16,4,128]{3,2,1,0:T(4,128)S(1)}) custom-call(s32[4]{0:T(128)S(1)} %add_convert_fusion.flag_ref.edge_ref, f32[2,3]{1,0:T(2,128)S(1)} %copy-done.5, s32[3,16,16,128]{3,2,1,0:T(8,128)S(1)} %copy-done, ...), custom_call_target="tpu_custom_call" | custom-call | tf_op jit(solution)/shard_map/pack/pallas_call | solution.py:237
  6.2 8.8 %collective-permute-start = (f32[22,16,128]{2,1,0:T(8,128)S(1)}, f32[22,16,128]{2,1,0:T(8,128)S(1)}, u32[]{:S(2)}, u32[]{:S(2)}) collective-permute-start(f32[22,16,128]{2,1,0:T(8,128)S(1)} %get-tuple-element.14), channel_id=1, source_target_pairs={{32,64},{96,128},{160,192},{224,256},{288,320},{352,384},{416,448}... | collective-permute-start | bytes 540680 | tf_op jit(solution)/shard_map/ppermute | solution.py:21
  15.0 1.9 %collective-permute-start.1 = (f32[22,16,128]{2,1,0:T(8,128)S(1)}, f32[22,16,128]{2,1,0:T(8,128)S(1)}, u32[]{:S(2)}, u32[]{:S(2)}) collective-permute-start(f32[22,16,128]{2,1,0:T(8,128)S(1)} %get-tuple-element.15), channel_id=1, source_target_pairs={{0,32},{32,0},{64,96},{96,64},{128,160},{160,128},{192,224},{224,1... | collective-permute-start | bytes 540680 | tf_op jit(solution)/shard_map/ppermute | solution.py:22
  17.0 4.0 %collective-permute-start.2 = (f32[6,16,4,128]{3,2,1,0:T(4,128)S(1)}, f32[6,16,4,128]{3,2,1,0:T(4,128)S(1)}, u32[]{:S(2)}, u32[]{:S(2)}) collective-permute-start(f32[6,16,4,128]{3,2,1,0:T(4,128)S(1)} %get-tuple-element.16), channel_id=1, source_target_pairs={{0,1},{1,0},{2,3},{3,2},{4,5},{5,4},{6,7},{7,6},{8,9},{9,8},{10,11... | collective-permute-start | bytes 589832 | tf_op jit(solution)/shard_map/ppermute | solution.py:22
  21.0 0.7 collective-permute-start.3
  21.7 0.0 collective-permute-done
  21.7 0.0 collective-permute-done.1
  21.8 7.3 %collective-permute-start.4 = (f32[44,4,128]{2,1,0:T(4,128)S(1)}, f32[44,4,128]{2,1,0:T(4,128)S(1)}, u32[]{:S(2)}, u32[]{:S(2)}) collective-permute-start(f32[44,4,128]{2,1,0:T(4,128)S(1)} %get-tuple-element.25), channel_id=1, source_target_pairs={{0,1},{1,0},{2,3},{3,2},{4,5},{5,4},{6,7},{7,6},{8,9},{9,8},{10,11... | collective-permute-start | bytes 270344 | tf_op jit(solution)/shard_map/ppermute | solution.py:22
  29.1 0.7 collective-permute-start.5
  29.8 0.0 collective-permute-done.2
  29.8 0.0 collective-permute-done.3
  29.9 0.1 pad_maximum_fusion.1.rim_ref
  30.0 1.0 %collective-permute-done.4 = f32[44,4,128]{2,1,0:T(4,128)S(1)} collective-permute-done((f32[44,4,128]{2,1,0:T(4,128)S(1)}, f32[44,4,128]{2,1,0:T(4,128)S(1)}, u32[]{:S(2)}, u32[]{:S(2)}) %collective-permute-start.4) | collective-permute-done | bytes 90144 | tf_op jit(solution)/shard_map/ppermute | solution.py:22
  31.0 0.0 collective-permute-done.5
  31.1 1.6 %basis.1 = (f32[64,8,128]{2,1,0:T(8,128)S(1)}, f32[2,24,24,128]{3,2,1,0:T(8,128)S(1)}, f32[2,24,24,128]{3,2,1,0:T(8,128)S(1)}, f32[2,24,24,128]{3,2,1,0:T(8,128)S(1)}, f32[2,24,24,128]{3,2,1,0:T(8,128)S(1)}) custom-call(f32[6,16,16,128]{3,2,1,0:T(8,128)S(1)} %get-tuple-element.13.own_ref, f32[44,16,128]{2,1,0:T(8,128)S(1)} %pad_maximum_fusion.side_ref, ...), custom_call_target="tpu_custom_call" | custom-call | tf_op jit(solution)/shard_map/basis/pallas_call | solution.py:256
  32.7 41.1 %all_to_all.5 = f32[512,1,128]{2,1,0:T(1,128)S(1)} all-to-all(f32[512,1,128]{2,1,0:T(1,128)S(1)} %bitcast.17), channel_id=1, replica_groups=mesh['gx'=16,'gy'=32] {'gx','gy'}, dimensions={0} | all-to-all | bytes 524288 | tf_op jit(solution)/shard_map/all_to_all | solution.py:269
  73.8 1.8 %combine.1 = (f32[16,16,128]{2,1,0:T(8,128)}, f32[16,16,128]{2,1,0:T(8,128)}, f32[3,16,16,128]{3,2,1,0:T(8,128)}) custom-call(s32[4]{0:T(128)S(1)} %add_convert_fusion.flag_ref.edge_ref, f32[64,8,128]{2,1,0:T(8,128)S(1)} %bitcast.16, f32[2,24,24,128]{3,2,1,0:T(8,128)S(1)} %get-tuple-element.19.p0, f32[2,24,24,128]{3,2,1,0:T(8,128)S(1)} %get-tuple-element.20.p1, ...), custom_call_target="tpu_custom_call" | custom-call | tf_op jit(solution)/shard_map/combine/pallas_call | solution.py:270
  (12 shorter events, 0.2 us)
Async XLA Ops:
  0.6 0.7 copy-start.4
  0.7 0.7 copy-start.5
  1.4 1.0 %copy-start = (s32[3,16,16,128]{3,2,1,0:T(8,128)S(1)}, s32[3,16,16,128]{3,2,1,0:T(8,128)}, u32[]{:S(2)}) copy-start(s32[3,16,16,128]{3,2,1,0:T(8,128)} %mask_ref.1) | copy-start | bytes 1179652
  2.4 0.9 %copy-start.1 = (f32[16,16,128]{2,1,0:T(8,128)S(1)}, f32[16,16,128]{2,1,0:T(8,128)}, u32[]{:S(2)}) copy-start(f32[16,16,128]{2,1,0:T(8,128)} %leak_ref.1) | copy-start | bytes 393220
  3.3 0.9 %copy-start.2 = (f32[16,16,128]{2,1,0:T(8,128)S(1)}, f32[16,16,128]{2,1,0:T(8,128)}, u32[]{:S(2)}) copy-start(f32[16,16,128]{2,1,0:T(8,128)} %source_ref.1) | copy-start | bytes 393220
  4.2 0.9 %copy-start.3 = (f32[16,16,128]{2,1,0:T(8,128)S(1)}, f32[16,16,128]{2,1,0:T(8,128)}, u32[]{:S(2)}) copy-start(f32[16,16,128]{2,1,0:T(8,128)} %weight_ref.1) | copy-start | bytes 393220
  6.2 15.5 %collective-permute-start = (f32[22,16,128]{2,1,0:T(8,128)S(1)}, f32[22,16,128]{2,1,0:T(8,128)S(1)}, u32[]{:S(2)}, u32[]{:S(2)}) collective-permute-start(f32[22,16,128]{2,1,0:T(8,128)S(1)} %get-tuple-element.14), channel_id=1, source_target_pairs={{32,64},{96,128},{160,192},{224,256},{288,320},{352,384},{416,448}... | collective-permute-start | bytes 540680 | tf_op jit(solution)/shard_map/ppermute | solution.py:21
  15.0 6.6 %collective-permute-start.1 = (f32[22,16,128]{2,1,0:T(8,128)S(1)}, f32[22,16,128]{2,1,0:T(8,128)S(1)}, u32[]{:S(2)}, u32[]{:S(2)}) collective-permute-start(f32[22,16,128]{2,1,0:T(8,128)S(1)} %get-tuple-element.15), channel_id=1, source_target_pairs={{0,32},{32,0},{64,96},{96,64},{128,160},{160,128},{192,224},{224,1... | collective-permute-start | bytes 540680 | tf_op jit(solution)/shard_map/ppermute | solution.py:22
  17.0 12.8 %collective-permute-start.2 = (f32[6,16,4,128]{3,2,1,0:T(4,128)S(1)}, f32[6,16,4,128]{3,2,1,0:T(4,128)S(1)}, u32[]{:S(2)}, u32[]{:S(2)}) collective-permute-start(f32[6,16,4,128]{3,2,1,0:T(4,128)S(1)} %get-tuple-element.16), channel_id=1, source_target_pairs={{0,1},{1,0},{2,3},{3,2},{4,5},{5,4},{6,7},{7,6},{8,9},{9,8},{10,11... | collective-permute-start | bytes 589832 | tf_op jit(solution)/shard_map/ppermute | solution.py:22
  21.0 8.8 %collective-permute-start.3 = (f32[6,16,4,128]{3,2,1,0:T(4,128)S(1)}, f32[6,16,4,128]{3,2,1,0:T(4,128)S(1)}, u32[]{:S(2)}, u32[]{:S(2)}) collective-permute-start(f32[6,16,4,128]{3,2,1,0:T(4,128)S(1)} %get-tuple-element.17), channel_id=1, source_target_pairs={{1,2},{3,4},{5,6},{7,8},{9,10},{11,12},{13,14},{15,16},{17,18},{19... | collective-permute-start | bytes 589832 | tf_op jit(solution)/shard_map/ppermute | solution.py:21
  21.8 9.2 %collective-permute-start.4 = (f32[44,4,128]{2,1,0:T(4,128)S(1)}, f32[44,4,128]{2,1,0:T(4,128)S(1)}, u32[]{:S(2)}, u32[]{:S(2)}) collective-permute-start(f32[44,4,128]{2,1,0:T(4,128)S(1)} %get-tuple-element.25), channel_id=1, source_target_pairs={{0,1},{1,0},{2,3},{3,2},{4,5},{5,4},{6,7},{7,6},{8,9},{9,8},{10,11... | collective-permute-start | bytes 270344 | tf_op jit(solution)/shard_map/ppermute | solution.py:22
  29.1 1.9 %collective-permute-start.5 = (f32[44,4,128]{2,1,0:T(4,128)S(1)}, f32[44,4,128]{2,1,0:T(4,128)S(1)}, u32[]{:S(2)}, u32[]{:S(2)}) collective-permute-start(f32[44,4,128]{2,1,0:T(4,128)S(1)} %get-tuple-element.26), channel_id=1, source_target_pairs={{1,2},{3,4},{5,6},{7,8},{9,10},{11,12},{13,14},{15,16},{17,18},{19... | collective-permute-start | bytes 270344 | tf_op jit(solution)/shard_map/ppermute | solution.py:21

commit v4 on v3

--- a/solution.py
+++ b/solution.py
@@ -13,14 +13,17 @@
 SIDE = 64
 
 
-def swapped(one, two, axis, even):
+def traded(one, two, axis):
     count = lax.axis_size(axis)
     inner = [(i, i ^ 1) for i in range(count)]
     outer = [(i, i + 1) for i in range(1, count - 1, 2)]
     outer = outer + [(target, source) for source, target in outer]
     two = lax.ppermute(two, axis, outer)
-    one = lax.ppermute(one, axis, inner)
-    return jnp.where(even, two, one), jnp.where(even, one, two)
+    return lax.ppermute(one, axis, inner), two
+
+
+def is_even(axis):
+    return lax.axis_index(axis) % 2 == 0
 
 
 def up_y(v):
@@ -52,18 +55,39 @@
     return out
 
 
-def pack_kernel(flag_ref, level_ref, mask_ref, elec_ref, leak_ref, source_ref, weight_ref,
-                own_ref, x_one, x_two, y_one, y_two):
+def pack_kernel(level_hbm, mask_hbm, elec_hbm, leak_hbm, source_hbm, weight_hbm,
+                own_ref, x_one, x_two, y_one, y_two,
+                level_ref, mask_ref, elec_ref, leak_ref, source_ref, weight_ref, sems):
     cx, cy, nz = leak_ref.shape
+    ix, iy = lax.axis_index("gx"), lax.axis_index("gy")
+    whole = [(level_hbm, level_ref), (elec_hbm, elec_ref)]
+    first = [pltpu.make_async_copy(a, b, sems.at[k]) for k, (a, b) in enumerate(whole)]
+    half = cx // 2
+    parts = []
+    for h in range(2):
+        at = pl.ds(h * half, half)
+        pairs = [(mask_hbm.at[d, at], mask_ref.at[d, at]) for d in range(3)]
+        pairs += [(leak_hbm.at[at], leak_ref.at[at]), (source_hbm.at[at], source_ref.at[at])]
+        pairs += [(weight_hbm.at[at], weight_ref.at[at])]
+        parts.append(
+            [pltpu.make_async_copy(a, b, sems.at[2 + 6 * h + k]) for k, (a, b) in enumerate(pairs)]
+        )
+    for copy in first + parts[0] + parts[1]:
+        copy.start()
+    for copy in first + parts[0]:
+        copy.wait()
     rows = lax.broadcasted_iota(jnp.int32, (cy, nz), 0)
     cols = lax.broadcasted_iota(jnp.int32, (cy, nz), 1)
-    even_x, even_y = flag_ref[0] == 1, flag_ref[1] == 1
-    keep_x = jnp.where(flag_ref[2] == 1, 0.0, 1.0)
-    keep_y = jnp.where((rows == cy - 1) & (flag_ref[3] == 1), 0.0, 1.0)
+    even_x, even_y = is_even("gx"), is_even("gy")
+    keep_x = jnp.where(ix == lax.axis_size("gx") - 1, 0.0, 1.0)
+    keep_y = jnp.where((rows == cy - 1) & (iy == lax.axis_size("gy") - 1), 0.0, 1.0)
     keep_z = jnp.where(cols == nz - 1, 0.0, 1.0)
     square = lax.broadcasted_iota(jnp.int32, (cy, cy), 0) == lax.broadcasted_iota(jnp.int32, (cy, cy), 1)
     before = None
     for x in range(cx):
+        if x == half:
+            for copy in parts[1]:
+                copy.wait()
         c = [
             jnp.where(mask_ref[d, x] == 1, level_ref[1, d], level_ref[0, d]) for d in range(3)
         ]
@@ -97,9 +121,29 @@
             y_two[f, x] = jnp.where(even_y, low, high)
 
 
-def basis_kernel(own_ref, side_ref, rim_ref, corner_ref, sums_ref, p0, p1, p2, p3, diag, inv, v0):
+def turn_kernel(y_one, y_two, rim_ref, c_one, c_two):
+    cx = y_one.shape[1]
+    even_x, even_y = is_even("gx"), is_even("gy")
+    for f in range(6):
+        for x in range(cx):
+            one, two = y_one[f, x], y_two[f, x]
+            low, high = jnp.where(even_y, two, one), jnp.where(even_y, one, two)
+            rim_ref[f, x] = jnp.concatenate([high, low], axis=0)
+    for k, (f, above, below) in enumerate(slab()):
+        low, high = rim_ref[f, above], rim_ref[f, cx + below]
+        c_one[k] = jnp.where(even_x, high, low)
+        c_two[k] = jnp.where(even_x, low, high)
+
+
+def basis_kernel(own_ref, x_one, x_two, rim_ref, c_one, c_two,
+                 sums_ref, p0, p1, p2, p3, diag, inv, v0, side_ref, corner_ref):
     cx = own_ref.shape[2]
     planes = cx + 2 * DEPTH
+    even = is_even("gx")
+    for one, two, to in ((x_one, x_two, side_ref), (c_one, c_two, corner_ref)):
+        for k in range(SLOTS):
+            to[k] = jnp.where(even, two[k], one[k])
+            to[SLOTS + k] = jnp.where(even, one[k], two[k])
 
     def field(f, x):
         if DEPTH <= x < DEPTH + cx:
@@ -172,7 +216,7 @@
         sums_ref[k] = jnp.broadcast_to(row, sums_ref.shape[1:])
 
 
-def combine_kernel(edge_ref, sums_ref, p0, p1, p2, p3, pot_ref, adj_ref, sens_ref, both):
+def combine_kernel(sums_ref, p0, p1, p2, p3, pot_ref, adj_ref, sens_ref, both):
     cx, cy, nz = pot_ref.shape
     total = jnp.sum(jnp.sum(sums_ref[...], axis=0), axis=0, keepdims=True)
     pair = jnp.concatenate([total, pltpu.roll(total, 128 - SIDE, 1)], axis=0)
@@ -209,8 +253,9 @@
             both[s, x] = v + c[0][s : s + 1] * p0[s, x + DEPTH]
     rows = lax.broadcasted_iota(jnp.int32, (cy, nz), 0)
     cols = lax.broadcasted_iota(jnp.int32, (cy, nz), 1)
-    in_x = jnp.where(edge_ref[2] == 1, 0.0, 1.0)
-    in_y = jnp.where((rows == cy - 1) & (edge_ref[3] == 1), 0.0, 1.0)
+    in_x = jnp.where(lax.axis_index("gx") == lax.axis_size("gx") - 1, 0.0, 1.0)
+    end_y = lax.axis_index("gy") == lax.axis_size("gy") - 1
+    in_y = jnp.where((rows == cy - 1) & end_y, 0.0, 1.0)
     in_z = jnp.where(cols == nz - 1, 0.0, 1.0)
     for x in range(cx):
         p, a = both[0, x], both[1, x]
@@ -226,46 +271,58 @@
 def body(bond_mask, levels, electrode, leakage, source, weight):
     cx, cy, nz = leakage.shape
     shape = (cx, cy, nz)
+    given = (levels, bond_mask, electrode, leakage, source, weight)
     nx, ny = lax.axis_size("gx"), lax.axis_size("gy")
-    ix, iy = lax.axis_index("gx"), lax.axis_index("gy")
-    even_x, even_y = ix % 2 == 0, iy % 2 == 0
-    flags = jnp.stack([even_x, even_y, ix == nx - 1, iy == ny - 1]).astype(jnp.int32)
     vmem = pl.BlockSpec(memory_space=pltpu.VMEM)
-    smem = pl.BlockSpec(memory_space=pltpu.SMEM)
     slots = jax.ShapeDtypeStruct((SLOTS, cy, nz), jnp.float32)
     strip = jax.ShapeDtypeStruct((6, cx, DEPTH, nz), jnp.float32)
     fields, x_one, x_two, y_one, y_two = pl.pallas_call(
         pack_kernel,
         out_shape=[jax.ShapeDtypeStruct((6, *shape), jnp.float32), slots, slots, strip, strip],
-        in_specs=[smem] * 2 + [vmem] * 5,
+        in_specs=[pl.BlockSpec(memory_space=pltpu.HBM)] * 6,
         out_specs=[vmem] * 5,
+        scratch_shapes=[
+            pltpu.SMEM(levels.shape, jnp.float32),
+            pltpu.VMEM(bond_mask.shape, jnp.int32),
+            pltpu.VMEM(electrode.shape, jnp.int32),
+            pltpu.VMEM(shape, jnp.float32),
+            pltpu.VMEM(shape, jnp.float32),
+            pltpu.VMEM(shape, jnp.float32),
+            pltpu.SemaphoreType.DMA((14,)),
+        ],
         compiler_params=pltpu.CompilerParams(vmem_limit_bytes=24 * 2**20),
         name="pack",
-    )(flags, levels, bond_mask, electrode, leakage, source, weight)
-    low, high = swapped(x_one, x_two, "gx", even_x)
-    side = jnp.concatenate([low, high], axis=0)
-    first, last = side[:, :DEPTH], side[:, cy - DEPTH :]
-    corner_one, corner_two = jnp.where(even_y, last, first), jnp.where(even_y, first, last)
-    low, high = swapped(y_one, y_two, "gy", even_y)
-    rim = jnp.concatenate([high, low], axis=2)
-    low, high = swapped(corner_one, corner_two, "gy", even_y)
-    corner = jnp.concatenate([high, low], axis=1)
+    )(*(pltpu.with_memory_space_constraint(a, pltpu.HBM) for a in given))
+    x_one, x_two = traded(x_one, x_two, "gx")
+    y_one, y_two = traded(y_one, y_two, "gy")
+    rest = jax.ShapeDtypeStruct((SLOTS, 2 * DEPTH, nz), jnp.float32)
+    rim, c_one, c_two = pl.pallas_call(
+        turn_kernel,
+        out_shape=[jax.ShapeDtypeStruct((6, cx, 2 * DEPTH, nz), jnp.float32), rest, rest],
+        in_specs=[vmem] * 2,
+        out_specs=[vmem] * 3,
+        compiler_params=pltpu.CompilerParams(vmem_limit_bytes=24 * 2**20),
+        name="turn",
+    )(y_one, y_two)
+    c_one, c_two = traded(c_one, c_two, "gx")
     planes, rows = cx + 2 * DEPTH, cy + 2 * DEPTH
     block = jax.ShapeDtypeStruct((2, planes, rows, nz), jnp.float32)
     parts = nx * ny
     sums, *basis = pl.pallas_call(
         basis_kernel,
         out_shape=[jax.ShapeDtypeStruct((parts // 8, 8, 128), jnp.float32)] + [block] * 4,
-        in_specs=[vmem] * 4,
+        in_specs=[vmem] * 6,
         out_specs=[vmem] * 5,
         scratch_shapes=[
             pltpu.VMEM((planes, rows, nz), jnp.float32),
             pltpu.VMEM((planes, rows, nz), jnp.float32),
             pltpu.VMEM((2, planes, rows, nz), jnp.float32),
+            pltpu.VMEM((2 * SLOTS, cy, nz), jnp.float32),
+            pltpu.VMEM((2 * SLOTS, 2 * DEPTH, nz), jnp.float32),
         ],
         compiler_params=pltpu.CompilerParams(vmem_limit_bytes=24 * 2**20),
         name="basis",
-    )(fields, side, rim, corner)
+    )(fields, x_one, x_two, rim, c_one, c_two)
     gathered = lax.all_to_all(sums.reshape(parts, 1, 128), ("gx", "gy"), 0, 0, tiled=True)
     return pl.pallas_call(
         combine_kernel,
@@ -274,12 +331,12 @@
             jax.ShapeDtypeStruct(shape, jnp.float32),
             jax.ShapeDtypeStruct((3, *shape), jnp.float32),
         ],
-        in_specs=[smem] + [vmem] * 5,
+        in_specs=[vmem] * 5,
         out_specs=[vmem] * 3,
         scratch_shapes=[pltpu.VMEM((2, cx + 1, rows, nz), jnp.float32)],
         compiler_params=pltpu.CompilerParams(vmem_limit_bytes=24 * 2**20),
         name="combine",
-    )(flags, gathered.reshape(parts // 8, 8, 128), *basis)
+    )(gathered.reshape(parts // 8, 8, 128), *basis)
 
 
 def solution(mesh):

time: 76 us -> 73.2 us (0.963)
  local copies, waits for them, and re-layouts: 4.32 us -> 0 us
  waiting for transfers between devices: 1.05 us -> 4.96 us
  blocking collectives: 41.1 us -> 39.9 us
    unnamed x12 -> x0, local copies, waits for them, and re-layouts: 4.32 us -> none
    ppermute x6, waiting for transfers between devices: 1.05 us -> 4.96 us  [the longest x3 4.95 us: traded(): two = lax.ppermute(two, axis, outer)]
    all_to_all x1, blocking collectives: 41.1 us -> 39.9 us  [body(): lax.all_to_all(sums.reshape(parts, 1, 128), ('gx', 'gy'), 0, 0, tiled=True)]
where the time goes in v4:
time: 73.2 us; the launch traced here: 72.9 us
  blocking collectives  39.9 us (55%)
  starting transfers between devices  22.8 us (31%)
  waiting for transfers between devices  4.96 us (7%)
  Pallas kernels  4.55 us (6%)
  between operations  0.74 us (1%)
    all_to_all x1, blocking collectives, body(): lax.all_to_all(sums.reshape(parts, 1, 128), ('gx', 'gy'), 0, 0, tiled=True)  39.9 us
    ppermute x3, starting transfers between devices, traded(): return (lax.ppermute(one, axis, inner), two)  12.6 us
    ppermute x3, starting transfers between devices, traded(): two = lax.ppermute(two, axis, outer)  10.1 us
    ppermute x3, waiting for transfers between devices, traded(): two = lax.ppermute(two, axis, outer)  4.95 us
    pallas_call x1, Pallas kernels, body(): pl.pallas_call(pack_kernel, out_shape=[jax.ShapeDtypeStruct((6, *shape),...  1.72 us
    pallas_call x1, Pallas kernels, body(): pl.pallas_call(basis_kernel, out_shape=[jax.ShapeDtypeStruct((parts // 8,...  1.5 us
  transfers between devices with their start and end apart: 6, of which 1 were waited for; matrix products, arithmetic and copies ran while one was open for 0% of the time, Pallas kernels for 0%

profile of v4, /device:TPU:1, one launch (start us, length us, event | category | flops | bytes accessed | tf_op | source)
XLA Modules:
  0.0 72.9 jit_solution(16248631795291824871)
XLA Ops:
  0.6 1.7 %pack.1 = (f32[6,16,16,128]{3,2,1,0:T(8,128)S(1)}, f32[22,16,128]{2,1,0:T(8,128)S(1)}, f32[22,16,128]{2,1,0:T(8,128)S(1)}, f32[6,16,4,128]{3,2,1,0:T(4,128)S(1)}, f32[6,16,4,128]{3,2,1,0:T(4,128)S(1)}) custom-call(f32[2,3]{1,0:T(2,128)} %level_hbm.1, s32[3,16,16,128]{3,2,1,0:T(8,128)} %mask_hbm.1, s32[2,16,16]{2,1,0:T(8,128)} %elec_hbm.1, ...), custom_call_target="tpu_custom_call" | custom-call | tf_op jit(solution)/shard_map/pack/pallas_call | solution.py:279
  2.4 4.8 %collective-permute-start.2 = (f32[6,16,4,128]{3,2,1,0:T(4,128)S(1)}, f32[6,16,4,128]{3,2,1,0:T(4,128)S(1)}, u32[]{:S(2)}, u32[]{:S(2)}) collective-permute-start(f32[6,16,4,128]{3,2,1,0:T(4,128)S(1)} %get-tuple-element.19), channel_id=1, source_target_pairs={{0,1},{1,0},{2,3},{3,2},{4,5},{5,4},{6,7},{7,6},{8,9},{9,8},{10,11... | collective-permute-start | bytes 589832 | tf_op jit(solution)/shard_map/ppermute | solution.py:22
  7.2 0.7 collective-permute-start.3
  7.9 5.9 %collective-permute-start = (f32[22,16,128]{2,1,0:T(8,128)S(1)}, f32[22,16,128]{2,1,0:T(8,128)S(1)}, u32[]{:S(2)}, u32[]{:S(2)}) collective-permute-start(f32[22,16,128]{2,1,0:T(8,128)S(1)} %get-tuple-element.17), channel_id=1, source_target_pairs={{0,32},{32,0},{64,96},{96,64},{128,160},{160,128},{192,224},{224,1... | collective-permute-start | bytes 540680 | tf_op jit(solution)/shard_map/ppermute | solution.py:22
  13.8 4.3 %collective-permute-start.1 = (f32[22,16,128]{2,1,0:T(8,128)S(1)}, f32[22,16,128]{2,1,0:T(8,128)S(1)}, u32[]{:S(2)}, u32[]{:S(2)}) collective-permute-start(f32[22,16,128]{2,1,0:T(8,128)S(1)} %get-tuple-element.18), channel_id=1, source_target_pairs={{32,64},{96,128},{160,192},{224,256},{288,320},{352,384},{416,448}... | collective-permute-start | bytes 540680 | tf_op jit(solution)/shard_map/ppermute | solution.py:21
  18.1 0.0 collective-permute-done.2.y_one
  18.1 0.0 collective-permute-done.3.y_two
  18.1 0.1 turn.1
  18.2 1.9 %collective-permute-start.4 = (f32[22,8,128]{2,1,0:T(8,128)S(1)}, f32[22,8,128]{2,1,0:T(8,128)S(1)}, u32[]{:S(2)}, u32[]{:S(2)}) collective-permute-start(f32[22,8,128]{2,1,0:T(8,128)S(1)} %get-tuple-element.22), channel_id=1, source_target_pairs={{0,32},{32,0},{64,96},{96,64},{128,160},{160,128},{192,224},{224,1... | collective-permute-start | bytes 270344 | tf_op jit(solution)/shard_map/ppermute | solution.py:22
  20.1 5.1 %collective-permute-start.5 = (f32[22,8,128]{2,1,0:T(8,128)S(1)}, f32[22,8,128]{2,1,0:T(8,128)S(1)}, u32[]{:S(2)}, u32[]{:S(2)}) collective-permute-start(f32[22,8,128]{2,1,0:T(8,128)S(1)} %get-tuple-element.23), channel_id=1, source_target_pairs={{32,64},{96,128},{160,192},{224,256},{288,320},{352,384},{416,448}... | collective-permute-start | bytes 270344 | tf_op jit(solution)/shard_map/ppermute | solution.py:21
  25.3 0.0 collective-permute-done.x_one
  25.3 0.0 collective-permute-done.1.x_two
  25.3 0.0 collective-permute-done.4.c_one
  25.3 4.9 %collective-permute-done.5.c_two = f32[22,8,128]{2,1,0:T(8,128)S(1)} collective-permute-done((f32[22,8,128]{2,1,0:T(8,128)S(1)}, f32[22,8,128]{2,1,0:T(8,128)S(1)}, u32[]{:S(2)}, u32[]{:S(2)}) %collective-permute-start.5) | collective-permute-done | bytes 90144 | tf_op jit(solution)/shard_map/ppermute | solution.py:21
  30.3 1.5 %basis.1 = (f32[64,8,128]{2,1,0:T(8,128)S(1)}, f32[2,24,24,128]{3,2,1,0:T(8,128)S(1)}, f32[2,24,24,128]{3,2,1,0:T(8,128)S(1)}, f32[2,24,24,128]{3,2,1,0:T(8,128)S(1)}, f32[2,24,24,128]{3,2,1,0:T(8,128)S(1)}) custom-call(f32[6,16,16,128]{3,2,1,0:T(8,128)S(1)} %get-tuple-element.16.own_ref, f32[22,16,128]{2,1,0:T(8,128)S(1)} %collective-permute-done.x_one, ...), custom_call_target="tpu_custom_call" | custom-call | tf_op jit(solution)/shard_map/basis/pallas_call | solution.py:311
  31.8 39.9 %all_to_all.5 = f32[512,1,128]{2,1,0:T(1,128)S(1)} all-to-all(f32[512,1,128]{2,1,0:T(1,128)S(1)} %bitcast.5), channel_id=1, replica_groups=mesh['gx'=16,'gy'=32] {'gx','gy'}, dimensions={0} | all-to-all | bytes 524288 | tf_op jit(solution)/shard_map/all_to_all | solution.py:326
  71.6 1.3 %combine.1 = (f32[16,16,128]{2,1,0:T(8,128)}, f32[16,16,128]{2,1,0:T(8,128)}, f32[3,16,16,128]{3,2,1,0:T(8,128)}) custom-call(f32[64,8,128]{2,1,0:T(8,128)S(1)} %bitcast.4, f32[2,24,24,128]{3,2,1,0:T(8,128)S(1)} %get-tuple-element.25.p0, f32[2,24,24,128]{3,2,1,0:T(8,128)S(1)} %get-tuple-element.26.p1, f32[2,24,24,128]{3,2,1,0:T(8,128)S(1)} %get-tuple-element.27.p2, ...), custom_call_target="tpu_custom_call" | custom-call | tf_op jit(solution)/shard_map/combine/pallas_call | solution.py:327
Async XLA Ops:
  2.4 15.8 %collective-permute-start.2 = (f32[6,16,4,128]{3,2,1,0:T(4,128)S(1)}, f32[6,16,4,128]{3,2,1,0:T(4,128)S(1)}, u32[]{:S(2)}, u32[]{:S(2)}) collective-permute-start(f32[6,16,4,128]{3,2,1,0:T(4,128)S(1)} %get-tuple-element.19), channel_id=1, source_target_pairs={{0,1},{1,0},{2,3},{3,2},{4,5},{5,4},{6,7},{7,6},{8,9},{9,8},{10,11... | collective-permute-start | bytes 589832 | tf_op jit(solution)/shard_map/ppermute | solution.py:22
  7.2 10.9 %collective-permute-start.3 = (f32[6,16,4,128]{3,2,1,0:T(4,128)S(1)}, f32[6,16,4,128]{3,2,1,0:T(4,128)S(1)}, u32[]{:S(2)}, u32[]{:S(2)}) collective-permute-start(f32[6,16,4,128]{3,2,1,0:T(4,128)S(1)} %get-tuple-element.20), channel_id=1, source_target_pairs={{1,2},{3,4},{5,6},{7,8},{9,10},{11,12},{13,14},{15,16},{17,18},{19... | collective-permute-start | bytes 589832 | tf_op jit(solution)/shard_map/ppermute | solution.py:21
  7.9 17.4 %collective-permute-start = (f32[22,16,128]{2,1,0:T(8,128)S(1)}, f32[22,16,128]{2,1,0:T(8,128)S(1)}, u32[]{:S(2)}, u32[]{:S(2)}) collective-permute-start(f32[22,16,128]{2,1,0:T(8,128)S(1)} %get-tuple-element.17), channel_id=1, source_target_pairs={{0,32},{32,0},{64,96},{96,64},{128,160},{160,128},{192,224},{224,1... | collective-permute-start | bytes 540680 | tf_op jit(solution)/shard_map/ppermute | solution.py:22
  13.8 11.5 %collective-permute-start.1 = (f32[22,16,128]{2,1,0:T(8,128)S(1)}, f32[22,16,128]{2,1,0:T(8,128)S(1)}, u32[]{:S(2)}, u32[]{:S(2)}) collective-permute-start(f32[22,16,128]{2,1,0:T(8,128)S(1)} %get-tuple-element.18), channel_id=1, source_target_pairs={{32,64},{96,128},{160,192},{224,256},{288,320},{352,384},{416,448}... | collective-permute-start | bytes 540680 | tf_op jit(solution)/shard_map/ppermute | solution.py:21
  18.2 7.1 %collective-permute-start.4 = (f32[22,8,128]{2,1,0:T(8,128)S(1)}, f32[22,8,128]{2,1,0:T(8,128)S(1)}, u32[]{:S(2)}, u32[]{:S(2)}) collective-permute-start(f32[22,8,128]{2,1,0:T(8,128)S(1)} %get-tuple-element.22), channel_id=1, source_target_pairs={{0,32},{32,0},{64,96},{96,64},{128,160},{160,128},{192,224},{224,1... | collective-permute-start | bytes 270344 | tf_op jit(solution)/shard_map/ppermute | solution.py:22
  20.1 10.1 %collective-permute-start.5 = (f32[22,8,128]{2,1,0:T(8,128)S(1)}, f32[22,8,128]{2,1,0:T(8,128)S(1)}, u32[]{:S(2)}, u32[]{:S(2)}) collective-permute-start(f32[22,8,128]{2,1,0:T(8,128)S(1)} %get-tuple-element.23), channel_id=1, source_target_pairs={{32,64},{96,128},{160,192},{224,256},{288,320},{352,384},{416,448}... | collective-permute-start | bytes 270344 | tf_op jit(solution)/shard_map/ppermute | solution.py:21

commit v5 on v4

--- a/solution.py
+++ b/solution.py
@@ -9,7 +9,9 @@
 
 DEPTH = 4
 SUMS = 14
-SLOTS = 22
+SLOTS = 21
+SPARE = 4
+TILES = 12
 SIDE = 64
 
 
@@ -43,14 +45,14 @@
 
 
 def slot(f, j, above=False):
-    start = (0, 4, 8, 12, 15, 19)[f]
-    return start + j - (0 if above or f in (0, 1, 2, 4) else 1)
+    start = (0, 4, 8, 12, 15, 18)[f]
+    return start + j - (0 if above or f < 3 else 1)
 
 
 def slab():
     out = []
     for f in range(6):
-        count = 3 if f in (3, 5) else DEPTH
+        count = DEPTH if f < 3 else 3
         out += [(f, k, k - count) for k in range(count)]
     return out
 
@@ -110,6 +112,9 @@
         own_ref[2, x] = part
         for d in range(3):
             own_ref[3 + d, x] = c[d]
+    for k in range(SPARE):
+        x_one[SLOTS + k] = jnp.zeros((cy, nz), jnp.float32)
+        x_two[SLOTS + k] = jnp.zeros((cy, nz), jnp.float32)
     for k, (f, above, below) in enumerate(slab()):
         low, high = own_ref[f, above], own_ref[f, cx + below]
         x_one[k] = jnp.where(even_x, high, low)
@@ -129,27 +134,66 @@
             one, two = y_one[f, x], y_two[f, x]
             low, high = jnp.where(even_y, two, one), jnp.where(even_y, one, two)
             rim_ref[f, x] = jnp.concatenate([high, low], axis=0)
-    for k, (f, above, below) in enumerate(slab()):
-        low, high = rim_ref[f, above], rim_ref[f, cx + below]
-        c_one[k] = jnp.where(even_x, high, low)
-        c_two[k] = jnp.where(even_x, low, high)
-
-
-def basis_kernel(own_ref, x_one, x_two, rim_ref, c_one, c_two,
-                 sums_ref, p0, p1, p2, p3, diag, inv, v0, side_ref, corner_ref):
+    at = lax.broadcasted_iota(jnp.int32, (8, 128), 0)
+    for f in range(6):
+        tiles = []
+        for order in ((0, 1, 2, 3), (cx - 1, cx - 2, cx - 3, cx - 4)):
+            near = rim_ref[f, order[0]]
+            if f == 4:
+                near = jnp.where(at == 4, pltpu.roll(rim_ref[f, order[3]], 5, 0), near)
+            third = rim_ref[f, order[2]]
+            far = jnp.where(at == 5, pltpu.roll(third, 6, 0), rim_ref[f, order[1]])
+            far = jnp.where(at == 2, pltpu.roll(third, 2, 0), far)
+            tiles.append((near, far))
+        for k in range(2):
+            low, high = tiles[0][k], tiles[1][k]
+            c_one[2 * f + k] = jnp.where(even_x, high, low)
+            c_two[2 * f + k] = jnp.where(even_x, low, high)
+
+
+def side_kernel(x_one, x_two, side_ref):
+    even = is_even("gx")
+    for k in range(SLOTS):
+        side_ref[k] = jnp.where(even, x_two[k], x_one[k])
+        side_ref[SLOTS + k] = jnp.where(even, x_one[k], x_two[k])
+
+
+def basis_kernel(own_ref, side_ref, rim_ref, c_one, c_two,
+                 sums_ref, p0, p1, p2, p3, diag, inv, v0, corner_ref):
     cx = own_ref.shape[2]
     planes = cx + 2 * DEPTH
     even = is_even("gx")
-    for one, two, to in ((x_one, x_two, side_ref), (c_one, c_two, corner_ref)):
-        for k in range(SLOTS):
-            to[k] = jnp.where(even, two[k], one[k])
-            to[SLOTS + k] = jnp.where(even, one[k], two[k])
+    at = lax.broadcasted_iota(jnp.int32, (8, 128), 0)
+    for f in range(6):
+        for k in range(2):
+            one, two = c_one[2 * f + k], c_two[2 * f + k]
+            corner_ref[0, f, k] = jnp.where(even, two, one)
+            corner_ref[1, f, k] = jnp.where(even, one, two)
+
+    def corner(f, above, depth):
+        if depth == 1:
+            return corner_ref[above, f, 0]
+        if depth == 2:
+            return corner_ref[above, f, 1]
+        if depth == 3:
+            t = corner_ref[above, f, 1]
+            return jnp.where(at == 0, pltpu.roll(t, 6, 0), pltpu.roll(t, 2, 0))
+        if f == 4:
+            return pltpu.roll(corner_ref[above, f, 0], 3, 0)
+        return jnp.zeros((8, 128), jnp.float32)
 
     def field(f, x):
         if DEPTH <= x < DEPTH + cx:
             return jnp.concatenate([own_ref[f, x - DEPTH], rim_ref[f, x - DEPTH]], axis=0)
-        k = slot(f, x) if x < DEPTH else SLOTS + slot(f, x - DEPTH - cx, above=True)
-        return jnp.concatenate([side_ref[k], corner_ref[k]], axis=0)
+        above = int(x >= DEPTH)
+        depth = x - DEPTH - cx + 1 if above else DEPTH - x
+        if f > 2 and depth > 3:
+            flat = jnp.zeros((cx, 128), jnp.float32)
+        elif above:
+            flat = side_ref[SLOTS + slot(f, depth - 1, above=True)]
+        else:
+            flat = side_ref[slot(f, x)]
+        return jnp.concatenate([flat, corner(f, above, depth)], axis=0)
 
     rows = lax.broadcasted_iota(jnp.int32, (cx + 2 * DEPTH, 128), 0)
     seam = (rows == 0) | (rows == cx)
@@ -274,7 +318,7 @@
     given = (levels, bond_mask, electrode, leakage, source, weight)
     nx, ny = lax.axis_size("gx"), lax.axis_size("gy")
     vmem = pl.BlockSpec(memory_space=pltpu.VMEM)
-    slots = jax.ShapeDtypeStruct((SLOTS, cy, nz), jnp.float32)
+    slots = jax.ShapeDtypeStruct((SLOTS + SPARE, cy, nz), jnp.float32)
     strip = jax.ShapeDtypeStruct((6, cx, DEPTH, nz), jnp.float32)
     fields, x_one, x_two, y_one, y_two = pl.pallas_call(
         pack_kernel,
@@ -295,7 +339,16 @@
     )(*(pltpu.with_memory_space_constraint(a, pltpu.HBM) for a in given))
     x_one, x_two = traded(x_one, x_two, "gx")
     y_one, y_two = traded(y_one, y_two, "gy")
-    rest = jax.ShapeDtypeStruct((SLOTS, 2 * DEPTH, nz), jnp.float32)
+    side = pl.pallas_call(
+        side_kernel,
+        out_shape=jax.ShapeDtypeStruct((2 * SLOTS, cy, nz), jnp.float32),
+        in_specs=[vmem] * 2,
+        out_specs=vmem,
+        compiler_params=pltpu.CompilerParams(vmem_limit_bytes=24 * 2**20),
+        cost_estimate=pl.CostEstimate(flops=10**11, bytes_accessed=10**8, transcendentals=0),
+        name="side",
+    )(x_one, x_two)
+    rest = jax.ShapeDtypeStruct((TILES, 2 * DEPTH, nz), jnp.float32)
     rim, c_one, c_two = pl.pallas_call(
         turn_kernel,
         out_shape=[jax.ShapeDtypeStruct((6, cx, 2 * DEPTH, nz), jnp.float32), rest, rest],
@@ -311,18 +364,17 @@
     sums, *basis = pl.pallas_call(
         basis_kernel,
         out_shape=[jax.ShapeDtypeStruct((parts // 8, 8, 128), jnp.float32)] + [block] * 4,
-        in_specs=[vmem] * 6,
+        in_specs=[vmem] * 5,
         out_specs=[vmem] * 5,
         scratch_shapes=[
             pltpu.VMEM((planes, rows, nz), jnp.float32),
             pltpu.VMEM((planes, rows, nz), jnp.float32),
             pltpu.VMEM((2, planes, rows, nz), jnp.float32),
-            pltpu.VMEM((2 * SLOTS, cy, nz), jnp.float32),
-            pltpu.VMEM((2 * SLOTS, 2 * DEPTH, nz), jnp.float32),
+            pltpu.VMEM((2, 6, 2, 2 * DEPTH, nz), jnp.float32),
         ],
         compiler_params=pltpu.CompilerParams(vmem_limit_bytes=24 * 2**20),
         name="basis",
-    )(fields, x_one, x_two, rim, c_one, c_two)
+    )(fields, side, rim, c_one, c_two)
     gathered = lax.all_to_all(sums.reshape(parts, 1, 128), ("gx", "gy"), 0, 0, tiled=True)
     return pl.pallas_call(
         combine_kernel,

time: 73.2 us -> 78.1 us (1.067)
  blocking collectives: 39.9 us -> 42.9 us
  starting transfers between devices: 22.8 us -> 24.7 us
    ppermute x3, waiting for transfers between devices: 4.95 us -> 1.87 us  [traded(): two = lax.ppermute(two, axis, outer)]
    all_to_all x1, blocking collectives: 39.9 us -> 42.9 us  [body(): lax.all_to_all(sums.reshape(parts, 1, 128), ('gx', 'gy'), 0, 0, tiled=True)]
    ppermute x3, waiting for transfers between devices: 0.01 us -> 3.01 us  [traded(): return (lax.ppermute(one, axis, inner), two)]
    ppermute x3, starting transfers between devices: 12.6 us -> 14.7 us  [traded(): return (lax.ppermute(one, axis, inner), two)]
  transfers between devices with their start and end apart: 6 -> 6, of which waited for: 1 -> 2; matrix products, arithmetic and copies ran while one was open for 0% -> 0% of each run, Pallas kernels for 0% -> 0%
where the time goes in v5:
time: 78.1 us; the launch traced here: 77.8 us
  blocking collectives  42.9 us (55%)
  starting transfers between devices  24.7 us (32%)
  waiting for transfers between devices  4.87 us (6%)
  Pallas kernels  4.58 us (6%)
    all_to_all x1, blocking collectives, body(): lax.all_to_all(sums.reshape(parts, 1, 128), ('gx', 'gy'), 0, 0, tiled=True)  42.9 us
    ppermute x3, starting transfers between devices, traded(): return (lax.ppermute(one, axis, inner), two)  14.7 us
    ppermute x3, starting transfers between devices, traded(): two = lax.ppermute(two, axis, outer)  10 us
    ppermute x3, waiting for transfers between devices, traded(): return (lax.ppermute(one, axis, inner), two)  3.01 us
    ppermute x3, waiting for transfers between devices, traded(): two = lax.ppermute(two, axis, outer)  1.87 us
    pallas_call x1, Pallas kernels, body(): pl.pallas_call(pack_kernel, out_shape=[jax.ShapeDtypeStruct((6, *shape),...  1.72 us
  transfers between devices with their start and end apart: 6, of which 2 were waited for; matrix products, arithmetic and copies ran while one was open for 0% of the time, Pallas kernels for 0%

profile of v5, /device:TPU:1, one launch (start us, length us, event | category | flops | bytes accessed | tf_op | source)
XLA Modules:
  0.0 77.8 jit_solution(7948399670015835064)
XLA Ops:
  0.6 1.7 %pack.1 = (f32[6,16,16,128]{3,2,1,0:T(8,128)S(1)}, f32[25,16,128]{2,1,0:T(8,128)S(1)}, f32[25,16,128]{2,1,0:T(8,128)S(1)}, f32[6,16,4,128]{3,2,1,0:T(4,128)S(1)}, f32[6,16,4,128]{3,2,1,0:T(4,128)S(1)}) custom-call(f32[2,3]{1,0:T(2,128)} %level_hbm.1, s32[3,16,16,128]{3,2,1,0:T(8,128)} %mask_hbm.1, s32[2,16,16]{2,1,0:T(8,128)} %elec_hbm.1, ...), custom_call_target="tpu_custom_call" | custom-call | tf_op jit(solution)/shard_map/pack/pallas_call | solution.py:323
  2.4 8.8 %collective-permute-start = (f32[25,16,128]{2,1,0:T(8,128)S(1)}, f32[25,16,128]{2,1,0:T(8,128)S(1)}, u32[]{:S(2)}, u32[]{:S(2)}) collective-permute-start(f32[25,16,128]{2,1,0:T(8,128)S(1)} %get-tuple-element.17), channel_id=1, source_target_pairs={{0,32},{32,0},{64,96},{96,64},{128,160},{160,128},{192,224},{224,1... | collective-permute-start | bytes 614408 | tf_op jit(solution)/shard_map/ppermute | solution.py:24
  11.2 2.0 %collective-permute-start.1 = (f32[25,16,128]{2,1,0:T(8,128)S(1)}, f32[25,16,128]{2,1,0:T(8,128)S(1)}, u32[]{:S(2)}, u32[]{:S(2)}) collective-permute-start(f32[25,16,128]{2,1,0:T(8,128)S(1)} %get-tuple-element.18), channel_id=1, source_target_pairs={{32,64},{96,128},{160,192},{224,256},{288,320},{352,384},{416,448}... | collective-permute-start | bytes 614408 | tf_op jit(solution)/shard_map/ppermute | solution.py:23
  13.1 4.0 %collective-permute-start.2 = (f32[6,16,4,128]{3,2,1,0:T(4,128)S(1)}, f32[6,16,4,128]{3,2,1,0:T(4,128)S(1)}, u32[]{:S(2)}, u32[]{:S(2)}) collective-permute-start(f32[6,16,4,128]{3,2,1,0:T(4,128)S(1)} %get-tuple-element.19), channel_id=1, source_target_pairs={{0,1},{1,0},{2,3},{3,2},{4,5},{5,4},{6,7},{7,6},{8,9},{9,8},{10,11... | collective-permute-start | bytes 589832 | tf_op jit(solution)/shard_map/ppermute | solution.py:24
  17.1 0.7 collective-permute-start.3
  17.8 3.0 %collective-permute-done.2.y_one = f32[6,16,4,128]{3,2,1,0:T(4,128)S(1)} collective-permute-done((f32[6,16,4,128]{3,2,1,0:T(4,128)S(1)}, f32[6,16,4,128]{3,2,1,0:T(4,128)S(1)}, u32[]{:S(2)}, u32[]{:S(2)}) %collective-permute-start.2) | collective-permute-done | bytes 196640 | tf_op jit(solution)/shard_map/ppermute | solution.py:24
  20.8 0.0 collective-permute-done.3.y_two
  20.8 0.1 turn.1
  20.9 1.9 %collective-permute-start.4 = (f32[12,8,128]{2,1,0:T(8,128)S(1)}, f32[12,8,128]{2,1,0:T(8,128)S(1)}, u32[]{:S(2)}, u32[]{:S(2)}) collective-permute-start(f32[12,8,128]{2,1,0:T(8,128)S(1)} %get-tuple-element.22), channel_id=1, source_target_pairs={{0,32},{32,0},{64,96},{96,64},{128,160},{160,128},{192,224},{224,1... | collective-permute-start | bytes 147464 | tf_op jit(solution)/shard_map/ppermute | solution.py:24
  22.8 7.4 %collective-permute-start.5 = (f32[12,8,128]{2,1,0:T(8,128)S(1)}, f32[12,8,128]{2,1,0:T(8,128)S(1)}, u32[]{:S(2)}, u32[]{:S(2)}) collective-permute-start(f32[12,8,128]{2,1,0:T(8,128)S(1)} %get-tuple-element.23), channel_id=1, source_target_pairs={{32,64},{96,128},{160,192},{224,256},{288,320},{352,384},{416,448}... | collective-permute-start | bytes 147464 | tf_op jit(solution)/shard_map/ppermute | solution.py:23
  30.2 0.0 collective-permute-done.x_one
  30.2 0.0 collective-permute-done.1.x_two
  30.3 0.0 collective-permute-done.4.c_one
  30.3 1.9 %collective-permute-done.5.c_two = f32[12,8,128]{2,1,0:T(8,128)S(1)} collective-permute-done((f32[12,8,128]{2,1,0:T(8,128)S(1)}, f32[12,8,128]{2,1,0:T(8,128)S(1)}, u32[]{:S(2)}, u32[]{:S(2)}) %collective-permute-start.5) | collective-permute-done | bytes 49184 | tf_op jit(solution)/shard_map/ppermute | solution.py:23
  32.2 1.5 %basis.1 = (f32[64,8,128]{2,1,0:T(8,128)S(1)}, f32[2,24,24,128]{3,2,1,0:T(8,128)S(1)}, f32[2,24,24,128]{3,2,1,0:T(8,128)S(1)}, f32[2,24,24,128]{3,2,1,0:T(8,128)S(1)}, f32[2,24,24,128]{3,2,1,0:T(8,128)S(1)}) custom-call(f32[6,16,16,128]{3,2,1,0:T(8,128)S(1)} %get-tuple-element.16.own_ref, f32[42,16,128]{2,1,0:T(8,128)S(1)} %side.1.side_ref, ...), custom_call_target="tpu_custom_call" | custom-call | tf_op jit(solution)/shard_map/basis/pallas_call | solution.py:364
  33.7 42.9 %all_to_all.5 = f32[512,1,128]{2,1,0:T(1,128)S(1)} all-to-all(f32[512,1,128]{2,1,0:T(1,128)S(1)} %bitcast.5), channel_id=1, replica_groups=mesh['gx'=16,'gy'=32] {'gx','gy'}, dimensions={0} | all-to-all | bytes 524288 | tf_op jit(solution)/shard_map/all_to_all | solution.py:378
  76.6 1.3 %combine.1 = (f32[16,16,128]{2,1,0:T(8,128)}, f32[16,16,128]{2,1,0:T(8,128)}, f32[3,16,16,128]{3,2,1,0:T(8,128)}) custom-call(f32[64,8,128]{2,1,0:T(8,128)S(1)} %bitcast.4, f32[2,24,24,128]{3,2,1,0:T(8,128)S(1)} %get-tuple-element.25.p0, f32[2,24,24,128]{3,2,1,0:T(8,128)S(1)} %get-tuple-element.26.p1, f32[2,24,24,128]{3,2,1,0:T(8,128)S(1)} %get-tuple-element.27.p2, ...), custom_call_target="tpu_custom_call" | custom-call | tf_op jit(solution)/shard_map/combine/pallas_call | solution.py:379
  (1 shorter events, 0.0 us)
Async XLA Ops:
  2.4 27.9 %collective-permute-start = (f32[25,16,128]{2,1,0:T(8,128)S(1)}, f32[25,16,128]{2,1,0:T(8,128)S(1)}, u32[]{:S(2)}, u32[]{:S(2)}) collective-permute-start(f32[25,16,128]{2,1,0:T(8,128)S(1)} %get-tuple-element.17), channel_id=1, source_target_pairs={{0,32},{32,0},{64,96},{96,64},{128,160},{160,128},{192,224},{224,1... | collective-permute-start | bytes 614408 | tf_op jit(solution)/shard_map/ppermute | solution.py:24
  11.2 19.1 %collective-permute-start.1 = (f32[25,16,128]{2,1,0:T(8,128)S(1)}, f32[25,16,128]{2,1,0:T(8,128)S(1)}, u32[]{:S(2)}, u32[]{:S(2)}) collective-permute-start(f32[25,16,128]{2,1,0:T(8,128)S(1)} %get-tuple-element.18), channel_id=1, source_target_pairs={{32,64},{96,128},{160,192},{224,256},{288,320},{352,384},{416,448}... | collective-permute-start | bytes 614408 | tf_op jit(solution)/shard_map/ppermute | solution.py:23
  13.1 7.7 %collective-permute-start.2 = (f32[6,16,4,128]{3,2,1,0:T(4,128)S(1)}, f32[6,16,4,128]{3,2,1,0:T(4,128)S(1)}, u32[]{:S(2)}, u32[]{:S(2)}) collective-permute-start(f32[6,16,4,128]{3,2,1,0:T(4,128)S(1)} %get-tuple-element.19), channel_id=1, source_target_pairs={{0,1},{1,0},{2,3},{3,2},{4,5},{5,4},{6,7},{7,6},{8,9},{9,8},{10,11... | collective-permute-start | bytes 589832 | tf_op jit(solution)/shard_map/ppermute | solution.py:24
  17.1 3.7 %collective-permute-start.3 = (f32[6,16,4,128]{3,2,1,0:T(4,128)S(1)}, f32[6,16,4,128]{3,2,1,0:T(4,128)S(1)}, u32[]{:S(2)}, u32[]{:S(2)}) collective-permute-start(f32[6,16,4,128]{3,2,1,0:T(4,128)S(1)} %get-tuple-element.20), channel_id=1, source_target_pairs={{1,2},{3,4},{5,6},{7,8},{9,10},{11,12},{13,14},{15,16},{17,18},{19... | collective-permute-start | bytes 589832 | tf_op jit(solution)/shard_map/ppermute | solution.py:23
  20.9 9.4 %collective-permute-start.4 = (f32[12,8,128]{2,1,0:T(8,128)S(1)}, f32[12,8,128]{2,1,0:T(8,128)S(1)}, u32[]{:S(2)}, u32[]{:S(2)}) collective-permute-start(f32[12,8,128]{2,1,0:T(8,128)S(1)} %get-tuple-element.22), channel_id=1, source_target_pairs={{0,32},{32,0},{64,96},{96,64},{128,160},{160,128},{192,224},{224,1... | collective-permute-start | bytes 147464 | tf_op jit(solution)/shard_map/ppermute | solution.py:24
  22.8 9.3 %collective-permute-start.5 = (f32[12,8,128]{2,1,0:T(8,128)S(1)}, f32[12,8,128]{2,1,0:T(8,128)S(1)}, u32[]{:S(2)}, u32[]{:S(2)}) collective-permute-start(f32[12,8,128]{2,1,0:T(8,128)S(1)} %get-tuple-element.23), channel_id=1, source_target_pairs={{32,64},{96,128},{160,192},{224,256},{288,320},{352,384},{416,448}... | collective-permute-start | bytes 147464 | tf_op jit(solution)/shard_map/ppermute | solution.py:23

commit v6 on v5

--- a/solution.py
+++ b/solution.py
@@ -10,7 +10,6 @@
 DEPTH = 4
 SUMS = 14
 SLOTS = 21
-SPARE = 4
 TILES = 12
 SIDE = 64
 
@@ -112,9 +111,6 @@
         own_ref[2, x] = part
         for d in range(3):
             own_ref[3 + d, x] = c[d]
-    for k in range(SPARE):
-        x_one[SLOTS + k] = jnp.zeros((cy, nz), jnp.float32)
-        x_two[SLOTS + k] = jnp.zeros((cy, nz), jnp.float32)
     for k, (f, above, below) in enumerate(slab()):
         low, high = own_ref[f, above], own_ref[f, cx + below]
         x_one[k] = jnp.where(even_x, high, low)
@@ -126,7 +122,7 @@
             y_two[f, x] = jnp.where(even_y, low, high)
 
 
-def turn_kernel(y_one, y_two, rim_ref, c_one, c_two):
+def turn_kernel(y_two, y_one, rim_ref, c_one, c_two):
     cx = y_one.shape[1]
     even_x, even_y = is_even("gx"), is_even("gy")
     for f in range(6):
@@ -151,19 +147,15 @@
             c_two[2 * f + k] = jnp.where(even_x, low, high)
 
 
-def side_kernel(x_one, x_two, side_ref):
-    even = is_even("gx")
-    for k in range(SLOTS):
-        side_ref[k] = jnp.where(even, x_two[k], x_one[k])
-        side_ref[SLOTS + k] = jnp.where(even, x_one[k], x_two[k])
-
-
-def basis_kernel(own_ref, side_ref, rim_ref, c_one, c_two,
-                 sums_ref, p0, p1, p2, p3, diag, inv, v0, corner_ref):
+def basis_kernel(own_ref, rim_ref, x_two, x_one, c_two, c_one,
+                 sums_ref, p0, p1, p2, p3, diag, inv, v0, side_ref, corner_ref):
     cx = own_ref.shape[2]
     planes = cx + 2 * DEPTH
     even = is_even("gx")
     at = lax.broadcasted_iota(jnp.int32, (8, 128), 0)
+    for k in range(SLOTS):
+        side_ref[k] = jnp.where(even, x_two[k], x_one[k])
+        side_ref[SLOTS + k] = jnp.where(even, x_one[k], x_two[k])
     for f in range(6):
         for k in range(2):
             one, two = c_one[2 * f + k], c_two[2 * f + k]
@@ -318,7 +310,7 @@
     given = (levels, bond_mask, electrode, leakage, source, weight)
     nx, ny = lax.axis_size("gx"), lax.axis_size("gy")
     vmem = pl.BlockSpec(memory_space=pltpu.VMEM)
-    slots = jax.ShapeDtypeStruct((SLOTS + SPARE, cy, nz), jnp.float32)
+    slots = jax.ShapeDtypeStruct((SLOTS, cy, nz), jnp.float32)
     strip = jax.ShapeDtypeStruct((6, cx, DEPTH, nz), jnp.float32)
     fields, x_one, x_two, y_one, y_two = pl.pallas_call(
         pack_kernel,
@@ -339,15 +331,6 @@
     )(*(pltpu.with_memory_space_constraint(a, pltpu.HBM) for a in given))
     x_one, x_two = traded(x_one, x_two, "gx")
     y_one, y_two = traded(y_one, y_two, "gy")
-    side = pl.pallas_call(
-        side_kernel,
-        out_shape=jax.ShapeDtypeStruct((2 * SLOTS, cy, nz), jnp.float32),
-        in_specs=[vmem] * 2,
-        out_specs=vmem,
-        compiler_params=pltpu.CompilerParams(vmem_limit_bytes=24 * 2**20),
-        cost_estimate=pl.CostEstimate(flops=10**11, bytes_accessed=10**8, transcendentals=0),
-        name="side",
-    )(x_one, x_two)
     rest = jax.ShapeDtypeStruct((TILES, 2 * DEPTH, nz), jnp.float32)
     rim, c_one, c_two = pl.pallas_call(
         turn_kernel,
@@ -356,7 +339,7 @@
         out_specs=[vmem] * 3,
         compiler_params=pltpu.CompilerParams(vmem_limit_bytes=24 * 2**20),
         name="turn",
-    )(y_one, y_two)
+    )(y_two, y_one)
     c_one, c_two = traded(c_one, c_two, "gx")
     planes, rows = cx + 2 * DEPTH, cy + 2 * DEPTH
     block = jax.ShapeDtypeStruct((2, planes, rows, nz), jnp.float32)
@@ -364,17 +347,18 @@
     sums, *basis = pl.pallas_call(
         basis_kernel,
         out_shape=[jax.ShapeDtypeStruct((parts // 8, 8, 128), jnp.float32)] + [block] * 4,
-        in_specs=[vmem] * 5,
+        in_specs=[vmem] * 6,
         out_specs=[vmem] * 5,
         scratch_shapes=[
             pltpu.VMEM((planes, rows, nz), jnp.float32),
             pltpu.VMEM((planes, rows, nz), jnp.float32),
             pltpu.VMEM((2, planes, rows, nz), jnp.float32),
+            pltpu.VMEM((2 * SLOTS, cy, nz), jnp.float32),
             pltpu.VMEM((2, 6, 2, 2 * DEPTH, nz), jnp.float32),
         ],
         compiler_params=pltpu.CompilerParams(vmem_limit_bytes=24 * 2**20),
         name="basis",
-    )(fields, side, rim, c_one, c_two)
+    )(fields, rim, x_two, x_one, c_two, c_one)
     gathered = lax.all_to_all(sums.reshape(parts, 1, 128), ("gx", "gy"), 0, 0, tiled=True)
     return pl.pallas_call(
         combine_kernel,

time: 78.1 us -> 68.9 us (0.88)
  blocking collectives: 42.9 us -> 33.7 us
    all_to_all x1, blocking collectives: 42.9 us -> 33.7 us  [body(): lax.all_to_all(sums.reshape(parts, 1, 128), ('gx', 'gy'), 0, 0, tiled=True)]
    ppermute x3, waiting for transfers between devices: 1.87 us -> 5.22 us  [traded(): two = lax.ppermute(two, axis, outer)]
    ppermute x3, waiting for transfers between devices: 3.01 us -> 0.01 us  [traded(): return (lax.ppermute(one, axis, inner), two)]
    ppermute x3, starting transfers between devices: 14.7 us -> 12 us  [traded(): return (lax.ppermute(one, axis, inner), two)]
    ppermute x3, starting transfers between devices: 10 us -> 12.3 us  [traded(): two = lax.ppermute(two, axis, outer)]
  transfers between devices with their start and end apart: 6 -> 6, of which waited for: 2 -> 1; matrix products, arithmetic and copies ran while one was open for 0% -> 0% of each run, Pallas kernels for 0% -> 0%
where the time goes in v6:
time: 68.9 us; the launch traced here: 68.6 us
  blocking collectives  33.7 us (49%)
  starting transfers between devices  24.3 us (35%)
  waiting for transfers between devices  5.23 us (8%)
  Pallas kernels  4.57 us (7%)
  between operations  0.73 us (1%)
    all_to_all x1, blocking collectives, body(): lax.all_to_all(sums.reshape(parts, 1, 128), ('gx', 'gy'), 0, 0, tiled=True)  33.7 us
    ppermute x3, starting transfers between devices, traded(): two = lax.ppermute(two, axis, outer)  12.3 us
    ppermute x3, starting transfers between devices, traded(): return (lax.ppermute(one, axis, inner), two)  12 us
    ppermute x3, waiting for transfers between devices, traded(): two = lax.ppermute(two, axis, outer)  5.22 us
    pallas_call x1, Pallas kernels, body(): pl.pallas_call(pack_kernel, out_shape=[jax.ShapeDtypeStruct((6, *shape),...  1.72 us
    pallas_call x1, Pallas kernels, body(): pl.pallas_call(basis_kernel, out_shape=[jax.ShapeDtypeStruct((parts // 8,...  1.52 us
  transfers between devices with their start and end apart: 6, of which 1 were waited for; matrix products, arithmetic and copies ran while one was open for 0% of the time, Pallas kernels for 0%

profile of v6, /device:TPU:1, one launch (start us, length us, event | category | flops | bytes accessed | tf_op | source)
XLA Modules:
  0.0 68.6 jit_solution(9704987528783195493)
XLA Ops:
  0.6 1.7 %pack.1 = (f32[6,16,16,128]{3,2,1,0:T(8,128)S(1)}, f32[21,16,128]{2,1,0:T(8,128)S(1)}, f32[21,16,128]{2,1,0:T(8,128)S(1)}, f32[6,16,4,128]{3,2,1,0:T(4,128)S(1)}, f32[6,16,4,128]{3,2,1,0:T(4,128)S(1)}) custom-call(f32[2,3]{1,0:T(2,128)} %level_hbm.1, s32[3,16,16,128]{3,2,1,0:T(8,128)} %mask_hbm.1, s32[2,16,16]{2,1,0:T(8,128)} %elec_hbm.1, ...), custom_call_target="tpu_custom_call" | custom-call | tf_op jit(solution)/shard_map/pack/pallas_call | solution.py:315
  2.4 0.7 collective-permute-start
  3.0 8.2 %collective-permute-start.1 = (f32[6,16,4,128]{3,2,1,0:T(4,128)S(1)}, f32[6,16,4,128]{3,2,1,0:T(4,128)S(1)}, u32[]{:S(2)}, u32[]{:S(2)}) collective-permute-start(f32[6,16,4,128]{3,2,1,0:T(4,128)S(1)} %get-tuple-element.18), channel_id=1, source_target_pairs={{0,1},{1,0},{2,3},{3,2},{4,5},{5,4},{6,7},{7,6},{8,9},{9,8},{10,11... | collective-permute-start | bytes 589832 | tf_op jit(solution)/shard_map/ppermute | solution.py:23
  11.2 8.6 %collective-permute-start.2 = (f32[21,16,128]{2,1,0:T(8,128)S(1)}, f32[21,16,128]{2,1,0:T(8,128)S(1)}, u32[]{:S(2)}, u32[]{:S(2)}) collective-permute-start(f32[21,16,128]{2,1,0:T(8,128)S(1)} %get-tuple-element.20), channel_id=1, source_target_pairs={{32,64},{96,128},{160,192},{224,256},{288,320},{352,384},{416,448}... | collective-permute-start | bytes 516104 | tf_op jit(solution)/shard_map/ppermute | solution.py:22
  19.8 1.9 %collective-permute-start.3 = (f32[21,16,128]{2,1,0:T(8,128)S(1)}, f32[21,16,128]{2,1,0:T(8,128)S(1)}, u32[]{:S(2)}, u32[]{:S(2)}) collective-permute-start(f32[21,16,128]{2,1,0:T(8,128)S(1)} %get-tuple-element.21), channel_id=1, source_target_pairs={{0,32},{32,0},{64,96},{96,64},{128,160},{160,128},{192,224},{224,1... | collective-permute-start | bytes 516104 | tf_op jit(solution)/shard_map/ppermute | solution.py:23
  21.7 0.0 collective-permute-done.y_two
  21.7 0.0 collective-permute-done.1.y_one
  21.7 0.1 turn.1
  21.8 3.0 %collective-permute-start.4 = (f32[12,8,128]{2,1,0:T(8,128)S(1)}, f32[12,8,128]{2,1,0:T(8,128)S(1)}, u32[]{:S(2)}, u32[]{:S(2)}) collective-permute-start(f32[12,8,128]{2,1,0:T(8,128)S(1)} %get-tuple-element.22), channel_id=1, source_target_pairs={{32,64},{96,128},{160,192},{224,256},{288,320},{352,384},{416,448}... | collective-permute-start | bytes 147464 | tf_op jit(solution)/shard_map/ppermute | solution.py:22
  24.9 1.9 %collective-permute-start.5 = (f32[12,8,128]{2,1,0:T(8,128)S(1)}, f32[12,8,128]{2,1,0:T(8,128)S(1)}, u32[]{:S(2)}, u32[]{:S(2)}) collective-permute-start(f32[12,8,128]{2,1,0:T(8,128)S(1)} %get-tuple-element.23), channel_id=1, source_target_pairs={{0,32},{32,0},{64,96},{96,64},{128,160},{160,128},{192,224},{224,1... | collective-permute-start | bytes 147464 | tf_op jit(solution)/shard_map/ppermute | solution.py:23
  26.8 0.0 collective-permute-done.2.x_two
  26.8 0.0 collective-permute-done.3.x_one
  26.8 5.2 %collective-permute-done.4.c_two = f32[12,8,128]{2,1,0:T(8,128)S(1)} collective-permute-done((f32[12,8,128]{2,1,0:T(8,128)S(1)}, f32[12,8,128]{2,1,0:T(8,128)S(1)}, u32[]{:S(2)}, u32[]{:S(2)}) %collective-permute-start.4) | collective-permute-done | bytes 49184 | tf_op jit(solution)/shard_map/ppermute | solution.py:22
  32.0 0.0 collective-permute-done.5.c_one
  32.0 1.5 %basis.1 = (f32[64,8,128]{2,1,0:T(8,128)S(1)}, f32[2,24,24,128]{3,2,1,0:T(8,128)S(1)}, f32[2,24,24,128]{3,2,1,0:T(8,128)S(1)}, f32[2,24,24,128]{3,2,1,0:T(8,128)S(1)}, f32[2,24,24,128]{3,2,1,0:T(8,128)S(1)}) custom-call(f32[6,16,16,128]{3,2,1,0:T(8,128)S(1)} %get-tuple-element.16.own_ref, f32[6,16,8,128]{3,2,1,0:T(8,128)S(1)} %get-tuple-element.19.rim_ref, ...), custom_call_target="tpu_custom_call" | custom-call | tf_op jit(solution)/shard_map/basis/pallas_call | solution.py:347
  33.6 33.7 %all_to_all.5 = f32[512,1,128]{2,1,0:T(1,128)S(1)} all-to-all(f32[512,1,128]{2,1,0:T(1,128)S(1)} %bitcast.5), channel_id=1, replica_groups=mesh['gx'=16,'gy'=32] {'gx','gy'}, dimensions={0} | all-to-all | bytes 524288 | tf_op jit(solution)/shard_map/all_to_all | solution.py:362
  67.3 1.3 %combine.1 = (f32[16,16,128]{2,1,0:T(8,128)}, f32[16,16,128]{2,1,0:T(8,128)}, f32[3,16,16,128]{3,2,1,0:T(8,128)}) custom-call(f32[64,8,128]{2,1,0:T(8,128)S(1)} %bitcast.4, f32[2,24,24,128]{3,2,1,0:T(8,128)S(1)} %get-tuple-element.25.p0, f32[2,24,24,128]{3,2,1,0:T(8,128)S(1)} %get-tuple-element.26.p1, f32[2,24,24,128]{3,2,1,0:T(8,128)S(1)} %get-tuple-element.27.p2, ...), custom_call_target="tpu_custom_call" | custom-call | tf_op jit(solution)/shard_map/combine/pallas_call | solution.py:363
Async XLA Ops:
  2.4 19.4 %collective-permute-start = (f32[6,16,4,128]{3,2,1,0:T(4,128)S(1)}, f32[6,16,4,128]{3,2,1,0:T(4,128)S(1)}, u32[]{:S(2)}, u32[]{:S(2)}) collective-permute-start(f32[6,16,4,128]{3,2,1,0:T(4,128)S(1)} %get-tuple-element.17), channel_id=1, source_target_pairs={{1,2},{3,4},{5,6},{7,8},{9,10},{11,12},{13,14},{15,16},{17,18},{19... | collective-permute-start | bytes 589832 | tf_op jit(solution)/shard_map/ppermute | solution.py:22
  3.0 18.7 %collective-permute-start.1 = (f32[6,16,4,128]{3,2,1,0:T(4,128)S(1)}, f32[6,16,4,128]{3,2,1,0:T(4,128)S(1)}, u32[]{:S(2)}, u32[]{:S(2)}) collective-permute-start(f32[6,16,4,128]{3,2,1,0:T(4,128)S(1)} %get-tuple-element.18), channel_id=1, source_target_pairs={{0,1},{1,0},{2,3},{3,2},{4,5},{5,4},{6,7},{7,6},{8,9},{9,8},{10,11... | collective-permute-start | bytes 589832 | tf_op jit(solution)/shard_map/ppermute | solution.py:23
  11.2 15.6 %collective-permute-start.2 = (f32[21,16,128]{2,1,0:T(8,128)S(1)}, f32[21,16,128]{2,1,0:T(8,128)S(1)}, u32[]{:S(2)}, u32[]{:S(2)}) collective-permute-start(f32[21,16,128]{2,1,0:T(8,128)S(1)} %get-tuple-element.20), channel_id=1, source_target_pairs={{32,64},{96,128},{160,192},{224,256},{288,320},{352,384},{416,448}... | collective-permute-start | bytes 516104 | tf_op jit(solution)/shard_map/ppermute | solution.py:22
  19.8 7.0 %collective-permute-start.3 = (f32[21,16,128]{2,1,0:T(8,128)S(1)}, f32[21,16,128]{2,1,0:T(8,128)S(1)}, u32[]{:S(2)}, u32[]{:S(2)}) collective-permute-start(f32[21,16,128]{2,1,0:T(8,128)S(1)} %get-tuple-element.21), channel_id=1, source_target_pairs={{0,32},{32,0},{64,96},{96,64},{128,160},{160,128},{192,224},{224,1... | collective-permute-start | bytes 516104 | tf_op jit(solution)/shard_map/ppermute | solution.py:23
  21.8 10.2 %collective-permute-start.4 = (f32[12,8,128]{2,1,0:T(8,128)S(1)}, f32[12,8,128]{2,1,0:T(8,128)S(1)}, u32[]{:S(2)}, u32[]{:S(2)}) collective-permute-start(f32[12,8,128]{2,1,0:T(8,128)S(1)} %get-tuple-element.22), channel_id=1, source_target_pairs={{32,64},{96,128},{160,192},{224,256},{288,320},{352,384},{416,448}... | collective-permute-start | bytes 147464 | tf_op jit(solution)/shard_map/ppermute | solution.py:22
  24.9 7.2 %collective-permute-start.5 = (f32[12,8,128]{2,1,0:T(8,128)S(1)}, f32[12,8,128]{2,1,0:T(8,128)S(1)}, u32[]{:S(2)}, u32[]{:S(2)}) collective-permute-start(f32[12,8,128]{2,1,0:T(8,128)S(1)} %get-tuple-element.23), channel_id=1, source_target_pairs={{0,32},{32,0},{64,96},{96,64},{128,160},{160,128},{192,224},{224,1... | collective-permute-start | bytes 147464 | tf_op jit(solution)/shard_map/ppermute | solution.py:23

commit v7 on v6

--- a/solution.py
+++ b/solution.py
@@ -9,8 +9,8 @@
 
 DEPTH = 4
 SUMS = 14
-SLOTS = 21
-TILES = 12
+SLOTS = 15
+TILES = 16
 SIDE = 64
 
 
@@ -43,15 +43,18 @@
     return pltpu.roll(v, 1, 1)
 
 
-def slot(f, j, above=False):
-    start = (0, 4, 8, 12, 15, 18)[f]
-    return start + j - (0 if above or f < 3 else 1)
+def slot(f, j):
+    return (0, 3, 6, 9, 11, 13)[f] + j
+
+
+def sent(f):
+    return 3 if f < 3 else 2
 
 
 def slab():
     out = []
     for f in range(6):
-        count = DEPTH if f < 3 else 3
+        count = sent(f)
         out += [(f, k, k - count) for k in range(count)]
     return out
 
@@ -122,29 +125,62 @@
             y_two[f, x] = jnp.where(even_y, low, high)
 
 
-def turn_kernel(y_two, y_one, rim_ref, c_one, c_two):
-    cx = y_one.shape[1]
+def neighbours(v, above, below, next_x, last_x, cy, cz):
+    beside = above * next_x + below * last_x
+    beside = beside + cy * up_y(v) + dn_y(cy * v)
+    return beside + cz * up_z(v) + dn_z(cz * v)
+
+
+def turn_kernel(y_two, y_one, own_ref, rim_ref, c_one, c_two):
+    cx, cy = own_ref.shape[1:3]
     even_x, even_y = is_even("gx"), is_even("gy")
     for f in range(6):
         for x in range(cx):
             one, two = y_one[f, x], y_two[f, x]
             low, high = jnp.where(even_y, two, one), jnp.where(even_y, one, two)
             rim_ref[f, x] = jnp.concatenate([high, low], axis=0)
+    def field(f, x):
+        return jnp.concatenate([own_ref[f, x], rim_ref[f, x]], axis=0)
+
+    rows = lax.broadcasted_iota(jnp.int32, (cx + 2 * DEPTH, 128), 0)
+    seam = (rows == 0) | (rows == cx)
+
+    def scaled(x):
+        d = field(2, x) + jnp.where(seam, dn_y(field(4, x)), 0.0)
+        r = jnp.where(d > 0.0, 1.0 / d, 0.0)
+        return r, [field(s, x) * r for s in range(2)]
+
+    summed = []
+    for x in (2, cx - 2):
+        (_, last), (r, here), (_, after) = scaled(x - 1), scaled(x), scaled(x + 1)
+        row = []
+        for s in range(2):
+            v = here[s]
+            beside = neighbours(v, field(3, x), field(3, x - 1), after[s], last[s], field(4, x), field(5, x))
+            row.append(v + r * beside)
+        summed.append(row)
     at = lax.broadcasted_iota(jnp.int32, (8, 128), 0)
     for f in range(6):
         tiles = []
-        for order in ((0, 1, 2, 3), (cx - 1, cx - 2, cx - 3, cx - 4)):
+        for e, order in enumerate(((0, 1, 2), (cx - 1, cx - 2, cx - 3))):
             near = rim_ref[f, order[0]]
-            if f == 4:
-                near = jnp.where(at == 4, pltpu.roll(rim_ref[f, order[3]], 5, 0), near)
             third = rim_ref[f, order[2]]
             far = jnp.where(at == 5, pltpu.roll(third, 6, 0), rim_ref[f, order[1]])
             far = jnp.where(at == 2, pltpu.roll(third, 2, 0), far)
+            if f == 4:
+                far = jnp.where(at == 3, pltpu.roll(own_ref[f, order[2], cy - 8 :], 4, 0), far)
+            if f < 2:
+                far = jnp.where(at == 3, pltpu.roll(summed[e][f][cy : cy + 8], 3, 0), far)
             tiles.append((near, far))
         for k in range(2):
             low, high = tiles[0][k], tiles[1][k]
             c_one[2 * f + k] = jnp.where(even_x, high, low)
             c_two[2 * f + k] = jnp.where(even_x, low, high)
+    for s in range(2):
+        for k in range(2):
+            low, high = (summed[e][s][8 * k : 8 * k + 8] for e in range(2))
+            c_one[12 + 2 * s + k] = jnp.where(even_x, high, low)
+            c_two[12 + 2 * s + k] = jnp.where(even_x, low, high)
 
 
 def basis_kernel(own_ref, rim_ref, x_two, x_one, c_two, c_one,
@@ -167,29 +203,25 @@
             return corner_ref[above, f, 0]
         if depth == 2:
             return corner_ref[above, f, 1]
-        if depth == 3:
-            t = corner_ref[above, f, 1]
-            return jnp.where(at == 0, pltpu.roll(t, 6, 0), pltpu.roll(t, 2, 0))
-        if f == 4:
-            return pltpu.roll(corner_ref[above, f, 0], 3, 0)
-        return jnp.zeros((8, 128), jnp.float32)
+        t = corner_ref[above, f, 1]
+        return jnp.where(at == 0, pltpu.roll(t, 6, 0), pltpu.roll(t, 2, 0))
 
     def field(f, x):
         if DEPTH <= x < DEPTH + cx:
             return jnp.concatenate([own_ref[f, x - DEPTH], rim_ref[f, x - DEPTH]], axis=0)
         above = int(x >= DEPTH)
         depth = x - DEPTH - cx + 1 if above else DEPTH - x
-        if f > 2 and depth > 3:
-            flat = jnp.zeros((cx, 128), jnp.float32)
-        elif above:
-            flat = side_ref[SLOTS + slot(f, depth - 1, above=True)]
+        count = sent(f)
+        if depth > count:
+            edge = jnp.where(at == 7, pltpu.roll(corner_ref[above, f, 1], 4, 0), 0.0)
+            flat = jnp.concatenate([jnp.zeros((cx - 8, 128), jnp.float32), edge], axis=0)
         else:
-            flat = side_ref[slot(f, x)]
+            flat = side_ref[SLOTS + slot(f, depth - 1) if above else slot(f, count - depth)]
         return jnp.concatenate([flat, corner(f, above, depth)], axis=0)
 
     rows = lax.broadcasted_iota(jnp.int32, (cx + 2 * DEPTH, 128), 0)
     seam = (rows == 0) | (rows == cx)
-    for x in range(1, planes):
+    for x in range(2, planes - 1):
         d = field(2, x) + jnp.where(seam, dn_y(field(4, x)), 0.0)
         if x in (DEPTH, DEPTH + cx):
             d = d + field(3, x - 1)
@@ -205,16 +237,22 @@
         out = []
         for s in range(2):
             v = ref[s, x]
-            beside = above * ref[s, x + 1] + below * ref[s, x - 1]
-            beside = beside + cy * up_y(v) + dn_y(cy * v)
-            beside = beside + cz * up_z(v) + dn_z(cz * v)
+            beside = neighbours(v, above, below, ref[s, x + 1], ref[s, x - 1], cy, cz)
             out.append((v, r * beside))
         return out
 
-    for x in range(2, planes - 1):
+    for x in range(3, planes - 2):
         for s, (v, w) in enumerate(jacobi(v0, x)):
             p0[s, x] = v + w
             p1[s, x] = v - w
+    for s in range(2):
+        beyond = [jnp.where(at == 0, pltpu.roll(corner_ref[e, s, 1], 5, 0), 0.0) for e in range(2)]
+        one = [c_one[12 + 2 * s + k] for k in range(2)]
+        two = [c_two[12 + 2 * s + k] for k in range(2)]
+        below = [jnp.where(even, b, a) for a, b in zip(one, two)]
+        above = [jnp.where(even, a, b) for a, b in zip(one, two)]
+        p0[s, 2] = jnp.concatenate(below + beyond[:1], axis=0)
+        p0[s, planes - 2] = jnp.concatenate(above + beyond[1:], axis=0)
     for x in range(3, planes - 2):
         for s, (v, w) in enumerate(jacobi(p0, x)):
             p2[s, x] = v - w
@@ -335,11 +373,11 @@
     rim, c_one, c_two = pl.pallas_call(
         turn_kernel,
         out_shape=[jax.ShapeDtypeStruct((6, cx, 2 * DEPTH, nz), jnp.float32), rest, rest],
-        in_specs=[vmem] * 2,
+        in_specs=[vmem] * 3,
         out_specs=[vmem] * 3,
         compiler_params=pltpu.CompilerParams(vmem_limit_bytes=24 * 2**20),
         name="turn",
-    )(y_two, y_one)
+    )(y_two, y_one, fields)
     c_one, c_two = traded(c_one, c_two, "gx")
     planes, rows = cx + 2 * DEPTH, cy + 2 * DEPTH
     block = jax.ShapeDtypeStruct((2, planes, rows, nz), jnp.float32)

time: 68.9 us -> 68.3 us (level)
  waiting for transfers between devices: 5.23 us -> 4.5 us
    ppermute x3, waiting for transfers between devices: 5.22 us -> 4.49 us  [traded(): two = lax.ppermute(two, axis, outer)]
where the time goes in v7:
time: 68.3 us; the launch traced here: 68 us
  blocking collectives  33.9 us (50%)
  starting transfers between devices  24.3 us (36%)
  Pallas kernels  4.58 us (7%)
  waiting for transfers between devices  4.5 us (7%)
  between operations  0.73 us (1%)
    all_to_all x1, blocking collectives, body(): lax.all_to_all(sums.reshape(parts, 1, 128), ('gx', 'gy'), 0, 0, tiled=True)  33.9 us
    ppermute x3, starting transfers between devices, traded(): two = lax.ppermute(two, axis, outer)  12.3 us
    ppermute x3, starting transfers between devices, traded(): return (lax.ppermute(one, axis, inner), two)  12 us
    ppermute x3, waiting for transfers between devices, traded(): two = lax.ppermute(two, axis, outer)  4.49 us
    pallas_call x1, Pallas kernels, body(): pl.pallas_call(pack_kernel, out_shape=[jax.ShapeDtypeStruct((6, *shape),...  1.72 us
    pallas_call x1, Pallas kernels, body(): pl.pallas_call(basis_kernel, out_shape=[jax.ShapeDtypeStruct((parts // 8,...  1.47 us
  transfers between devices with their start and end apart: 6, of which 1 were waited for; matrix products, arithmetic and copies ran while one was open for 0% of the time, Pallas kernels for 0%

profile of v7, /device:TPU:1, one launch (start us, length us, event | category | flops | bytes accessed | tf_op | source)
XLA Modules:
  0.0 68.0 jit_solution(1891235929247175008)
XLA Ops:
  0.6 1.7 %pack.1 = (f32[6,16,16,128]{3,2,1,0:T(8,128)S(1)}, f32[15,16,128]{2,1,0:T(8,128)S(1)}, f32[15,16,128]{2,1,0:T(8,128)S(1)}, f32[6,16,4,128]{3,2,1,0:T(4,128)S(1)}, f32[6,16,4,128]{3,2,1,0:T(4,128)S(1)}) custom-call(f32[2,3]{1,0:T(2,128)} %level_hbm.1, s32[3,16,16,128]{3,2,1,0:T(8,128)} %mask_hbm.1, s32[2,16,16]{2,1,0:T(8,128)} %elec_hbm.1, ...), custom_call_target="tpu_custom_call" | custom-call | tf_op jit(solution)/shard_map/pack/pallas_call | solution.py:353
  2.4 0.7 collective-permute-start
  3.0 8.2 %collective-permute-start.1 = (f32[6,16,4,128]{3,2,1,0:T(4,128)S(1)}, f32[6,16,4,128]{3,2,1,0:T(4,128)S(1)}, u32[]{:S(2)}, u32[]{:S(2)}) collective-permute-start(f32[6,16,4,128]{3,2,1,0:T(4,128)S(1)} %get-tuple-element.18), channel_id=1, source_target_pairs={{0,1},{1,0},{2,3},{3,2},{4,5},{5,4},{6,7},{7,6},{8,9},{9,8},{10,11... | collective-permute-start | bytes 589832 | tf_op jit(solution)/shard_map/ppermute | solution.py:23
  11.2 8.6 %collective-permute-start.2 = (f32[15,16,128]{2,1,0:T(8,128)S(1)}, f32[15,16,128]{2,1,0:T(8,128)S(1)}, u32[]{:S(2)}, u32[]{:S(2)}) collective-permute-start(f32[15,16,128]{2,1,0:T(8,128)S(1)} %get-tuple-element.20), channel_id=1, source_target_pairs={{32,64},{96,128},{160,192},{224,256},{288,320},{352,384},{416,448}... | collective-permute-start | bytes 368648 | tf_op jit(solution)/shard_map/ppermute | solution.py:22
  19.8 1.9 %collective-permute-start.3 = (f32[15,16,128]{2,1,0:T(8,128)S(1)}, f32[15,16,128]{2,1,0:T(8,128)S(1)}, u32[]{:S(2)}, u32[]{:S(2)}) collective-permute-start(f32[15,16,128]{2,1,0:T(8,128)S(1)} %get-tuple-element.21), channel_id=1, source_target_pairs={{0,32},{32,0},{64,96},{96,64},{128,160},{160,128},{192,224},{224,1... | collective-permute-start | bytes 368648 | tf_op jit(solution)/shard_map/ppermute | solution.py:23
  21.7 0.0 collective-permute-done.y_two
  21.7 0.0 collective-permute-done.1.y_one
  21.7 0.1 turn.1
  21.9 3.0 %collective-permute-start.4 = (f32[16,8,128]{2,1,0:T(8,128)S(1)}, f32[16,8,128]{2,1,0:T(8,128)S(1)}, u32[]{:S(2)}, u32[]{:S(2)}) collective-permute-start(f32[16,8,128]{2,1,0:T(8,128)S(1)} %get-tuple-element.22), channel_id=1, source_target_pairs={{32,64},{96,128},{160,192},{224,256},{288,320},{352,384},{416,448}... | collective-permute-start | bytes 196616 | tf_op jit(solution)/shard_map/ppermute | solution.py:22
  24.9 1.9 %collective-permute-start.5 = (f32[16,8,128]{2,1,0:T(8,128)S(1)}, f32[16,8,128]{2,1,0:T(8,128)S(1)}, u32[]{:S(2)}, u32[]{:S(2)}) collective-permute-start(f32[16,8,128]{2,1,0:T(8,128)S(1)} %get-tuple-element.23), channel_id=1, source_target_pairs={{0,32},{32,0},{64,96},{96,64},{128,160},{160,128},{192,224},{224,1... | collective-permute-start | bytes 196616 | tf_op jit(solution)/shard_map/ppermute | solution.py:23
  26.9 0.0 collective-permute-done.2.x_two
  26.9 0.0 collective-permute-done.3.x_one
  26.9 4.5 %collective-permute-done.4.c_two = f32[16,8,128]{2,1,0:T(8,128)S(1)} collective-permute-done((f32[16,8,128]{2,1,0:T(8,128)S(1)}, f32[16,8,128]{2,1,0:T(8,128)S(1)}, u32[]{:S(2)}, u32[]{:S(2)}) %collective-permute-start.4) | collective-permute-done | bytes 65568 | tf_op jit(solution)/shard_map/ppermute | solution.py:22
  31.4 0.0 collective-permute-done.5.c_one
  31.4 1.5 %basis.1 = (f32[64,8,128]{2,1,0:T(8,128)S(1)}, f32[2,24,24,128]{3,2,1,0:T(8,128)S(1)}, f32[2,24,24,128]{3,2,1,0:T(8,128)S(1)}, f32[2,24,24,128]{3,2,1,0:T(8,128)S(1)}, f32[2,24,24,128]{3,2,1,0:T(8,128)S(1)}) custom-call(f32[6,16,16,128]{3,2,1,0:T(8,128)S(1)} %get-tuple-element.16.own_ref, f32[6,16,8,128]{3,2,1,0:T(8,128)S(1)} %get-tuple-element.19.rim_ref, ...), custom_call_target="tpu_custom_call" | custom-call | tf_op jit(solution)/shard_map/basis/pallas_call | solution.py:385
  32.8 33.9 %all_to_all.5 = f32[512,1,128]{2,1,0:T(1,128)S(1)} all-to-all(f32[512,1,128]{2,1,0:T(1,128)S(1)} %bitcast.5), channel_id=1, replica_groups=mesh['gx'=16,'gy'=32] {'gx','gy'}, dimensions={0} | all-to-all | bytes 524288 | tf_op jit(solution)/shard_map/all_to_all | solution.py:400
  66.7 1.3 %combine.1 = (f32[16,16,128]{2,1,0:T(8,128)}, f32[16,16,128]{2,1,0:T(8,128)}, f32[3,16,16,128]{3,2,1,0:T(8,128)}) custom-call(f32[64,8,128]{2,1,0:T(8,128)S(1)} %bitcast.4, f32[2,24,24,128]{3,2,1,0:T(8,128)S(1)} %get-tuple-element.25.p0, f32[2,24,24,128]{3,2,1,0:T(8,128)S(1)} %get-tuple-element.26.p1, f32[2,24,24,128]{3,2,1,0:T(8,128)S(1)} %get-tuple-element.27.p2, ...), custom_call_target="tpu_custom_call" | custom-call | tf_op jit(solution)/shard_map/combine/pallas_call | solution.py:401
Async XLA Ops:
  2.4 19.4 %collective-permute-start = (f32[6,16,4,128]{3,2,1,0:T(4,128)S(1)}, f32[6,16,4,128]{3,2,1,0:T(4,128)S(1)}, u32[]{:S(2)}, u32[]{:S(2)}) collective-permute-start(f32[6,16,4,128]{3,2,1,0:T(4,128)S(1)} %get-tuple-element.17), channel_id=1, source_target_pairs={{1,2},{3,4},{5,6},{7,8},{9,10},{11,12},{13,14},{15,16},{17,18},{19... | collective-permute-start | bytes 589832 | tf_op jit(solution)/shard_map/ppermute | solution.py:22
  3.0 18.7 %collective-permute-start.1 = (f32[6,16,4,128]{3,2,1,0:T(4,128)S(1)}, f32[6,16,4,128]{3,2,1,0:T(4,128)S(1)}, u32[]{:S(2)}, u32[]{:S(2)}) collective-permute-start(f32[6,16,4,128]{3,2,1,0:T(4,128)S(1)} %get-tuple-element.18), channel_id=1, source_target_pairs={{0,1},{1,0},{2,3},{3,2},{4,5},{5,4},{6,7},{7,6},{8,9},{9,8},{10,11... | collective-permute-start | bytes 589832 | tf_op jit(solution)/shard_map/ppermute | solution.py:23
  11.2 15.7 %collective-permute-start.2 = (f32[15,16,128]{2,1,0:T(8,128)S(1)}, f32[15,16,128]{2,1,0:T(8,128)S(1)}, u32[]{:S(2)}, u32[]{:S(2)}) collective-permute-start(f32[15,16,128]{2,1,0:T(8,128)S(1)} %get-tuple-element.20), channel_id=1, source_target_pairs={{32,64},{96,128},{160,192},{224,256},{288,320},{352,384},{416,448}... | collective-permute-start | bytes 368648 | tf_op jit(solution)/shard_map/ppermute | solution.py:22
  19.8 7.1 %collective-permute-start.3 = (f32[15,16,128]{2,1,0:T(8,128)S(1)}, f32[15,16,128]{2,1,0:T(8,128)S(1)}, u32[]{:S(2)}, u32[]{:S(2)}) collective-permute-start(f32[15,16,128]{2,1,0:T(8,128)S(1)} %get-tuple-element.21), channel_id=1, source_target_pairs={{0,32},{32,0},{64,96},{96,64},{128,160},{160,128},{192,224},{224,1... | collective-permute-start | bytes 368648 | tf_op jit(solution)/shard_map/ppermute | solution.py:23
  21.9 9.5 %collective-permute-start.4 = (f32[16,8,128]{2,1,0:T(8,128)S(1)}, f32[16,8,128]{2,1,0:T(8,128)S(1)}, u32[]{:S(2)}, u32[]{:S(2)}) collective-permute-start(f32[16,8,128]{2,1,0:T(8,128)S(1)} %get-tuple-element.22), channel_id=1, source_target_pairs={{32,64},{96,128},{160,192},{224,256},{288,320},{352,384},{416,448}... | collective-permute-start | bytes 196616 | tf_op jit(solution)/shard_map/ppermute | solution.py:22
  24.9 6.4 %collective-permute-start.5 = (f32[16,8,128]{2,1,0:T(8,128)S(1)}, f32[16,8,128]{2,1,0:T(8,128)S(1)}, u32[]{:S(2)}, u32[]{:S(2)}) collective-permute-start(f32[16,8,128]{2,1,0:T(8,128)S(1)} %get-tuple-element.23), channel_id=1, source_target_pairs={{0,32},{32,0},{64,96},{96,64},{128,160},{160,128},{192,224},{224,1... | collective-permute-start | bytes 196616 | tf_op jit(solution)/shard_map/ppermute | solution.py:23

commit v8 on v7

--- a/solution.py
+++ b/solution.py
@@ -14,13 +14,13 @@
 SIDE = 64
 
 
-def traded(one, two, axis):
-    count = lax.axis_size(axis)
-    inner = [(i, i ^ 1) for i in range(count)]
-    outer = [(i, i + 1) for i in range(1, count - 1, 2)]
-    outer = outer + [(target, source) for source, target in outer]
-    two = lax.ppermute(two, axis, outer)
-    return lax.ppermute(one, axis, inner), two
+def trade_one(value, axis):
+    return lax.ppermute(value, axis, [(i, i ^ 1) for i in range(lax.axis_size(axis))])
+
+
+def trade_two(value, axis):
+    outer = [(i, i + 1) for i in range(1, lax.axis_size(axis) - 1, 2)]
+    return lax.ppermute(value, axis, outer + [(target, source) for source, target in outer])
 
 
 def is_even(axis):
@@ -131,8 +131,12 @@
     return beside + cz * up_z(v) + dn_z(cz * v)
 
 
-def turn_kernel(y_two, y_one, own_ref, rim_ref, c_one, c_two):
+def turn_kernel(y_two, y_one, own_ref, x_one, rim_ref, one_ref, c_two):
     cx, cy = own_ref.shape[1:3]
+    c_one = one_ref.at[pl.ds(2 * SLOTS, TILES)]
+    for k in range(SLOTS):
+        one_ref[2 * k] = x_one[k, :8]
+        one_ref[2 * k + 1] = x_one[k, 8:]
     even_x, even_y = is_even("gx"), is_even("gy")
     for f in range(6):
         for x in range(cx):
@@ -183,15 +187,25 @@
             c_two[12 + 2 * s + k] = jnp.where(even_x, low, high)
 
 
-def basis_kernel(own_ref, rim_ref, x_two, x_one, c_two, c_one,
+def slab_kernel(given_ref, out_ref):
+    out_ref[...] = given_ref[...]
+
+
+def far_kernel(slab_hbm, given_ref, out_ref):
+    out_ref[...] = given_ref[...]
+
+
+def basis_kernel(own_ref, rim_ref, x_two, c_two, one_ref,
                  sums_ref, p0, p1, p2, p3, diag, inv, v0, side_ref, corner_ref):
     cx = own_ref.shape[2]
     planes = cx + 2 * DEPTH
     even = is_even("gx")
     at = lax.broadcasted_iota(jnp.int32, (8, 128), 0)
+    c_one = one_ref.at[pl.ds(2 * SLOTS, TILES)]
     for k in range(SLOTS):
-        side_ref[k] = jnp.where(even, x_two[k], x_one[k])
-        side_ref[SLOTS + k] = jnp.where(even, x_one[k], x_two[k])
+        one = jnp.concatenate([one_ref[2 * k], one_ref[2 * k + 1]], axis=0)
+        side_ref[k] = jnp.where(even, x_two[k], one)
+        side_ref[SLOTS + k] = jnp.where(even, one, x_two[k])
     for f in range(6):
         for k in range(2):
             one, two = c_one[2 * f + k], c_two[2 * f + k]
@@ -367,25 +381,46 @@
         compiler_params=pltpu.CompilerParams(vmem_limit_bytes=24 * 2**20),
         name="pack",
     )(*(pltpu.with_memory_space_constraint(a, pltpu.HBM) for a in given))
-    x_one, x_two = traded(x_one, x_two, "gx")
-    y_one, y_two = traded(y_one, y_two, "gy")
+    x_two = trade_two(x_two, "gx")
+    y_one, y_two = trade_one(y_one, "gy"), trade_two(y_two, "gy")
     rest = jax.ShapeDtypeStruct((TILES, 2 * DEPTH, nz), jnp.float32)
-    rim, c_one, c_two = pl.pallas_call(
+    near = jax.ShapeDtypeStruct((2 * SLOTS + TILES, 2 * DEPTH, nz), jnp.float32)
+    rim, one, c_two = pl.pallas_call(
         turn_kernel,
-        out_shape=[jax.ShapeDtypeStruct((6, cx, 2 * DEPTH, nz), jnp.float32), rest, rest],
-        in_specs=[vmem] * 3,
+        out_shape=[jax.ShapeDtypeStruct((6, cx, 2 * DEPTH, nz), jnp.float32), near, rest],
+        in_specs=[vmem] * 4,
         out_specs=[vmem] * 3,
         compiler_params=pltpu.CompilerParams(vmem_limit_bytes=24 * 2**20),
         name="turn",
-    )(y_two, y_one, fields)
-    c_one, c_two = traded(c_one, c_two, "gx")
+    )(y_two, y_one, fields, x_one)
+    c_two = trade_two(c_two, "gx")
+    hint = pl.CostEstimate(flops=10**11, bytes_accessed=10**8, transcendentals=0)
+    x_two = pl.pallas_call(
+        slab_kernel,
+        out_shape=slots,
+        in_specs=[vmem],
+        out_specs=vmem,
+        compiler_params=pltpu.CompilerParams(vmem_limit_bytes=24 * 2**20),
+        cost_estimate=hint,
+        name="slab",
+    )(x_two)
+    c_two = pl.pallas_call(
+        far_kernel,
+        out_shape=rest,
+        in_specs=[pl.BlockSpec(memory_space=pl.ANY), vmem],
+        out_specs=vmem,
+        compiler_params=pltpu.CompilerParams(vmem_limit_bytes=24 * 2**20),
+        cost_estimate=hint,
+        name="far",
+    )(x_two, c_two)
+    one = trade_one(one, "gx")
     planes, rows = cx + 2 * DEPTH, cy + 2 * DEPTH
     block = jax.ShapeDtypeStruct((2, planes, rows, nz), jnp.float32)
     parts = nx * ny
     sums, *basis = pl.pallas_call(
         basis_kernel,
         out_shape=[jax.ShapeDtypeStruct((parts // 8, 8, 128), jnp.float32)] + [block] * 4,
-        in_specs=[vmem] * 6,
+        in_specs=[vmem] * 5,
         out_specs=[vmem] * 5,
         scratch_shapes=[
             pltpu.VMEM((planes, rows, nz), jnp.float32),
@@ -396,7 +431,7 @@
         ],
         compiler_params=pltpu.CompilerParams(vmem_limit_bytes=24 * 2**20),
         name="basis",
-    )(fields, rim, x_two, x_one, c_two, c_one)
+    )(fields, rim, x_two, c_two, one)
     gathered = lax.all_to_all(sums.reshape(parts, 1, 128), ("gx", "gy"), 0, 0, tiled=True)
     return pl.pallas_call(
         combine_kernel,

time: 68.3 us -> 68 us (level)
  local copies, waits for them, and re-layouts: 0 us -> 0.88 us
  blocking collectives: 33.9 us -> 33.1 us
    unnamed x0 -> x4, local copies, waits for them, and re-layouts: none -> 0.88 us
    all_to_all x1, blocking collectives: 33.9 us -> 33.1 us  [body(): lax.all_to_all(sums.reshape(parts, 1, 128), ('gx', 'gy'), 0, 0, tiled=True)]
    ppermute x6 -> x5, starting transfers between devices: 24.3 us -> 24 us  [the longest x3 13.8 us: trade_two(): lax.ppermute(value, axis, outer + [(target, source) for source, target in...]
    ppermute x6 -> x5, waiting for transfers between devices: 4.5 us -> 4.32 us  [the longest x3 4.32 us: trade_two(): lax.ppermute(value, axis, outer + [(target, source) for source, target in...]
  transfers between devices with their start and end apart: 6 -> 5, of which waited for: 1 -> 1; matrix products, arithmetic and copies ran while one was open for 0% -> 0% of each run, Pallas kernels for 0% -> 0%
where the time goes in v8:
time: 68 us; the launch traced here: 67.7 us
  blocking collectives  33.1 us (49%)
  starting transfers between devices  24 us (35%)
  Pallas kernels  4.61 us (7%)
  waiting for transfers between devices  4.32 us (6%)
  local copies, waits for them, and re-layouts  0.88 us (1%)
  between operations  0.75 us (1%)
    all_to_all x1, blocking collectives, body(): lax.all_to_all(sums.reshape(parts, 1, 128), ('gx', 'gy'), 0, 0, tiled=True)  33.1 us
    ppermute x3, starting transfers between devices, trade_two(): lax.ppermute(value, axis, outer + [(target, source) for source, target in...  13.8 us
    ppermute x2, starting transfers between devices, trade_one(): lax.ppermute(value, axis, [(i, i ^ 1) for i in range(lax.axis_size(axis))])  10.2 us
    ppermute x3, waiting for transfers between devices, trade_two(): lax.ppermute(value, axis, outer + [(target, source) for source, target in...  4.32 us
    pallas_call x1, Pallas kernels, body(): pl.pallas_call(pack_kernel, out_shape=[jax.ShapeDtypeStruct((6, *shape),...  1.72 us
    pallas_call x1, Pallas kernels, body(): pl.pallas_call(basis_kernel, out_shape=[jax.ShapeDtypeStruct((parts // 8,...  1.48 us
  transfers between devices with their start and end apart: 5, of which 1 were waited for; matrix products, arithmetic and copies ran while one was open for 0% of the time, Pallas kernels for 0%

profile of v8, /device:TPU:1, one launch (start us, length us, event | category | flops | bytes accessed | tf_op | source)
XLA Modules:
  0.0 67.7 jit_solution(598398497313914051)
XLA Ops:
  0.6 1.7 %pack.1 = (f32[6,16,16,128]{3,2,1,0:T(8,128)S(1)}, f32[15,16,128]{2,1,0:T(8,128)S(1)}, f32[15,16,128]{2,1,0:T(8,128)S(1)}, f32[6,16,4,128]{3,2,1,0:T(4,128)S(1)}, f32[6,16,4,128]{3,2,1,0:T(4,128)S(1)}) custom-call(f32[2,3]{1,0:T(2,128)} %level_hbm.1, s32[3,16,16,128]{3,2,1,0:T(8,128)} %mask_hbm.1, s32[2,16,16]{2,1,0:T(8,128)} %elec_hbm.1, ...), custom_call_target="tpu_custom_call" | custom-call | tf_op jit(solution)/shard_map/pack/pallas_call | solution.py:367
  2.4 0.7 collective-permute-start
  3.0 8.2 %collective-permute-start.1 = (f32[6,16,4,128]{3,2,1,0:T(4,128)S(1)}, f32[6,16,4,128]{3,2,1,0:T(4,128)S(1)}, u32[]{:S(2)}, u32[]{:S(2)}) collective-permute-start(f32[6,16,4,128]{3,2,1,0:T(4,128)S(1)} %get-tuple-element.18), channel_id=1, source_target_pairs={{0,1},{1,0},{2,3},{3,2},{4,5},{5,4},{6,7},{7,6},{8,9},{9,8},{10,11... | collective-permute-start | bytes 589832 | tf_op jit(solution)/shard_map/ppermute | solution.py:18
  11.2 8.6 %collective-permute-start.2 = (f32[15,16,128]{2,1,0:T(8,128)S(1)}, f32[15,16,128]{2,1,0:T(8,128)S(1)}, u32[]{:S(2)}, u32[]{:S(2)}) collective-permute-start(f32[15,16,128]{2,1,0:T(8,128)S(1)} %get-tuple-element.21), channel_id=1, source_target_pairs={{32,64},{96,128},{160,192},{224,256},{288,320},{352,384},{416,448}... | collective-permute-start | bytes 368648 | tf_op jit(solution)/shard_map/ppermute | solution.py:23
  19.8 0.0 collective-permute-done.y_two
  19.8 0.0 collective-permute-done.1.y_one
  19.8 0.1 turn.1
  19.9 0.0 copy-start
  20.0 0.9 %copy-done = f32[6,16,16,128]{3,2,1,0:T(8,128)} copy-done((f32[6,16,16,128]{3,2,1,0:T(8,128)}, f32[6,16,16,128]{3,2,1,0:T(8,128)S(1)}, u32[]{:S(2)}) %copy-start) | copy-done | bytes 786456
  20.8 4.6 %collective-permute-start.3 = (f32[16,8,128]{2,1,0:T(8,128)S(1)}, f32[16,8,128]{2,1,0:T(8,128)S(1)}, u32[]{:S(2)}, u32[]{:S(2)}) collective-permute-start(f32[16,8,128]{2,1,0:T(8,128)S(1)} %get-tuple-element.22), channel_id=1, source_target_pairs={{32,64},{96,128},{160,192},{224,256},{288,320},{352,384},{416,448}... | collective-permute-start | bytes 196616 | tf_op jit(solution)/shard_map/ppermute | solution.py:23
  25.4 0.0 collective-permute-done.2.given_ref
  25.4 0.0 copy-start.1
  25.4 2.1 %collective-permute-start.4 = (f32[46,8,128]{2,1,0:T(8,128)S(1)}, f32[46,8,128]{2,1,0:T(8,128)S(1)}, u32[]{:S(2)}, u32[]{:S(2)}) collective-permute-start(f32[46,8,128]{2,1,0:T(8,128)S(1)} %get-tuple-element.23), channel_id=1, source_target_pairs={{0,32},{32,0},{64,96},{96,64},{128,160},{160,128},{192,224},{224,1... | collective-permute-start | bytes 565256 | tf_op jit(solution)/shard_map/ppermute | solution.py:18
  27.5 4.3 %collective-permute-done.3.given_ref = f32[16,8,128]{2,1,0:T(8,128)S(1)} collective-permute-done((f32[16,8,128]{2,1,0:T(8,128)S(1)}, f32[16,8,128]{2,1,0:T(8,128)S(1)}, u32[]{:S(2)}, u32[]{:S(2)}) %collective-permute-start.3) | collective-permute-done | bytes 65568 | tf_op jit(solution)/shard_map/ppermute | solution.py:23
  31.8 0.0 collective-permute-done.4.one_ref
  31.8 0.0 copy-done.1
  31.8 1.5 %basis.1 = (f32[64,8,128]{2,1,0:T(8,128)S(1)}, f32[2,24,24,128]{3,2,1,0:T(8,128)S(1)}, f32[2,24,24,128]{3,2,1,0:T(8,128)S(1)}, f32[2,24,24,128]{3,2,1,0:T(8,128)S(1)}, f32[2,24,24,128]{3,2,1,0:T(8,128)S(1)}) custom-call(f32[6,16,16,128]{3,2,1,0:T(8,128)S(1)} %copy-done.1, f32[6,16,8,128]{3,2,1,0:T(8,128)S(1)} %get-tuple-element.20.rim_ref, ...), custom_call_target="tpu_custom_call" | custom-call | tf_op jit(solution)/shard_map/basis/pallas_call | solution.py:420
  33.3 33.1 %all_to_all.5 = f32[512,1,128]{2,1,0:T(1,128)S(1)} all-to-all(f32[512,1,128]{2,1,0:T(1,128)S(1)} %bitcast.5), channel_id=1, replica_groups=mesh['gx'=16,'gy'=32] {'gx','gy'}, dimensions={0} | all-to-all | bytes 524288 | tf_op jit(solution)/shard_map/all_to_all | solution.py:435
  66.4 1.3 %combine.1 = (f32[16,16,128]{2,1,0:T(8,128)}, f32[16,16,128]{2,1,0:T(8,128)}, f32[3,16,16,128]{3,2,1,0:T(8,128)}) custom-call(f32[64,8,128]{2,1,0:T(8,128)S(1)} %bitcast.4, f32[2,24,24,128]{3,2,1,0:T(8,128)S(1)} %get-tuple-element.25.p0, f32[2,24,24,128]{3,2,1,0:T(8,128)S(1)} %get-tuple-element.26.p1, f32[2,24,24,128]{3,2,1,0:T(8,128)S(1)} %get-tuple-element.27.p2, ...), custom_call_target="tpu_custom_call" | custom-call | tf_op jit(solution)/shard_map/combine/pallas_call | solution.py:436
  (2 shorter events, 0.0 us)
Async XLA Ops:
  2.4 17.4 %collective-permute-start = (f32[6,16,4,128]{3,2,1,0:T(4,128)S(1)}, f32[6,16,4,128]{3,2,1,0:T(4,128)S(1)}, u32[]{:S(2)}, u32[]{:S(2)}) collective-permute-start(f32[6,16,4,128]{3,2,1,0:T(4,128)S(1)} %get-tuple-element.17), channel_id=1, source_target_pairs={{1,2},{3,4},{5,6},{7,8},{9,10},{11,12},{13,14},{15,16},{17,18},{19... | collective-permute-start | bytes 589832 | tf_op jit(solution)/shard_map/ppermute | solution.py:23
  3.0 16.8 %collective-permute-start.1 = (f32[6,16,4,128]{3,2,1,0:T(4,128)S(1)}, f32[6,16,4,128]{3,2,1,0:T(4,128)S(1)}, u32[]{:S(2)}, u32[]{:S(2)}) collective-permute-start(f32[6,16,4,128]{3,2,1,0:T(4,128)S(1)} %get-tuple-element.18), channel_id=1, source_target_pairs={{0,1},{1,0},{2,3},{3,2},{4,5},{5,4},{6,7},{7,6},{8,9},{9,8},{10,11... | collective-permute-start | bytes 589832 | tf_op jit(solution)/shard_map/ppermute | solution.py:18
  11.2 14.2 %collective-permute-start.2 = (f32[15,16,128]{2,1,0:T(8,128)S(1)}, f32[15,16,128]{2,1,0:T(8,128)S(1)}, u32[]{:S(2)}, u32[]{:S(2)}) collective-permute-start(f32[15,16,128]{2,1,0:T(8,128)S(1)} %get-tuple-element.21), channel_id=1, source_target_pairs={{32,64},{96,128},{160,192},{224,256},{288,320},{352,384},{416,448}... | collective-permute-start | bytes 368648 | tf_op jit(solution)/shard_map/ppermute | solution.py:23
  19.9 0.9 %copy-start = (f32[6,16,16,128]{3,2,1,0:T(8,128)}, f32[6,16,16,128]{3,2,1,0:T(8,128)S(1)}, u32[]{:S(2)}) copy-start(f32[6,16,16,128]{3,2,1,0:T(8,128)S(1)} %get-tuple-element.16.own_ref) | copy-start | bytes 2359300
  20.8 11.0 %collective-permute-start.3 = (f32[16,8,128]{2,1,0:T(8,128)S(1)}, f32[16,8,128]{2,1,0:T(8,128)S(1)}, u32[]{:S(2)}, u32[]{:S(2)}) collective-permute-start(f32[16,8,128]{2,1,0:T(8,128)S(1)} %get-tuple-element.22), channel_id=1, source_target_pairs={{32,64},{96,128},{160,192},{224,256},{288,320},{352,384},{416,448}... | collective-permute-start | bytes 196616 | tf_op jit(solution)/shard_map/ppermute | solution.py:23
  25.4 6.4 %copy-start.1 = (f32[6,16,16,128]{3,2,1,0:T(8,128)S(1)}, f32[6,16,16,128]{3,2,1,0:T(8,128)}, u32[]{:S(2)}) copy-start(f32[6,16,16,128]{3,2,1,0:T(8,128)} %copy-done) | copy-start | bytes 2359300
  25.4 6.4 %collective-permute-start.4 = (f32[46,8,128]{2,1,0:T(8,128)S(1)}, f32[46,8,128]{2,1,0:T(8,128)S(1)}, u32[]{:S(2)}, u32[]{:S(2)}) collective-permute-start(f32[46,8,128]{2,1,0:T(8,128)S(1)} %get-tuple-element.23), channel_id=1, source_target_pairs={{0,32},{32,0},{64,96},{96,64},{128,160},{160,128},{192,224},{224,1... | collective-permute-start | bytes 565256 | tf_op jit(solution)/shard_map/ppermute | solution.py:18

commit v9 on v8

--- a/solution.py
+++ b/solution.py
@@ -394,7 +394,7 @@
         name="turn",
     )(y_two, y_one, fields, x_one)
     c_two = trade_two(c_two, "gx")
-    hint = pl.CostEstimate(flops=10**11, bytes_accessed=10**8, transcendentals=0)
+    hint = pl.CostEstimate(flops=10**10, bytes_accessed=10**6, transcendentals=0)
     x_two = pl.pallas_call(
         slab_kernel,
         out_shape=slots,

time: 68 us -> 69.1 us (1.016)
  blocking collectives: 33.1 us -> 35.1 us
  local copies, waits for them, and re-layouts: 0.88 us -> 0 us
    all_to_all x1, blocking collectives: 33.1 us -> 35.1 us  [body(): lax.all_to_all(sums.reshape(parts, 1, 128), ('gx', 'gy'), 0, 0, tiled=True)]
    unnamed x4 -> x0, local copies, waits for them, and re-layouts: 0.88 us -> none
where the time goes in v9:
time: 69.1 us; the launch traced here: 68.8 us
  blocking collectives  35.1 us (51%)
  starting transfers between devices  23.9 us (35%)
  Pallas kernels  4.61 us (7%)
  waiting for transfers between devices  4.47 us (6%)
  between operations  0.73 us (1%)
    all_to_all x1, blocking collectives, body(): lax.all_to_all(sums.reshape(parts, 1, 128), ('gx', 'gy'), 0, 0, tiled=True)  35.1 us
    ppermute x3, starting transfers between devices, trade_two(): lax.ppermute(value, axis, outer + [(target, source) for source, target in...  13.8 us
    ppermute x2, starting transfers between devices, trade_one(): lax.ppermute(value, axis, [(i, i ^ 1) for i in range(lax.axis_size(axis))])  10.1 us
    ppermute x3, waiting for transfers between devices, trade_two(): lax.ppermute(value, axis, outer + [(target, source) for source, target in...  4.46 us
    pallas_call x1, Pallas kernels, body(): pl.pallas_call(pack_kernel, out_shape=[jax.ShapeDtypeStruct((6, *shape),...  1.72 us
    pallas_call x1, Pallas kernels, body(): pl.pallas_call(basis_kernel, out_shape=[jax.ShapeDtypeStruct((parts // 8,...  1.48 us
  transfers between devices with their start and end apart: 5, of which 1 were waited for; matrix products, arithmetic and copies ran while one was open for 0% of the time, Pallas kernels for 0%

profile of v9, /device:TPU:1, one launch (start us, length us, event | category | flops | bytes accessed | tf_op | source)
XLA Modules:
  0.0 68.8 jit_solution(1619480298477899070)
XLA Ops:
  0.6 1.7 %pack.1 = (f32[6,16,16,128]{3,2,1,0:T(8,128)S(1)}, f32[15,16,128]{2,1,0:T(8,128)S(1)}, f32[15,16,128]{2,1,0:T(8,128)S(1)}, f32[6,16,4,128]{3,2,1,0:T(4,128)S(1)}, f32[6,16,4,128]{3,2,1,0:T(4,128)S(1)}) custom-call(f32[2,3]{1,0:T(2,128)} %level_hbm.1, s32[3,16,16,128]{3,2,1,0:T(8,128)} %mask_hbm.1, s32[2,16,16]{2,1,0:T(8,128)} %elec_hbm.1, ...), custom_call_target="tpu_custom_call" | custom-call | tf_op jit(solution)/shard_map/pack/pallas_call | solution.py:367
  2.4 0.7 collective-permute-start
  3.0 8.2 %collective-permute-start.1 = (f32[6,16,4,128]{3,2,1,0:T(4,128)S(1)}, f32[6,16,4,128]{3,2,1,0:T(4,128)S(1)}, u32[]{:S(2)}, u32[]{:S(2)}) collective-permute-start(f32[6,16,4,128]{3,2,1,0:T(4,128)S(1)} %get-tuple-element.18), channel_id=1, source_target_pairs={{0,1},{1,0},{2,3},{3,2},{4,5},{5,4},{6,7},{7,6},{8,9},{9,8},{10,11... | collective-permute-start | bytes 589832 | tf_op jit(solution)/shard_map/ppermute | solution.py:18
  11.2 8.6 %collective-permute-start.2 = (f32[15,16,128]{2,1,0:T(8,128)S(1)}, f32[15,16,128]{2,1,0:T(8,128)S(1)}, u32[]{:S(2)}, u32[]{:S(2)}) collective-permute-start(f32[15,16,128]{2,1,0:T(8,128)S(1)} %get-tuple-element.21), channel_id=1, source_target_pairs={{32,64},{96,128},{160,192},{224,256},{288,320},{352,384},{416,448}... | collective-permute-start | bytes 368648 | tf_op jit(solution)/shard_map/ppermute | solution.py:23
  19.8 0.0 collective-permute-done.y_two
  19.8 0.0 collective-permute-done.1.y_one
  19.8 0.1 turn.1
  19.9 4.6 %collective-permute-start.3 = (f32[16,8,128]{2,1,0:T(8,128)S(1)}, f32[16,8,128]{2,1,0:T(8,128)S(1)}, u32[]{:S(2)}, u32[]{:S(2)}) collective-permute-start(f32[16,8,128]{2,1,0:T(8,128)S(1)} %get-tuple-element.22), channel_id=1, source_target_pairs={{32,64},{96,128},{160,192},{224,256},{288,320},{352,384},{416,448}... | collective-permute-start | bytes 196616 | tf_op jit(solution)/shard_map/ppermute | solution.py:23
  24.5 0.0 collective-permute-done.2.given_ref
  24.6 1.9 %collective-permute-start.4 = (f32[46,8,128]{2,1,0:T(8,128)S(1)}, f32[46,8,128]{2,1,0:T(8,128)S(1)}, u32[]{:S(2)}, u32[]{:S(2)}) collective-permute-start(f32[46,8,128]{2,1,0:T(8,128)S(1)} %get-tuple-element.23), channel_id=1, source_target_pairs={{0,32},{32,0},{64,96},{96,64},{128,160},{160,128},{192,224},{224,1... | collective-permute-start | bytes 565256 | tf_op jit(solution)/shard_map/ppermute | solution.py:18
  26.5 4.5 %collective-permute-done.3.given_ref = f32[16,8,128]{2,1,0:T(8,128)S(1)} collective-permute-done((f32[16,8,128]{2,1,0:T(8,128)S(1)}, f32[16,8,128]{2,1,0:T(8,128)S(1)}, u32[]{:S(2)}, u32[]{:S(2)}) %collective-permute-start.3) | collective-permute-done | bytes 65568 | tf_op jit(solution)/shard_map/ppermute | solution.py:23
  30.9 0.0 collective-permute-done.4.one_ref
  31.0 1.5 %basis.1 = (f32[64,8,128]{2,1,0:T(8,128)S(1)}, f32[2,24,24,128]{3,2,1,0:T(8,128)S(1)}, f32[2,24,24,128]{3,2,1,0:T(8,128)S(1)}, f32[2,24,24,128]{3,2,1,0:T(8,128)S(1)}, f32[2,24,24,128]{3,2,1,0:T(8,128)S(1)}) custom-call(f32[6,16,16,128]{3,2,1,0:T(8,128)S(1)} %get-tuple-element.16.own_ref, f32[6,16,8,128]{3,2,1,0:T(8,128)S(1)} %get-tuple-element.20.rim_ref, ...), custom_call_target="tpu_custom_call" | custom-call | tf_op jit(solution)/shard_map/basis/pallas_call | solution.py:420
  32.4 35.1 %all_to_all.5 = f32[512,1,128]{2,1,0:T(1,128)S(1)} all-to-all(f32[512,1,128]{2,1,0:T(1,128)S(1)} %bitcast.5), channel_id=1, replica_groups=mesh['gx'=16,'gy'=32] {'gx','gy'}, dimensions={0} | all-to-all | bytes 524288 | tf_op jit(solution)/shard_map/all_to_all | solution.py:435
  67.5 1.3 %combine.1 = (f32[16,16,128]{2,1,0:T(8,128)}, f32[16,16,128]{2,1,0:T(8,128)}, f32[3,16,16,128]{3,2,1,0:T(8,128)}) custom-call(f32[64,8,128]{2,1,0:T(8,128)S(1)} %bitcast.4, f32[2,24,24,128]{3,2,1,0:T(8,128)S(1)} %get-tuple-element.25.p0, f32[2,24,24,128]{3,2,1,0:T(8,128)S(1)} %get-tuple-element.26.p1, f32[2,24,24,128]{3,2,1,0:T(8,128)S(1)} %get-tuple-element.27.p2, ...), custom_call_target="tpu_custom_call" | custom-call | tf_op jit(solution)/shard_map/combine/pallas_call | solution.py:436
  (2 shorter events, 0.0 us)
Async XLA Ops:
  2.4 17.4 %collective-permute-start = (f32[6,16,4,128]{3,2,1,0:T(4,128)S(1)}, f32[6,16,4,128]{3,2,1,0:T(4,128)S(1)}, u32[]{:S(2)}, u32[]{:S(2)}) collective-permute-start(f32[6,16,4,128]{3,2,1,0:T(4,128)S(1)} %get-tuple-element.17), channel_id=1, source_target_pairs={{1,2},{3,4},{5,6},{7,8},{9,10},{11,12},{13,14},{15,16},{17,18},{19... | collective-permute-start | bytes 589832 | tf_op jit(solution)/shard_map/ppermute | solution.py:23
  3.0 16.8 %collective-permute-start.1 = (f32[6,16,4,128]{3,2,1,0:T(4,128)S(1)}, f32[6,16,4,128]{3,2,1,0:T(4,128)S(1)}, u32[]{:S(2)}, u32[]{:S(2)}) collective-permute-start(f32[6,16,4,128]{3,2,1,0:T(4,128)S(1)} %get-tuple-element.18), channel_id=1, source_target_pairs={{0,1},{1,0},{2,3},{3,2},{4,5},{5,4},{6,7},{7,6},{8,9},{9,8},{10,11... | collective-permute-start | bytes 589832 | tf_op jit(solution)/shard_map/ppermute | solution.py:18
  11.2 13.3 %collective-permute-start.2 = (f32[15,16,128]{2,1,0:T(8,128)S(1)}, f32[15,16,128]{2,1,0:T(8,128)S(1)}, u32[]{:S(2)}, u32[]{:S(2)}) collective-permute-start(f32[15,16,128]{2,1,0:T(8,128)S(1)} %get-tuple-element.21), channel_id=1, source_target_pairs={{32,64},{96,128},{160,192},{224,256},{288,320},{352,384},{416,448}... | collective-permute-start | bytes 368648 | tf_op jit(solution)/shard_map/ppermute | solution.py:23
  19.9 11.0 %collective-permute-start.3 = (f32[16,8,128]{2,1,0:T(8,128)S(1)}, f32[16,8,128]{2,1,0:T(8,128)S(1)}, u32[]{:S(2)}, u32[]{:S(2)}) collective-permute-start(f32[16,8,128]{2,1,0:T(8,128)S(1)} %get-tuple-element.22), channel_id=1, source_target_pairs={{32,64},{96,128},{160,192},{224,256},{288,320},{352,384},{416,448}... | collective-permute-start | bytes 196616 | tf_op jit(solution)/shard_map/ppermute | solution.py:23
  24.6 6.4 %collective-permute-start.4 = (f32[46,8,128]{2,1,0:T(8,128)S(1)}, f32[46,8,128]{2,1,0:T(8,128)S(1)}, u32[]{:S(2)}, u32[]{:S(2)}) collective-permute-start(f32[46,8,128]{2,1,0:T(8,128)S(1)} %get-tuple-element.23), channel_id=1, source_target_pairs={{0,32},{32,0},{64,96},{96,64},{128,160},{160,128},{192,224},{224,1... | collective-permute-start | bytes 565256 | tf_op jit(solution)/shard_map/ppermute | solution.py:18

commit v10 on v9

--- a/solution.py
+++ b/solution.py
@@ -131,7 +131,7 @@
     return beside + cz * up_z(v) + dn_z(cz * v)
 
 
-def turn_kernel(y_two, y_one, own_ref, x_one, rim_ref, one_ref, c_two):
+def turn_kernel(y_one, y_two, own_ref, x_one, rim_ref, one_ref, c_two):
     cx, cy = own_ref.shape[1:3]
     c_one = one_ref.at[pl.ds(2 * SLOTS, TILES)]
     for k in range(SLOTS):
@@ -392,7 +392,7 @@
         out_specs=[vmem] * 3,
         compiler_params=pltpu.CompilerParams(vmem_limit_bytes=24 * 2**20),
         name="turn",
-    )(y_two, y_one, fields, x_one)
+    )(y_one, y_two, fields, x_one)
     c_two = trade_two(c_two, "gx")
     hint = pl.CostEstimate(flops=10**10, bytes_accessed=10**6, transcendentals=0)
     x_two = pl.pallas_call(

time: 69.1 us -> 70.5 us (1.020)
  blocking collectives: 35.1 us -> 41 us
  starting transfers between devices: 23.9 us -> 19.9 us
    all_to_all x1, blocking collectives: 35.1 us -> 41 us  [body(): lax.all_to_all(sums.reshape(parts, 1, 128), ('gx', 'gy'), 0, 0, tiled=True)]
    ppermute x2, starting transfers between devices: 10.1 us -> 6.75 us  [trade_one(): lax.ppermute(value, axis, [(i, i ^ 1) for i in range(lax.axis_size(axis))])]
where the time goes in v10:
time: 70.5 us; the launch traced here: 70.2 us
  blocking collectives  41 us (58%)
  starting transfers between devices  19.9 us (28%)
  Pallas kernels  4.61 us (7%)
  waiting for transfers between devices  3.92 us (6%)
  between operations  0.73 us (1%)
    all_to_all x1, blocking collectives, body(): lax.all_to_all(sums.reshape(parts, 1, 128), ('gx', 'gy'), 0, 0, tiled=True)  41 us
    ppermute x3, starting transfers between devices, trade_two(): lax.ppermute(value, axis, outer + [(target, source) for source, target in...  13.1 us
    ppermute x2, starting transfers between devices, trade_one(): lax.ppermute(value, axis, [(i, i ^ 1) for i in range(lax.axis_size(axis))])  6.75 us
    ppermute x3, waiting for transfers between devices, trade_two(): lax.ppermute(value, axis, outer + [(target, source) for source, target in...  3.92 us
    pallas_call x1, Pallas kernels, body(): pl.pallas_call(pack_kernel, out_shape=[jax.ShapeDtypeStruct((6, *shape),...  1.72 us
    pallas_call x1, Pallas kernels, body(): pl.pallas_call(basis_kernel, out_shape=[jax.ShapeDtypeStruct((parts // 8,...  1.48 us
  transfers between devices with their start and end apart: 5, of which 1 were waited for; matrix products, arithmetic and copies ran while one was open for 0% of the time, Pallas kernels for 0%

profile of v10, /device:TPU:1, one launch (start us, length us, event | category | flops | bytes accessed | tf_op | source)
XLA Modules:
  0.0 70.2 jit_solution(13615190752895621783)
XLA Ops:
  0.6 1.7 %pack.1 = (f32[6,16,16,128]{3,2,1,0:T(8,128)S(1)}, f32[15,16,128]{2,1,0:T(8,128)S(1)}, f32[15,16,128]{2,1,0:T(8,128)S(1)}, f32[6,16,4,128]{3,2,1,0:T(4,128)S(1)}, f32[6,16,4,128]{3,2,1,0:T(4,128)S(1)}) custom-call(f32[2,3]{1,0:T(2,128)} %level_hbm.1, s32[3,16,16,128]{3,2,1,0:T(8,128)} %mask_hbm.1, s32[2,16,16]{2,1,0:T(8,128)} %elec_hbm.1, ...), custom_call_target="tpu_custom_call" | custom-call | tf_op jit(solution)/shard_map/pack/pallas_call | solution.py:367
  2.4 4.8 %collective-permute-start = (f32[6,16,4,128]{3,2,1,0:T(4,128)S(1)}, f32[6,16,4,128]{3,2,1,0:T(4,128)S(1)}, u32[]{:S(2)}, u32[]{:S(2)}) collective-permute-start(f32[6,16,4,128]{3,2,1,0:T(4,128)S(1)} %get-tuple-element.17), channel_id=1, source_target_pairs={{0,1},{1,0},{2,3},{3,2},{4,5},{5,4},{6,7},{7,6},{8,9},{9,8},{10,11... | collective-permute-start | bytes 589832 | tf_op jit(solution)/shard_map/ppermute | solution.py:18
  7.2 0.7 collective-permute-start.1
  7.9 8.3 %collective-permute-start.2 = (f32[15,16,128]{2,1,0:T(8,128)S(1)}, f32[15,16,128]{2,1,0:T(8,128)S(1)}, u32[]{:S(2)}, u32[]{:S(2)}) collective-permute-start(f32[15,16,128]{2,1,0:T(8,128)S(1)} %get-tuple-element.21), channel_id=1, source_target_pairs={{32,64},{96,128},{160,192},{224,256},{288,320},{352,384},{416,448}... | collective-permute-start | bytes 368648 | tf_op jit(solution)/shard_map/ppermute | solution.py:23
  16.2 0.0 collective-permute-done.y_one
  16.2 0.0 collective-permute-done.1.y_two
  16.2 0.1 turn.1
  16.3 4.2 %collective-permute-start.3 = (f32[16,8,128]{2,1,0:T(8,128)S(1)}, f32[16,8,128]{2,1,0:T(8,128)S(1)}, u32[]{:S(2)}, u32[]{:S(2)}) collective-permute-start(f32[16,8,128]{2,1,0:T(8,128)S(1)} %get-tuple-element.22), channel_id=1, source_target_pairs={{32,64},{96,128},{160,192},{224,256},{288,320},{352,384},{416,448}... | collective-permute-start | bytes 196616 | tf_op jit(solution)/shard_map/ppermute | solution.py:23
  20.5 0.0 collective-permute-done.2.given_ref
  20.6 1.9 %collective-permute-start.4 = (f32[46,8,128]{2,1,0:T(8,128)S(1)}, f32[46,8,128]{2,1,0:T(8,128)S(1)}, u32[]{:S(2)}, u32[]{:S(2)}) collective-permute-start(f32[46,8,128]{2,1,0:T(8,128)S(1)} %get-tuple-element.23), channel_id=1, source_target_pairs={{0,32},{32,0},{64,96},{96,64},{128,160},{160,128},{192,224},{224,1... | collective-permute-start | bytes 565256 | tf_op jit(solution)/shard_map/ppermute | solution.py:18
  22.5 3.9 %collective-permute-done.3.given_ref = f32[16,8,128]{2,1,0:T(8,128)S(1)} collective-permute-done((f32[16,8,128]{2,1,0:T(8,128)S(1)}, f32[16,8,128]{2,1,0:T(8,128)S(1)}, u32[]{:S(2)}, u32[]{:S(2)}) %collective-permute-start.3) | collective-permute-done | bytes 65568 | tf_op jit(solution)/shard_map/ppermute | solution.py:23
  26.4 0.0 collective-permute-done.4.one_ref
  26.4 1.5 %basis.1 = (f32[64,8,128]{2,1,0:T(8,128)S(1)}, f32[2,24,24,128]{3,2,1,0:T(8,128)S(1)}, f32[2,24,24,128]{3,2,1,0:T(8,128)S(1)}, f32[2,24,24,128]{3,2,1,0:T(8,128)S(1)}, f32[2,24,24,128]{3,2,1,0:T(8,128)S(1)}) custom-call(f32[6,16,16,128]{3,2,1,0:T(8,128)S(1)} %get-tuple-element.16.own_ref, f32[6,16,8,128]{3,2,1,0:T(8,128)S(1)} %get-tuple-element.20.rim_ref, ...), custom_call_target="tpu_custom_call" | custom-call | tf_op jit(solution)/shard_map/basis/pallas_call | solution.py:420
  27.9 41.0 %all_to_all.5 = f32[512,1,128]{2,1,0:T(1,128)S(1)} all-to-all(f32[512,1,128]{2,1,0:T(1,128)S(1)} %bitcast.5), channel_id=1, replica_groups=mesh['gx'=16,'gy'=32] {'gx','gy'}, dimensions={0} | all-to-all | bytes 524288 | tf_op jit(solution)/shard_map/all_to_all | solution.py:435
  68.9 1.3 %combine.1 = (f32[16,16,128]{2,1,0:T(8,128)}, f32[16,16,128]{2,1,0:T(8,128)}, f32[3,16,16,128]{3,2,1,0:T(8,128)}) custom-call(f32[64,8,128]{2,1,0:T(8,128)S(1)} %bitcast.4, f32[2,24,24,128]{3,2,1,0:T(8,128)S(1)} %get-tuple-element.25.p0, f32[2,24,24,128]{3,2,1,0:T(8,128)S(1)} %get-tuple-element.26.p1, f32[2,24,24,128]{3,2,1,0:T(8,128)S(1)} %get-tuple-element.27.p2, ...), custom_call_target="tpu_custom_call" | custom-call | tf_op jit(solution)/shard_map/combine/pallas_call | solution.py:436
  (2 shorter events, 0.0 us)
Async XLA Ops:
  2.4 13.8 %collective-permute-start = (f32[6,16,4,128]{3,2,1,0:T(4,128)S(1)}, f32[6,16,4,128]{3,2,1,0:T(4,128)S(1)}, u32[]{:S(2)}, u32[]{:S(2)}) collective-permute-start(f32[6,16,4,128]{3,2,1,0:T(4,128)S(1)} %get-tuple-element.17), channel_id=1, source_target_pairs={{0,1},{1,0},{2,3},{3,2},{4,5},{5,4},{6,7},{7,6},{8,9},{9,8},{10,11... | collective-permute-start | bytes 589832 | tf_op jit(solution)/shard_map/ppermute | solution.py:18
  7.2 9.0 %collective-permute-start.1 = (f32[6,16,4,128]{3,2,1,0:T(4,128)S(1)}, f32[6,16,4,128]{3,2,1,0:T(4,128)S(1)}, u32[]{:S(2)}, u32[]{:S(2)}) collective-permute-start(f32[6,16,4,128]{3,2,1,0:T(4,128)S(1)} %get-tuple-element.18), channel_id=1, source_target_pairs={{1,2},{3,4},{5,6},{7,8},{9,10},{11,12},{13,14},{15,16},{17,18},{19... | collective-permute-start | bytes 589832 | tf_op jit(solution)/shard_map/ppermute | solution.py:23
  7.9 12.7 %collective-permute-start.2 = (f32[15,16,128]{2,1,0:T(8,128)S(1)}, f32[15,16,128]{2,1,0:T(8,128)S(1)}, u32[]{:S(2)}, u32[]{:S(2)}) collective-permute-start(f32[15,16,128]{2,1,0:T(8,128)S(1)} %get-tuple-element.21), channel_id=1, source_target_pairs={{32,64},{96,128},{160,192},{224,256},{288,320},{352,384},{416,448}... | collective-permute-start | bytes 368648 | tf_op jit(solution)/shard_map/ppermute | solution.py:23
  16.3 10.1 %collective-permute-start.3 = (f32[16,8,128]{2,1,0:T(8,128)S(1)}, f32[16,8,128]{2,1,0:T(8,128)S(1)}, u32[]{:S(2)}, u32[]{:S(2)}) collective-permute-start(f32[16,8,128]{2,1,0:T(8,128)S(1)} %get-tuple-element.22), channel_id=1, source_target_pairs={{32,64},{96,128},{160,192},{224,256},{288,320},{352,384},{416,448}... | collective-permute-start | bytes 196616 | tf_op jit(solution)/shard_map/ppermute | solution.py:23
  20.6 5.9 %collective-permute-start.4 = (f32[46,8,128]{2,1,0:T(8,128)S(1)}, f32[46,8,128]{2,1,0:T(8,128)S(1)}, u32[]{:S(2)}, u32[]{:S(2)}) collective-permute-start(f32[46,8,128]{2,1,0:T(8,128)S(1)} %get-tuple-element.23), channel_id=1, source_target_pairs={{0,32},{32,0},{64,96},{96,64},{128,160},{160,128},{192,224},{224,1... | collective-permute-start | bytes 565256 | tf_op jit(solution)/shard_map/ppermute | solution.py:18

commit v11 on v9

--- a/solution.py
+++ b/solution.py
@@ -394,7 +394,7 @@
         name="turn",
     )(y_two, y_one, fields, x_one)
     c_two = trade_two(c_two, "gx")
-    hint = pl.CostEstimate(flops=10**10, bytes_accessed=10**6, transcendentals=0)
+    hint = pl.CostEstimate(flops=10**9, bytes_accessed=10**6, transcendentals=0)
     x_two = pl.pallas_call(
         slab_kernel,
         out_shape=slots,

time: 69.1 us -> 69.4 us (level)
  no operation moved by 1% of the time
where the time goes in v11:
time: 69.4 us; the launch traced here: 69.1 us
  blocking collectives  35 us (50%)
  starting transfers between devices  23.9 us (34%)
  waiting for transfers between devices  4.89 us (7%)
  Pallas kernels  4.61 us (7%)
  between operations  0.73 us (1%)
    all_to_all x1, blocking collectives, body(): lax.all_to_all(sums.reshape(parts, 1, 128), ('gx', 'gy'), 0, 0, tiled=True)  35 us
    ppermute x3, starting transfers between devices, trade_two(): lax.ppermute(value, axis, outer + [(target, source) for source, target in...  13.8 us
    ppermute x2, starting transfers between devices, trade_one(): lax.ppermute(value, axis, [(i, i ^ 1) for i in range(lax.axis_size(axis))])  10.1 us
    ppermute x3, waiting for transfers between devices, trade_two(): lax.ppermute(value, axis, outer + [(target, source) for source, target in...  4.89 us
    pallas_call x1, Pallas kernels, body(): pl.pallas_call(pack_kernel, out_shape=[jax.ShapeDtypeStruct((6, *shape),...  1.72 us
    pallas_call x1, Pallas kernels, body(): pl.pallas_call(basis_kernel, out_shape=[jax.ShapeDtypeStruct((parts // 8,...  1.48 us
  transfers between devices with their start and end apart: 5, of which 1 were waited for; matrix products, arithmetic and copies ran while one was open for 0% of the time, Pallas kernels for 0%

profile of v11, /device:TPU:1, one launch (start us, length us, event | category | flops | bytes accessed | tf_op | source)
XLA Modules:
  0.0 69.1 jit_solution(7245641128291194620)
XLA Ops:
  0.6 1.7 %pack.1 = (f32[6,16,16,128]{3,2,1,0:T(8,128)S(1)}, f32[15,16,128]{2,1,0:T(8,128)S(1)}, f32[15,16,128]{2,1,0:T(8,128)S(1)}, f32[6,16,4,128]{3,2,1,0:T(4,128)S(1)}, f32[6,16,4,128]{3,2,1,0:T(4,128)S(1)}) custom-call(f32[2,3]{1,0:T(2,128)} %level_hbm.1, s32[3,16,16,128]{3,2,1,0:T(8,128)} %mask_hbm.1, s32[2,16,16]{2,1,0:T(8,128)} %elec_hbm.1, ...), custom_call_target="tpu_custom_call" | custom-call | tf_op jit(solution)/shard_map/pack/pallas_call | solution.py:367
  2.4 0.7 collective-permute-start
  3.0 8.2 %collective-permute-start.1 = (f32[6,16,4,128]{3,2,1,0:T(4,128)S(1)}, f32[6,16,4,128]{3,2,1,0:T(4,128)S(1)}, u32[]{:S(2)}, u32[]{:S(2)}) collective-permute-start(f32[6,16,4,128]{3,2,1,0:T(4,128)S(1)} %get-tuple-element.18), channel_id=1, source_target_pairs={{0,1},{1,0},{2,3},{3,2},{4,5},{5,4},{6,7},{7,6},{8,9},{9,8},{10,11... | collective-permute-start | bytes 589832 | tf_op jit(solution)/shard_map/ppermute | solution.py:18
  11.2 8.6 %collective-permute-start.2 = (f32[15,16,128]{2,1,0:T(8,128)S(1)}, f32[15,16,128]{2,1,0:T(8,128)S(1)}, u32[]{:S(2)}, u32[]{:S(2)}) collective-permute-start(f32[15,16,128]{2,1,0:T(8,128)S(1)} %get-tuple-element.21), channel_id=1, source_target_pairs={{32,64},{96,128},{160,192},{224,256},{288,320},{352,384},{416,448}... | collective-permute-start | bytes 368648 | tf_op jit(solution)/shard_map/ppermute | solution.py:23
  19.8 0.0 collective-permute-done.y_two
  19.8 0.0 collective-permute-done.1.y_one
  19.8 0.1 turn.1
  19.9 1.9 %collective-permute-start.4 = (f32[46,8,128]{2,1,0:T(8,128)S(1)}, f32[46,8,128]{2,1,0:T(8,128)S(1)}, u32[]{:S(2)}, u32[]{:S(2)}) collective-permute-start(f32[46,8,128]{2,1,0:T(8,128)S(1)} %get-tuple-element.23), channel_id=1, source_target_pairs={{0,32},{32,0},{64,96},{96,64},{128,160},{160,128},{192,224},{224,1... | collective-permute-start | bytes 565256 | tf_op jit(solution)/shard_map/ppermute | solution.py:18
  21.9 4.6 %collective-permute-start.3 = (f32[16,8,128]{2,1,0:T(8,128)S(1)}, f32[16,8,128]{2,1,0:T(8,128)S(1)}, u32[]{:S(2)}, u32[]{:S(2)}) collective-permute-start(f32[16,8,128]{2,1,0:T(8,128)S(1)} %get-tuple-element.22), channel_id=1, source_target_pairs={{32,64},{96,128},{160,192},{224,256},{288,320},{352,384},{416,448}... | collective-permute-start | bytes 196616 | tf_op jit(solution)/shard_map/ppermute | solution.py:23
  26.5 0.0 collective-permute-done.2.given_ref
  26.5 4.9 %collective-permute-done.3.given_ref = f32[16,8,128]{2,1,0:T(8,128)S(1)} collective-permute-done((f32[16,8,128]{2,1,0:T(8,128)S(1)}, f32[16,8,128]{2,1,0:T(8,128)S(1)}, u32[]{:S(2)}, u32[]{:S(2)}) %collective-permute-start.3) | collective-permute-done | bytes 65568 | tf_op jit(solution)/shard_map/ppermute | solution.py:23
  31.4 0.0 collective-permute-done.4.one_ref
  31.4 1.5 %basis.1 = (f32[64,8,128]{2,1,0:T(8,128)S(1)}, f32[2,24,24,128]{3,2,1,0:T(8,128)S(1)}, f32[2,24,24,128]{3,2,1,0:T(8,128)S(1)}, f32[2,24,24,128]{3,2,1,0:T(8,128)S(1)}, f32[2,24,24,128]{3,2,1,0:T(8,128)S(1)}) custom-call(f32[6,16,16,128]{3,2,1,0:T(8,128)S(1)} %get-tuple-element.16.own_ref, f32[6,16,8,128]{3,2,1,0:T(8,128)S(1)} %get-tuple-element.20.rim_ref, ...), custom_call_target="tpu_custom_call" | custom-call | tf_op jit(solution)/shard_map/basis/pallas_call | solution.py:420
  32.9 35.0 %all_to_all.5 = f32[512,1,128]{2,1,0:T(1,128)S(1)} all-to-all(f32[512,1,128]{2,1,0:T(1,128)S(1)} %bitcast.5), channel_id=1, replica_groups=mesh['gx'=16,'gy'=32] {'gx','gy'}, dimensions={0} | all-to-all | bytes 524288 | tf_op jit(solution)/shard_map/all_to_all | solution.py:435
  67.8 1.3 %combine.1 = (f32[16,16,128]{2,1,0:T(8,128)}, f32[16,16,128]{2,1,0:T(8,128)}, f32[3,16,16,128]{3,2,1,0:T(8,128)}) custom-call(f32[64,8,128]{2,1,0:T(8,128)S(1)} %bitcast.4, f32[2,24,24,128]{3,2,1,0:T(8,128)S(1)} %get-tuple-element.25.p0, f32[2,24,24,128]{3,2,1,0:T(8,128)S(1)} %get-tuple-element.26.p1, f32[2,24,24,128]{3,2,1,0:T(8,128)S(1)} %get-tuple-element.27.p2, ...), custom_call_target="tpu_custom_call" | custom-call | tf_op jit(solution)/shard_map/combine/pallas_call | solution.py:436
  (2 shorter events, 0.0 us)
Async XLA Ops:
  2.4 17.4 %collective-permute-start = (f32[6,16,4,128]{3,2,1,0:T(4,128)S(1)}, f32[6,16,4,128]{3,2,1,0:T(4,128)S(1)}, u32[]{:S(2)}, u32[]{:S(2)}) collective-permute-start(f32[6,16,4,128]{3,2,1,0:T(4,128)S(1)} %get-tuple-element.17), channel_id=1, source_target_pairs={{1,2},{3,4},{5,6},{7,8},{9,10},{11,12},{13,14},{15,16},{17,18},{19... | collective-permute-start | bytes 589832 | tf_op jit(solution)/shard_map/ppermute | solution.py:23
  3.0 16.8 %collective-permute-start.1 = (f32[6,16,4,128]{3,2,1,0:T(4,128)S(1)}, f32[6,16,4,128]{3,2,1,0:T(4,128)S(1)}, u32[]{:S(2)}, u32[]{:S(2)}) collective-permute-start(f32[6,16,4,128]{3,2,1,0:T(4,128)S(1)} %get-tuple-element.18), channel_id=1, source_target_pairs={{0,1},{1,0},{2,3},{3,2},{4,5},{5,4},{6,7},{7,6},{8,9},{9,8},{10,11... | collective-permute-start | bytes 589832 | tf_op jit(solution)/shard_map/ppermute | solution.py:18
  11.2 15.3 %collective-permute-start.2 = (f32[15,16,128]{2,1,0:T(8,128)S(1)}, f32[15,16,128]{2,1,0:T(8,128)S(1)}, u32[]{:S(2)}, u32[]{:S(2)}) collective-permute-start(f32[15,16,128]{2,1,0:T(8,128)S(1)} %get-tuple-element.21), channel_id=1, source_target_pairs={{32,64},{96,128},{160,192},{224,256},{288,320},{352,384},{416,448}... | collective-permute-start | bytes 368648 | tf_op jit(solution)/shard_map/ppermute | solution.py:23
  19.9 11.4 %collective-permute-start.4 = (f32[46,8,128]{2,1,0:T(8,128)S(1)}, f32[46,8,128]{2,1,0:T(8,128)S(1)}, u32[]{:S(2)}, u32[]{:S(2)}) collective-permute-start(f32[46,8,128]{2,1,0:T(8,128)S(1)} %get-tuple-element.23), channel_id=1, source_target_pairs={{0,32},{32,0},{64,96},{96,64},{128,160},{160,128},{192,224},{224,1... | collective-permute-start | bytes 565256 | tf_op jit(solution)/shard_map/ppermute | solution.py:18
  21.9 9.5 %collective-permute-start.3 = (f32[16,8,128]{2,1,0:T(8,128)S(1)}, f32[16,8,128]{2,1,0:T(8,128)S(1)}, u32[]{:S(2)}, u32[]{:S(2)}) collective-permute-start(f32[16,8,128]{2,1,0:T(8,128)S(1)} %get-tuple-element.22), channel_id=1, source_target_pairs={{32,64},{96,128},{160,192},{224,256},{288,320},{352,384},{416,448}... | collective-permute-start | bytes 196616 | tf_op jit(solution)/shard_map/ppermute | solution.py:23
